TPU v7x, 32 devices: a whole 2x2x4 slice. The times are simulated.
32 devices in a mesh: col: 4 (over z), row: 8 (over y, x, core).
Axes of the slice: x: 2, y: 2, z: 4, core: 2. Of those that a mesh axis runs over, the one named last changes fastest.
Arguments:
- matrix: bfloat16 [24576, 24576], P('row', 'col'), may hold values from -9 to 9
- left_basis: float32 [320, 24576], P(None, ('row', 'col')), may hold values from -6 to 6
- right_basis: float32 [320, 24576], P(None, ('col', 'row')), may hold values from -6 to 6
- right_block: float32 [64, 24576], P(None, ('col', 'row')), may hold values from -6 to 6
Outputs:
- left_blocks: float32 [64, 24576], P(None, ('row', 'col'))
- right_blocks: float32 [64, 24576], P(None, ('col', 'row'))
- factors: float32 [2, 64, 64], replicated
All inputs are finite; a program needn't handle non-finite values.
Results may differ from a plain program's by a relative error of at most 0.0041.
Values may be sent and summed in bfloat16 or wider, within the bound.
No kernel may reach another device: no remote copies, remote signals or barrier semaphores. Data moves between devices by JAX's collectives and lax.ppermute only.
A program may use at most 128 MiB of HBM per device.

v0:
```python
import jax
import jax.numpy as jnp
from jax import lax
from jax.sharding import PartitionSpec as P

N = 24576


highest_precision = lax.Precision.HIGHEST


def contract(first, second, contracted):
    return lax.dot_general(first, second, (contracted, ((), ())), precision=highest_precision)


def summed(values):
    return lax.psum(values, ("col", "row"))


def orthonormalize(image, basis_set, basis_gram):
    coef_sum, self_sum = summed(
        (contract(basis_set, image, ((1,), (1,))), contract(image, image, ((1,), (1,))))
    )
    coefficients = coef_sum / N
    own_gram = self_sum / N
    gram_times = jnp.dot(basis_gram, coefficients, precision=highest_precision)
    squared = contract(coefficients, coefficients, ((0,), (0,)))
    weighted = contract(coefficients, gram_times, ((0,), (0,)))
    gram_matrix = own_gram - 2.0 * squared + weighted
    projected = image - contract(coefficients, basis_set, ((0,), (0,)))
    factor_low = jnp.linalg.cholesky(gram_matrix)
    new_block = lax.linalg.triangular_solve(factor_low, projected, left_side=True, lower=True)
    cross_rows = lax.linalg.triangular_solve(
        factor_low, (coefficients - gram_times).T, left_side=True, lower=True
    )
    identity = jnp.eye(image.shape[0], dtype=jnp.float32)
    upper_part = jnp.concatenate([basis_gram, cross_rows.T], 1)
    lower_part = jnp.concatenate([cross_rows, identity], 1)
    return (new_block, factor_low, jnp.concatenate([upper_part, lower_part], 0))


def forward(current, matrix):
    partial_sum = lax.dot_general(
        lax.all_gather(current, "row", axis=1, tiled=True),
        matrix,
        (((1,), (1,)), ((), ())),
        preferred_element_type=jnp.float32,
    )
    return lax.psum_scatter(partial_sum, "col", scatter_dimension=1, tiled=True)


def backward(left_new, matrix):
    partial_sum = jnp.dot(
        lax.all_gather(left_new, "col", axis=1, tiled=True),
        matrix,
        preferred_element_type=jnp.float32,
    )
    return lax.psum_scatter(partial_sum, "row", scatter_dimension=1, tiled=True)


def shards(matrix, left_basis, right_basis, right_block):
    right_set = jnp.concatenate([right_basis, right_block], 0)
    left_gram = summed(contract(left_basis, left_basis, ((1,), (1,)))) / N
    right_gram = summed(contract(right_set, right_set, ((1,), (1,)))) / N
    factor_list = []
    image = forward(right_block.astype(jnp.bfloat16), matrix)
    left_new, left_low, left_gram = orthonormalize(image, left_basis, left_gram)
    coimage = backward(left_new.astype(jnp.bfloat16), matrix)
    right_new, right_low, right_gram = orthonormalize(coimage, right_set, right_gram)
    factor_list.append(left_low)
    factor_list.append(right_low)
    return (left_new, right_new, jnp.stack(factor_list))


def solution(mesh):
    in_specs = (
        P("row", "col"),
        P(None, ("row", "col")),
        P(None, ("col", "row")),
        P(None, ("col", "row")),
    )
    out_specs = (P(None, ("row", "col")), P(None, ("col", "row")), P())
    return jax.shard_map(shards, mesh=mesh, in_specs=in_specs, out_specs=out_specs, check_vma=False)
```

profile of v0, /device:TPU:0, one launch (start us, length us, event | category | flops | bytes accessed | tf_op | source)
XLA Modules:
  0.0 445.8 jit_solution(5861997199976218185)
XLA Ops:
  7.2 0.0 copy-start
  7.2 0.0 copy-start.5
  7.2 0.0 reduce-scatter.3.cloned.1.call-start
  7.2 1.4 constant_dynamic-update-slice_fusion.1
  8.6 0.0 copy-done.5
  8.7 12.4 %all_gather.6 = bf16[64,6144]{1,0:T(8,128)(2,1)S(1)} all-gather(bf16[64,768]{1,0:T(8,128)(2,1)S(1)} %get-tuple-element.10), channel_id=1, replica_groups=mesh['col'=4,'row'=8] {'row'}, dimensions={1}, use_global_device_ids=true | all-gather | bytes 884736 | tf_op jit(solution)/shard_map/all_gather | solution.py:44
  21.1 17.9 %fusion.42 = f32[64,3072]{1,0:T(8,128)} fusion(bf16[64,6144]{1,0:T(8,128)(2,1)S(1)} %all_gather.6, bf16[3072,6144]{1,0:T(8,128)(2,1)} %param.7), kind=kOutput, calls=%fused_computation.63 | convolution fusion | flops 2415919104 | bytes 39321600 | tf_op jit(solution)/shard_map/dot_general | solution.py:43
  39.0 0.0 reduce-scatter.3.cloned.1.call-update
  39.0 0.0 all-reduce.7.cloned.1.call-start
  39.0 0.0 copy-done
  39.0 2.5 fusion.44
  41.5 21.1 %reduce-scatter.3.cloned.1.call-done = f32[64,768]{1,0:T(8,128)} async-done(((f32[64,3072]{1,0:T(8,128)}), f32[64,768]{1,0:T(8,128)}) %reduce-scatter.3.cloned.1.call-update) | async-done | bytes 196624 | tf_op jit(solution)/shard_map/reduce_scatter | solution.py:49
  62.6 0.0 copy-start.1
  62.6 2.6 convolution_bitcast_fusion
  65.2 0.0 all-reduce.7.cloned.1.call-update
  65.2 0.0 reduce-scatter.5.cloned.1.call-start
  65.3 0.0 copy-done.1
  65.3 0.3 fusion.43
  65.6 38.9 %psum.42 = f32[64,64]{0,1:T(8,128)S(1)} all-reduce(f32[64,64]{0,1:T(8,128)S(1)} %fusion.43), channel_id=1, replica_groups=mesh['col'=4,'row'=8] {'col','row'}, use_global_device_ids=true, to_apply=%region_1.0 | all-reduce | flops 4096 | bytes 32768 | tf_op jit(solution)/shard_map/psum | solution.py:17
  104.5 92.5 %all-reduce.7.cloned.1.call-done = (f32[320,64]{0,1:T(8,128)}, f32[320,320]{1,0:T(8,128)}) async-done(((f32[320,64]{0,1:T(8,128)}, f32[320,320]{1,0:T(8,128)}), (f32[320,64]{0,1:T(8,128)}, f32[320,320]{1,0:T(8,128)})) %all-reduce.7.cloned.1.call-update) | async-done | bytes 491536 | tf_op jit(solution)/shard_map/psum | solution.py:17
  197.0 0.0 copy-start.4
  197.0 1.3 fusion.1
  198.3 1.6 fusion.4
  199.9 1.3 convolution_add_fusion.1
  201.3 0.1 copy.10
  201.4 5.8 %cholesky.44 = f32[64,64]{1,0:T(8,128)S(1)} custom-call(f32[64,64]{1,0:T(8,128)S(1)} %fusion.29), custom_call_target="Cholesky" | custom-call | tf_op jit(solution)/shard_map/jit(cholesky)/cholesky | solution.py:31
  207.2 0.6 compare_reduce_fusion.1
  207.9 0.7 fusion.31
  208.5 4.9 %custom-call.6 = f32[1,64,64]{1,2,0:T(8,128)S(1)} custom-call(f32[1,64,64]{2,1,0:T(8,128)S(1)} %get-tuple-element.12), custom_call_target="InvertDiagBlocksLowerTriangular" | custom-call | tf_op jit(solution)/shard_map/triangular_solve/custom-call.0 | solution.py:32
  213.4 0.0 copy-done.4
  213.5 0.8 convolution_subtract_fusion
  214.3 1.1 fusion.41
  215.3 15.6 %all_gather.7 = bf16[64,3072]{1,0:T(8,128)(2,1)S(1)} all-gather(bf16[64,768]{1,0:T(8,128)(2,1)S(1)} %get-tuple-element.15), channel_id=1, replica_groups=mesh['col'=4,'row'=8] {'col'}, dimensions={1}, use_global_device_ids=true | all-gather | bytes 491520 | tf_op jit(solution)/shard_map/all_gather | solution.py:54
  230.9 16.3 %fusion.45 = f32[64,6144]{1,0:T(8,128)} fusion(bf16[64,3072]{1,0:T(8,128)(2,1)S(1)} %all_gather.7, bf16[3072,6144]{1,0:T(8,128)(2,1)} %param.7), kind=kOutput, calls=%fused_computation.66 | convolution fusion | flops 2415919104 | bytes 39714816 | tf_op jit(solution)/shard_map/dot_general | solution.py:53
  247.2 0.0 reduce-scatter.5.cloned.1.call-update
  247.2 0.0 all-reduce.5.cloned.1.call-start
  247.3 2.9 fusion.48
  250.2 35.5 %reduce-scatter.5.cloned.1.call-done = f32[64,768]{1,0:T(8,128)} async-done(((f32[64,6144]{1,0:T(8,128)}), f32[64,768]{1,0:T(8,128)}) %reduce-scatter.5.cloned.1.call-update) | async-done | bytes 196624 | tf_op jit(solution)/shard_map/reduce_scatter | solution.py:58
  285.7 0.0 copy-start.2
  285.7 2.9 fusion.47
  288.6 0.0 all-reduce.5.cloned.1.call-update
  288.6 0.0 copy-done.2
  288.6 0.3 fusion.46
  288.9 39.7 %psum.45 = f32[64,64]{0,1:T(8,128)S(1)} all-reduce(f32[64,64]{0,1:T(8,128)S(1)} %fusion.46), channel_id=1, replica_groups=mesh['col'=4,'row'=8] {'col','row'}, use_global_device_ids=true, to_apply=%region_7.10 | all-reduce | flops 4096 | bytes 32768 | tf_op jit(solution)/shard_map/psum | solution.py:17
  328.6 91.5 %all-reduce.5.cloned.1.call-done = (f32[384,64]{0,1:T(8,128)}, f32[384,384]{1,0:T(8,128)}) async-done(((f32[384,64]{0,1:T(8,128)}, f32[384,384]{1,0:T(8,128)}), (f32[384,64]{0,1:T(8,128)}, f32[384,384]{1,0:T(8,128)})) %all-reduce.5.cloned.1.call-update) | async-done | bytes 688144 | tf_op jit(solution)/shard_map/psum | solution.py:17
  420.1 0.0 copy-start.3
  420.1 1.3 fusion
  421.4 1.7 fusion.2
  423.2 1.4 convolution_add_fusion
  424.5 0.1 copy.14
  424.6 5.8 %cholesky.55 = f32[64,64]{1,0:T(8,128)S(1)} custom-call(f32[64,64]{1,0:T(8,128)S(1)} %fusion.26), custom_call_target="Cholesky" | custom-call | tf_op jit(solution)/shard_map/jit(cholesky)/cholesky | solution.py:31
  430.5 0.6 compare_reduce_fusion
  431.2 0.7 fusion.32
  431.8 4.9 %custom-call.7 = f32[1,64,64]{1,2,0:T(8,128)S(1)} custom-call(f32[1,64,64]{2,1,0:T(8,128)S(1)} %get-tuple-element.14), custom_call_target="InvertDiagBlocksLowerTriangular" | custom-call | tf_op jit(solution)/shard_map/triangular_solve/custom-call.0 | solution.py:32
  436.7 0.0 copy-done.3
  436.7 0.8 convolution_subtract_fusion.1
  437.6 1.1 fusion.24
  438.6 0.6 pad_maximum_fusion
  (5 shorter events, 0.1 us)
Async XLA Ops:
  7.2 31.9 %copy-start = (f32[320,768]{1,0:T(8,128)S(1)}, f32[320,768]{1,0:T(8,128)}, u32[]{:S(2)}) copy-start(f32[320,768]{1,0:T(8,128)} %param.8) | copy-start | bytes 2949124
  7.2 1.4 copy-start.5
  7.2 55.4 %reduce-scatter.3.cloned.1.call-start = ((), (), s32[]{:S(2)}) async-start(), calls=%async_computation.2 | async-start | bytes 983040 | tf_op jit(solution)/shard_map/reduce_scatter | solution.py:49
  39.0 158.0 %all-reduce.7.cloned.1.call-start = ((), (), s32[]{:S(2)}) async-start(), calls=%async_computation.5 | async-start | bytes 1179648 | tf_op jit(solution)/shard_map/psum | solution.py:17
  62.6 2.7 copy-start.1
  65.2 220.5 %reduce-scatter.5.cloned.1.call-start = ((), (), s32[]{:S(2)}) async-start(), calls=%async_computation.3 | async-start | bytes 1769472 | tf_op jit(solution)/shard_map/reduce_scatter | solution.py:58
  197.0 16.4 %copy-start.4 = (f32[320,64]{0,1:T(8,128)S(1)}, f32[320,64]{0,1:T(8,128)}, u32[]{:S(2)}) copy-start(f32[320,64]{0,1:T(8,128)} %get-tuple-element.7) | copy-start | bytes 245764
  247.2 172.9 %all-reduce.5.cloned.1.call-start = ((), (), s32[]{:S(2)}) async-start(), calls=%async_computation.4 | async-start | bytes 1376256 | tf_op jit(solution)/shard_map/psum | solution.py:17
  285.7 2.9 copy-start.2
  420.1 16.6 %copy-start.3 = (f32[384,64]{0,1:T(8,128)S(1)}, f32[384,64]{0,1:T(8,128)}, u32[]{:S(2)}) copy-start(f32[384,64]{0,1:T(8,128)} %get-tuple-element.5) | copy-start | bytes 294916
Sparse Core Ops, SparseCore 0:
  39.1 23.4 reduce-scatter.2
  68.5 128.4 all-reduce.6
  247.4 38.2 reduce-scatter.4
  291.4 128.6 all-reduce.4
where the time goes:
time: 447 us; the launch traced here: 446 us
  waiting for transfers between devices  241 us (54%)
  blocking collectives  107 us (24%)
  matrix products  58 us (13%)
  other arithmetic  24.8 us (6%)
  between operations  14 us (3%)
    psum x2, waiting for transfers between devices, summed(): return lax.psum(values, ('col', 'row'))  184 us
    psum x2, blocking collectives, summed(): return lax.psum(values, ('col', 'row'))  78.6 us
    reduce_scatter x1, waiting for transfers between devices, backward(): return lax.psum_scatter(partial_sum, 'row', scatter_dimension=1, tiled=True)  35.5 us
    reduce_scatter x1, waiting for transfers between devices, forward(): return lax.psum_scatter(partial_sum, 'col', scatter_dimension=1, tiled=True)  21.1 us
    dot_general x12, matrix products, contract(): lax.dot_general(first, second, (contracted, ((), ())), precision=highest_...  18.4 us
    dot_general x1, matrix products, forward(): lax.dot_general(lax.all_gather(current, 'row', axis=1, tiled=True), matri...  17.9 us
    dot_general x1, matrix products, backward(): jnp.dot(lax.all_gather(left_new, 'col', axis=1, tiled=True), matrix, pref...  16.3 us
    all_gather x1, blocking collectives, backward(): lax.all_gather(left_new, 'col', axis=1, tiled=True)  15.6 us
  transfers between devices with their start and end apart: 4, of which 4 were waited for; matrix products, arithmetic and copies ran while one was open for 1% of the time, Pallas kernels for 0%

commit v1 on v0

v1 whole, which is shorter than its diff:
```python
import functools

import jax
import jax.numpy as jnp
from jax import lax
from jax.experimental import pallas as pl
from jax.experimental.pallas import tpu as pltpu
from jax.sharding import PartitionSpec as P

f32 = jnp.float32
bf16 = jnp.bfloat16
CROSS = bf16
ANY = pl.BlockSpec(memory_space=pltpu.HBM)
VMEM = pl.BlockSpec(memory_space=pltpu.VMEM)


def dot16(first, second, dims):
    return lax.dot_general(first, second, (dims, ((), ())), preferred_element_type=f32)


def dot32(first, second, dims):
    return lax.dot_general(first, second, (dims, ((), ())), precision=lax.Precision.HIGHEST, preferred_element_type=f32)


def split(values):
    high = values.astype(bf16)
    return high, (values - high.astype(f32)).astype(bf16)


def limit(mebibytes):
    return pltpu.CompilerParams(vmem_limit_bytes=mebibytes << 20)


def shape(dims, dtype=f32):
    return jax.ShapeDtypeStruct(dims, dtype)


def padded(count):
    return -(-count // 128) * 128


def call(kernel, inputs, outputs, name, specs=None, scratch=(), mebibytes=8):
    return pl.pallas_call(
        kernel,
        in_specs=specs or [VMEM] * len(inputs),
        out_specs=[VMEM] * len(outputs),
        out_shape=outputs,
        scratch_shapes=list(scratch),
        compiler_params=limit(mebibytes),
        name=name,
    )(*inputs)


def swap(values, axis, size, bit):
    return lax.ppermute(values, axis, [(i, i ^ bit) for i in range(size)])


def exchange_sum(values, axis, size, bit):
    while bit < size:
        if bit * 2 < size:
            one, two, three = (swap(values, axis, size, m) for m in (bit, bit * 2, bit * 3))
            values = (values + one) + (two + three)
            bit *= 4
        else:
            values = values + swap(values, axis, size, bit)
            bit *= 2
    return values


HALVES = 2


def fetch_copies(a_hbm, targets, sems, chunks, chunk):
    me = lax.axis_index("col")
    part = chunk // HALVES
    copies = []
    for n, j in enumerate(chunks):
        for h in range(HALVES):
            start = pl.multiple_of((me ^ j) * chunk + h * part, part)
            copies.append(
                pltpu.make_async_copy(
                    a_hbm.at[pl.ds(start, part), :], targets[n].at[pl.ds(h * part, part), :], sems.at[n, h]
                )
            )
    return copies


def fetch(matrix, chunk, j, bases):
    cols = matrix.shape[1]
    flat = [b for group in bases for b in group]
    width = flat[0].shape[1]
    counts = [sum(b.shape[0] for b in group) for group in bases]
    n_flat = len(flat)

    def kernel(a_hbm, *rest):
        sources, target, outs = rest[:n_flat], rest[n_flat], rest[n_flat + 1 : -n_flat - 2]
        held, sems, base_sems = rest[-n_flat - 2 : -2], rest[-2], rest[-1]
        brought = [pltpu.make_async_copy(src, dst, base_sems.at[n]) for n, (src, dst) in enumerate(zip(sources, held))]
        copies = fetch_copies(a_hbm, [target], sems, [j], chunk)
        for copy in brought + copies:
            copy.start()
        n_base = 0
        for n, group in enumerate(bases):
            rows_high, rows_low, turned = outs[3 * n : 3 * n + 3]
            size = padded(counts[n])
            if counts[n] != size:
                rows_high[...] = jnp.zeros_like(rows_high)
                rows_low[...] = jnp.zeros_like(rows_low)
                turned[...] = jnp.zeros_like(turned)
            at = 0
            for _ in group:
                brought[n_base].wait()
                values = held[n_base][...]
                n_base += 1
                count = values.shape[0]
                high, low = split(values)
                rows_high[at : at + count, :] = high
                rows_low[at : at + count, :] = low
                high, low = split(values.T)
                turned[:, at : at + count] = high
                turned[:, size + at : size + at + count] = low
                at += count
        for copy in copies:
            copy.wait()

    outputs = [shape((chunk, cols), bf16)]
    for count in counts:
        size = padded(count)
        outputs += [shape((size, width), bf16), shape((size, width), bf16), shape((width, 2 * size), bf16)]
    return call(
        kernel,
        [matrix] + flat,
        outputs,
        "fetch",
        specs=[ANY] * (1 + n_flat),
        scratch=[pltpu.VMEM(b.shape, f32) for b in flat]
        + [pltpu.SemaphoreType.DMA((1, HALVES)), pltpu.SemaphoreType.DMA((n_flat,))],
    )


def forward(lefts, order, held, matrix, chunk, products, brought):
    cols = matrix.shape[1]
    block = lefts[0].shape[0]
    step = chunk // 3 if chunk % 384 == 0 else chunk

    def kernel(*rest):
        rest = list(rest)
        parts = [rest.pop(0) for _ in lefts]
        chunks = {j: rest.pop(0) for j in held}
        a_hbm = rest.pop(0)
        outs = [rest.pop(0) for _ in products]
        targets = [rest.pop(0) for _ in brought]
        copies = fetch_copies(a_hbm, targets, rest[-1], brought, chunk)
        for copy in copies:
            copy.start()
        if order is None:
            whole = parts[0]
        else:
            whole = rest.pop(0)
            me = lax.axis_index("row")
            width = parts[0].shape[1]
            for part, m in zip(parts, order):
                whole[:, pl.ds(pl.multiple_of((me ^ m) * width, width), width)] = part[...]
        waited = 0
        for j, out in zip(products, outs):
            if j not in chunks:
                at = brought.index(j)
                for copy in copies[waited : HALVES * (at + 1)]:
                    copy.wait()
                waited = HALVES * (at + 1)
                chunks[j] = targets[at]
            right = chunks[j]

            def one(n, _, right=right, out=out):
                at = pl.ds(pl.multiple_of(n * step, step), step)
                out[:, at] = dot16(whole[...], right[at, :], ((1,), (1,))).astype(out.dtype)
                return _

            lax.fori_loop(0, chunk // step, one, 0)
        for copy in copies[waited:]:
            copy.wait()

    outputs = [shape((block, chunk), f32 if j == 0 else CROSS) for j in products]
    outputs += [shape((chunk, cols), bf16) for _ in brought]
    if order is not None:
        outputs.append(shape((block, cols), bf16))
    return call(
        kernel,
        list(lefts) + list(held.values()) + [matrix],
        outputs,
        "forward_%d" % products[0],
        specs=[VMEM] * (len(lefts) + len(held)) + [ANY],
        scratch=[pltpu.SemaphoreType.DMA((len(brought), HALVES))],
    )


def backward_begin(piece, chunk_j, begun=None):
    given = [] if begun is None else [begun]

    def kernel(p_ref, a_ref, *rest):
        got = dot16(p_ref[...], a_ref[...], ((1,), (0,)))
        rest[-1][...] = rest[0][...] + got if given else got

    name = "backward_more" if given else "backward_own"
    return call(kernel, [piece, chunk_j, *given], [shape((piece.shape[0], chunk_j.shape[1]))], name)[0]


def backward(pieces, chunks, begun, targets, parts):
    groups = len(pieces)
    block = pieces[0].shape[0]
    width = chunks[0].shape[1] // parts

    def kernel(*rest):
        lefts, rights, begun_ref, outs = rest[:groups], rest[groups : 2 * groups], rest[2 * groups], rest[2 * groups + 1 :]
        me = lax.axis_index("row")
        for out, wanted in zip(outs, targets):
            for n, j in enumerate(wanted):
                at = pl.ds(pl.multiple_of((me ^ j) * width, width), width)
                total = begun_ref[:, at]
                for left, right in zip(lefts, rights):
                    total = total + dot16(left[...], right[:, at], ((1,), (0,)))
                out[n] = total

    outputs = [shape((len(wanted), block, width)) for wanted in targets]
    return call(kernel, [*pieces, *chunks, begun], outputs, "backward_%d" % targets[0][0])


def combine(mine, theirs):
    count, block, width = mine.shape

    def kernel(mine_ref, theirs_ref, *outs):
        for n, out in enumerate(outs):
            out[...] = (mine_ref[n] + theirs_ref[n]).astype(CROSS)

    return call(kernel, [mine, theirs], [shape((block, width), CROSS)] * count, "combine")


def coefficients(pieces, turned, total, further=None):
    block, width = pieces[0].shape[-2:]
    size = turned.shape[1] // 2
    half = block // 2
    n_pieces = len(pieces)
    given = [] if further is None else [further]
    count = size + (further.shape[1] if given else 0)

    def kernel(*rest):
        parts, turned_ref = rest[:n_pieces], rest[n_pieces]
        more = rest[n_pieces + 1 : n_pieces + 1 + len(given)]
        image_ref, mine_ref, theirs_ref, held = rest[n_pieces + 1 + len(given) :]
        image = parts[0][...].astype(f32).reshape(block, width)
        for part in parts[1:]:
            image = image + part[...].astype(f32).reshape(block, width)
        image_ref[...] = image
        high, low = split(image)
        right = turned_ref[...]
        got = dot16(high, right, ((1,), (0,)))
        got = got[:, :size] + (got[:, size:] + dot16(low, right[:, :size], ((1,), (0,))))
        held[:, :size] = got * (1.0 / total)
        if more:
            held[:, size:] = more[0][...]
        own = lax.axis_index("row") % 2
        mine_ref[...] = held[pl.ds(pl.multiple_of(own * half, half), half), :]
        theirs_ref[...] = held[pl.ds(pl.multiple_of((1 - own) * half, half), half), :]

    return call(
        kernel,
        [*pieces, turned, *given],
        [shape((block, width)), shape((half, count)), shape((half, count))],
        "coefficients",
        scratch=[pltpu.VMEM((block, count), f32)],
    )


def project(image, rows_high, rows_low, mine, other, total):
    block, width = image.shape
    size = rows_high.shape[0]
    half = block // 2
    count = mine.shape[1]

    def kernel(image_ref, high_ref, low_ref, mine_ref, other_ref, *rest):
        out_ref, round_ref, gram_ref = rest[:3]
        held = rest[-1]
        own = lax.axis_index("row") % 2
        held[pl.ds(pl.multiple_of(own * half, half), half), :] = mine_ref[...]
        held[pl.ds(pl.multiple_of((1 - own) * half, half), half), :] = other_ref[...]
        high, low = split(held[:, :size])
        right = high_ref[...]
        taken = dot16(high, right, ((1,), (0,))) + (
            dot16(low, right, ((1,), (0,))) + dot16(high, low_ref[...], ((1,), (0,)))
        )
        out = image_ref[...] - taken
        high, low = split(out)
        out_ref[...] = out
        round_ref[...] = high
        cross = dot16(high, low, ((1,), (1,))) + dot16(low, high, ((1,), (1,)))
        gram_ref[...] = (dot16(high, high, ((1,), (1,))) + cross) * (1.0 / total)
        if count > size:
            rest[3][...] = held[:, size:]

    outputs = [shape((block, width)), shape((block, width), bf16), shape((block, block))]
    if count > size:
        outputs.append(shape((block, count - size)))
    return call(
        kernel,
        [image, rows_high, rows_low, mine, other],
        outputs,
        "project",
        scratch=[pltpu.VMEM((block, count), f32)],
    )


GROUP = 8


def eliminate(gram):
    block = gram.shape[0]
    line = lax.broadcasted_iota(jnp.int32, (block, block), 0)
    lane = lax.broadcasted_iota(jnp.int32, (block, block), 1)
    both = jnp.concatenate([gram, jnp.where(line == lane, 1.0, 0.0).astype(f32)], 1)
    place = lax.broadcasted_iota(jnp.int32, both.shape, 0)
    for base in range(0, block, GROUP):
        count = min(GROUP, block - base)
        columns = [jnp.broadcast_to(both[:, base + q : base + q + 1], both.shape) for q in range(count)]
        for q in range(count):
            j = base + q
            pivot = 1.0 / columns[q][j : j + 1, :]
            ratio = jnp.where(place > j, columns[q] * pivot, 0.0)
            for p in range(q + 1, count):
                columns[p] = columns[p] - ratio * columns[p][j : j + 1, :]
            both = both - ratio * both[j : j + 1, :]
    upper = both[:, :block]
    diagonal = jnp.sum(jnp.where(line == lane, upper, 0.0), axis=1, keepdims=True)
    scale = 1.0 / jnp.sqrt(diagonal)
    inverse = jnp.where(line >= lane, both[:, block:] * scale, 0.0)
    return jnp.where(lane >= line, upper * scale, 0.0).T, inverse


def factor_left(gram, rows):
    def kernel(gram_ref, rows_ref, low_ref, inverse_ref, new_ref):
        low, inverse = eliminate(gram_ref[...])
        low_ref[...] = low
        inverse_ref[...] = inverse
        new_ref[...] = dot32(inverse, rows_ref[...], ((1,), (0,)))

    small = shape(gram.shape)
    return call(kernel, [gram, rows], [small, small, shape(rows.shape)], "factor_left")


def factor_right(gram, rows, left_low, left_inverse):
    def kernel(gram_ref, rows_ref, left_low_ref, left_inverse_ref, factors_ref, new_ref):
        turn = left_inverse_ref[...]
        gram_here = dot32(dot32(turn, gram_ref[...], ((1,), (0,))), turn, ((1,), (1,)))
        low, inverse = eliminate(gram_here)
        factors_ref[0] = left_low_ref[...]
        factors_ref[1] = low
        new_ref[...] = dot32(dot32(inverse, turn, ((1,), (0,))), rows_ref[...], ((1,), (0,)))

    return call(
        kernel,
        [gram, rows, left_low, left_inverse],
        [shape((2, *gram.shape)), shape(rows.shape)],
        "factor_right",
    )


def bases_split(bases):
    out = []
    for group in bases:
        rows = jnp.concatenate(group, 0)
        rows = jnp.pad(rows, ((0, padded(rows.shape[0]) - rows.shape[0]), (0, 0)))
        high, low = split(rows)
        out += [high, low, jnp.concatenate([high.T, low.T], 1)]
    return out


def shards(matrix, left_basis, right_basis, right_block, *, n_col, n_row):
    total = left_basis.shape[1] * n_col * n_row
    chunk, width = matrix.shape[0] // n_col, matrix.shape[1] // n_row
    tiled = n_col == 4 and n_row == 8 and width % 128 == 0 and chunk % 32 == 0
    row_swap = lambda values, bit: swap(values, "row", n_row, bit)
    col_swap = lambda values, bit: swap(values, "col", n_col, bit)

    def all_sum(values):
        values = values + row_swap(values, 1)
        values = exchange_sum(values, "row", n_row, 2)
        return exchange_sum(values, "col", n_col, 1)

    def split_sum(mine, theirs):
        mine = mine + row_swap(theirs, 1)
        mine = exchange_sum(mine, "row", n_row, 2)
        mine = exchange_sum(mine, "col", n_col, 1)
        return mine, row_swap(mine, 1)

    rounded = right_block.astype(bf16)
    bases = ([left_basis], [right_basis, right_block])
    if tiled:
        lefts = {m: row_swap(rounded, m) for m in range(2, n_row, 2)}
        lefts[0], lefts[1] = rounded, row_swap(rounded, 1)
        chunk_2, *prepared = fetch(matrix, chunk, 2, bases)
        chunk_2, *after = lax.optimization_barrier((chunk_2, *(lefts[m] for m in range(2, n_row, 2))))
        for m, values in zip(range(2, n_row, 2), after):
            lefts[m] = values
            lefts[m + 1] = row_swap(values, 1)
        order = sorted(lefts)
        piece_2, piece_3, chunk_3, chunk_1, whole = forward(
            [lefts[m] for m in order], order, {2: chunk_2}, matrix, chunk, [2, 3], [3, 1]
        )
        piece_1, piece_0, chunk_0 = forward([whole], None, {1: chunk_1}, matrix, chunk, [1, 0], [0])
        pieces = [piece_0, col_swap(piece_1, 1), col_swap(piece_2, 2), col_swap(piece_3, 3)]
    else:
        prepared = bases_split(bases)
        whole = lax.all_gather(rounded, "row", axis=1, tiled=True)
        partial = dot16(whole, matrix, ((1,), (1,)))
        me = lax.axis_index("col")
        pieces = [lax.dynamic_slice_in_dim(partial, (me ^ j) * chunk, chunk, 1) for j in range(n_col)]
        pieces = [pieces[0]] + [col_swap(pieces[j].astype(CROSS), j) for j in range(1, n_col)]
    left_high, left_low, left_turned, right_high, right_low, right_turned = prepared

    image, mine, theirs = coefficients(pieces, left_turned, total)
    mine, other = split_sum(mine, theirs)
    projected, low, gram = project(image, left_high, left_low, mine, other, total)
    lows = [col_swap(low, j) for j in range(1, n_col)]
    if tiled:
        begun = backward_begin(lows[0], chunk_1, backward_begin(low, chunk_0))
        ready = (lows[1:], [chunk_2, chunk_3], begun)
        far = list(range(2, n_row, 2))
        (theirs,) = backward(*ready, [[m + 1 for m in far]], n_row)
        theirs = row_swap(theirs, 1)
        (mine,) = backward(*ready, [far], n_row)
        begun, *sent = lax.optimization_barrier((begun, *combine(mine, theirs)))
        pieces = [row_swap(values, m) for m, values in zip(far, sent)]
        theirs, mine = backward(*ready[:2], begun, [[1], [0]], n_row)
        pieces = [mine, row_swap(theirs, 1)] + pieces
    else:
        me_col, me = lax.axis_index("col"), lax.axis_index("row")
        partial = sum(
            dot16(piece, lax.dynamic_slice_in_dim(matrix, (me_col ^ g) * chunk, chunk, 0), ((1,), (0,)))
            for g, piece in enumerate([low] + lows)
        )
        cut = [lax.dynamic_slice_in_dim(partial, (me ^ j) * width, width, 1) for j in range(n_row)]
        mine = jnp.stack(cut[0::2]) + row_swap(jnp.stack(cut[1::2]), 1)
        pieces = [mine[0]] + [row_swap(mine[m].astype(CROSS), 2 * m) for m in range(1, n_row // 2)]
    coimage, mine, theirs = coefficients(pieces, right_turned, total, gram)
    mine, other = split_sum(mine, theirs)
    coprojected, _, cogram, gram = project(coimage, right_high, right_low, mine, other, total)
    cogram = all_sum(cogram)
    factor, inverse, left_new = factor_left(gram, projected)
    factors, right_new = factor_right(cogram, coprojected, factor, inverse)
    return left_new, right_new, factors


def solution(mesh):
    in_specs = (
        P("row", "col"),
        P(None, ("row", "col")),
        P(None, ("col", "row")),
        P(None, ("col", "row")),
    )
    out_specs = (P(None, ("row", "col")), P(None, ("col", "row")), P())
    body = functools.partial(shards, n_col=mesh.shape["col"], n_row=mesh.shape["row"])
    return jax.shard_map(body, mesh=mesh, in_specs=in_specs, out_specs=out_specs, check_vma=False)
```

time: 447 us -> 121 us (0.27)
  waiting for transfers between devices: 241 us -> 38.6 us
  blocking collectives: 107 us -> 0 us
  matrix products: 58 us -> 0 us
  starting transfers between devices: 0.16 us -> 42.1 us
  Pallas kernels: 0 us -> 35.3 us
  other arithmetic: 24.8 us -> 1.05 us
  between operations: 14 us -> 0.85 us
    psum x2 -> x0, waiting for transfers between devices: 184 us -> none  [summed(): return lax.psum(values, ('col', 'row'))]
    psum x2 -> x0, blocking collectives: 78.6 us -> none  [summed(): return lax.psum(values, ('col', 'row'))]
    reduce_scatter x2 -> x0, waiting for transfers between devices: 56.6 us -> none  [the longest x1 35.5 us: backward(): return lax.psum_scatter(partial_sum, 'row', scatter_dimension=1, tiled=True)]
    dot_general x16 -> x0, matrix products: 55.9 us -> none  [the longest x12 18.4 us: contract(): lax.dot_general(first, second, (contracted, ((), ())), precision=highest_...]
    ppermute x0 -> x41, starting transfers between devices: none -> 42.1 us  [swap(): return lax.ppermute(values, axis, [(i, i ^ bit) for i in range(size)])]
    ppermute x0 -> x41, waiting for transfers between devices: none -> 38.6 us  [swap(): return lax.ppermute(values, axis, [(i, i ^ bit) for i in range(size)])]
    pallas_call x0 -> x15, Pallas kernels: none -> 35.3 us  [call(): pl.pallas_call(kernel, in_specs=specs or [VMEM] * len(inputs), out_specs=...]
    all_gather x2 -> x0, blocking collectives: 28 us -> none  [the longest x1 15.6 us: backward(): lax.all_gather(left_new, 'col', axis=1, tiled=True)]
  transfers between devices with their start and end apart: 4 -> 41, of which waited for: 4 -> 28; matrix products, arithmetic and copies ran while one was open for 1% -> 0% of each run, Pallas kernels for 0% -> 16%
where the time goes in v1:
time: 121 us
  starting transfers between devices  42.1 us (35%)
  waiting for transfers between devices  38.6 us (32%)
  Pallas kernels  35.3 us (29%)
  local copies, waits for them, and re-layouts  3.33 us (3%)
    ppermute x41, starting transfers between devices, swap(): return lax.ppermute(values, axis, [(i, i ^ bit) for i in range(size)])  42.1 us
    ppermute x41, waiting for transfers between devices, swap(): return lax.ppermute(values, axis, [(i, i ^ bit) for i in range(size)])  38.6 us
    pallas_call x15, Pallas kernels, call(): pl.pallas_call(kernel, in_specs=specs or [VMEM] * len(inputs), out_specs=...  35.3 us
    unnamed x6, local copies, waits for them, and re-layouts  3.33 us
  transfers between devices with their start and end apart: 41, of which 28 were waited for; matrix products, arithmetic and copies ran while one was open for 0% of the time, Pallas kernels for 16%

profile of v1, /device:TPU:0, one launch (start us, length us, event | category | flops | bytes accessed | tf_op | source)
XLA Modules:
  0.0 121.2 jit_solution(3981178271853173270)
XLA Ops:
  0.6 0.9 convert_element_type.3.rest_0_
  1.6 4.0 %collective-permute-start.3 = (bf16[64,768]{1,0:T(8,128)(2,1)S(1)}, bf16[64,768]{1,0:T(8,128)(2,1)S(1)}, u32[]{:S(2)}, u32[]{:S(2)}) collective-permute-start(bf16[64,768]{1,0:T(8,128)(2,1)S(1)} %convert_element_type.3.rest_0_), channel_id=1, source_target_pairs={{0,6},{1,7},{2,4},{3,5},{4,2},{5,3},{6,0},{7,1},{8,14},{9,15},{10,... | collective-permute-start | bytes 294920 | tf_op jit(solution)/shard_map/ppermute | solution.py:55
  6.2 1.2 copy-done
  7.4 1.2 copy-done.1
  8.6 0.9 copy-done.2
  9.5 4.7 %fetch.1 = (bf16[768,6144]{1,0:T(8,128)(2,1)S(1)}, bf16[384,768]{1,0:T(8,128)(2,1)S(1)}, bf16[384,768]{1,0:T(8,128)(2,1)S(1)}, bf16[768,768]{1,0:T(8,128)(2,1)S(...) custom-call(bf16[3072,6144]{1,0:T(8,128)(2,1)} %rest_2_.3, ...), custom_call_target="tpu_custom_call" | custom-call | tf_op jit(solution)/shard_map/fetch/pallas_call | solution.py:43
  14.3 0.6 collective-permute-start.4
  16.3 7.1 %forward_2.1 = (bf16[64,768]{1,0:T(8,128)(2,1)S(1)}, bf16[64,768]{1,0:T(8,128)(2,1)S(1)}, bf16[768,6144]{1,0:T(8,128)(2,1)S(1)}, bf16[768,6144]{1,0:T(8,128)(2,1)S(1)}, bf16[64,6144]{1,0:T(8,128)(2,1)S(1)}) custom-call(bf16[64,768]{1,0:T(8,128)(2,1)S(1)} %convert_element_type.3.rest_0_, bf16[64,768]{1,0:T(8,128)(2,1)S(1)} %collective-permute-done.rest_1_, ...), custom_call_target="tpu_custom_call" | custom-call | tf_op jit(solution)/shard_map/forward_2/pallas_call | solution.py:43
  23.4 3.1 %collective-permute-start.8 = (bf16[64,768]{1,0:T(8,128)(2,1)S(1)}, bf16[64,768]{1,0:T(8,128)(2,1)S(1)}, u32[]{:S(2)}, u32[]{:S(2)}) collective-permute-start(bf16[64,768]{1,0:T(8,128)(2,1)S(1)} %get-tuple-element.57), channel_id=1, source_target_pairs={{0,16},{8,24},{16,0},{24,8},{1,17},{9,25},{17,1},{25,9},{2,18},{10... | collective-permute-start | bytes 294920 | tf_op jit(solution)/shard_map/ppermute | solution.py:55
  26.4 1.3 %collective-permute-start.9 = (bf16[64,768]{1,0:T(8,128)(2,1)S(1)}, bf16[64,768]{1,0:T(8,128)(2,1)S(1)}, u32[]{:S(2)}, u32[]{:S(2)}) collective-permute-start(bf16[64,768]{1,0:T(8,128)(2,1)S(1)} %get-tuple-element.58), channel_id=1, source_target_pairs={{0,24},{8,16},{16,8},{24,0},{1,25},{9,17},{17,9},{25,1},{2,26},{10... | collective-permute-start | bytes 294920 | tf_op jit(solution)/shard_map/ppermute | solution.py:55
  27.8 7.2 %forward_1.1 = (bf16[64,768]{1,0:T(8,128)(2,1)S(1)}, f32[64,768]{1,0:T(8,128)S(1)}, bf16[768,6144]{1,0:T(8,128)(2,1)S(1)}) custom-call(bf16[64,6144]{1,0:T(8,128)(2,1)S(1)} %get-tuple-element.53.rest_0_, bf16[768,6144]{1,0:T(8,128)(2,1)S(1)} %get-tuple-element.54.rest_1_.a_ref, bf16[3072,6144]{1,0:T(8,128)(2,1)} %rest_2_.3), custom_call_target="tpu_custom_call" | custom-call | tf_op jit(solution)/shard_map/forward_1/pallas_call | solution.py:43
  35.3 4.4 %collective-permute-done.7.rest_1_ = bf16[64,768]{1,0:T(8,128)(2,1)S(1)} collective-permute-done((bf16[64,768]{1,0:T(8,128)(2,1)S(1)}, bf16[64,768]{1,0:T(8,128)(2,1)S(1)}, u32[]{:S(2)}, u32[]{:S(2)}) %collective-permute-start.7) | collective-permute-done | bytes 98336 | tf_op jit(solution)/shard_map/ppermute | solution.py:55
  40.2 1.2 %collective-permute-done.10 = f32[32,384]{1,0:T(8,128)S(1)} collective-permute-done((f32[32,384]{1,0:T(8,128)S(1)}, f32[32,384]{1,0:T(8,128)S(1)}, u32[]{:S(2)}, u32[]{:S(2)}) %collective-permute-start.10) | collective-permute-done | bytes 49184 | tf_op jit(solution)/shard_map/ppermute | solution.py:55
  41.4 2.5 %collective-permute-start.13 = (f32[32,384]{1,0:T(8,128)S(1)}, f32[32,384]{1,0:T(8,128)S(1)}, u32[]{:S(2)}, u32[]{:S(2)}) collective-permute-start(f32[32,384]{1,0:T(8,128)S(1)} %add.63), channel_id=1, source_target_pairs={{0,6},{1,7},{2,4},{3,5},{4,2},{5,3},{6,0},{7,1},{8,14},{9,15},{10,... | collective-permute-start | bytes 147464 | tf_op jit(solution)/shard_map/ppermute | solution.py:55
  43.9 0.5 collective-permute-start.12
  44.4 0.5 collective-permute-start.11
  45.0 1.5 %collective-permute-done.13 = f32[32,384]{1,0:T(8,128)S(1)} collective-permute-done((f32[32,384]{1,0:T(8,128)S(1)}, f32[32,384]{1,0:T(8,128)S(1)}, u32[]{:S(2)}, u32[]{:S(2)}) %collective-permute-start.13) | collective-permute-done | bytes 49184 | tf_op jit(solution)/shard_map/ppermute | solution.py:55
  46.5 1.5 %collective-permute-done.12 = f32[32,384]{1,0:T(8,128)S(1)} collective-permute-done((f32[32,384]{1,0:T(8,128)S(1)}, f32[32,384]{1,0:T(8,128)S(1)}, u32[]{:S(2)}, u32[]{:S(2)}) %collective-permute-start.12) | collective-permute-done | bytes 49184 | tf_op jit(solution)/shard_map/ppermute | solution.py:55
  48.0 0.5 collective-permute-done.11
  48.5 2.5 %collective-permute-start.16 = (f32[32,384]{1,0:T(8,128)S(1)}, f32[32,384]{1,0:T(8,128)S(1)}, u32[]{:S(2)}, u32[]{:S(2)}) collective-permute-start(f32[32,384]{1,0:T(8,128)S(1)} %add_add_fusion.3), channel_id=1, source_target_pairs={{0,24},{8,16},{16,8},{24,0},{1,25},{9,17},{17,9},{25,1},{2,26},{10... | collective-permute-start | bytes 147464 | tf_op jit(solution)/shard_map/ppermute | solution.py:55
  51.1 1.9 %collective-permute-start.14 = (f32[32,384]{1,0:T(8,128)S(1)}, f32[32,384]{1,0:T(8,128)S(1)}, u32[]{:S(2)}, u32[]{:S(2)}) collective-permute-start(f32[32,384]{1,0:T(8,128)S(1)} %add_add_fusion.3), channel_id=1, source_target_pairs={{0,8},{8,0},{16,24},{24,16},{1,9},{9,1},{17,25},{25,17},{2,10},{10... | collective-permute-start | bytes 147464 | tf_op jit(solution)/shard_map/ppermute | solution.py:55
  53.0 2.0 %collective-permute-done.16 = f32[32,384]{1,0:T(8,128)S(1)} collective-permute-done((f32[32,384]{1,0:T(8,128)S(1)}, f32[32,384]{1,0:T(8,128)S(1)}, u32[]{:S(2)}, u32[]{:S(2)}) %collective-permute-start.16) | collective-permute-done | bytes 49184 | tf_op jit(solution)/shard_map/ppermute | solution.py:55
  55.0 1.0 collective-permute-done.15
  56.2 1.2 %collective-permute-done.17.other_ref = f32[32,384]{1,0:T(8,128)S(1)} collective-permute-done((f32[32,384]{1,0:T(8,128)S(1)}, f32[32,384]{1,0:T(8,128)S(1)}, u32[]{:S(2)}, u32[]{:S(2)}) %collective-permute-start.17) | collective-permute-done | bytes 49184 | tf_op jit(solution)/shard_map/ppermute | solution.py:55
  57.4 0.7 project.2
  58.1 1.1 collective-permute-start.20
  59.2 2.5 %collective-permute-start.19 = (bf16[64,768]{1,0:T(8,128)(2,1)S(1)}, bf16[64,768]{1,0:T(8,128)(2,1)S(1)}, u32[]{:S(2)}, u32[]{:S(2)}) collective-permute-start(bf16[64,768]{1,0:T(8,128)(2,1)S(1)} %get-tuple-element.65.p_ref), channel_id=1, source_target_pairs={{0,24},{8,16},{16,8},{24,0},{1,25},{9,17},{17,9},{25,1},{2,26},{10... | collective-permute-start | bytes 294920 | tf_op jit(solution)/shard_map/ppermute | solution.py:55
  61.7 1.7 %backward_own.1.rest_0_ = f32[64,6144]{1,0:T(8,128)S(1)} custom-call(bf16[64,768]{1,0:T(8,128)(2,1)S(1)} %get-tuple-element.65.p_ref, bf16[768,6144]{1,0:T(8,128)(2,1)S(1)} %get-tuple-element.67.a_ref), custom_call_target="tpu_custom_call" | custom-call | tf_op jit(solution)/shard_map/backward_own/pallas_call | solution.py:43
  63.4 1.8 %backward_more.1.rest_4_ = f32[64,6144]{1,0:T(8,128)S(1)} custom-call(bf16[64,768]{1,0:T(8,128)(2,1)S(1)} %collective-permute-done.20.p_ref, bf16[768,6144]{1,0:T(8,128)(2,1)S(1)} %get-tuple-element.54.rest_1_.a_ref, f32[64,6144]{1,0:T(8,128)S(1)} %backward_own.1.rest_0_), custom_call_target="tpu_custom_call" | custom-call | tf_op jit(solution)/shard_map/backward_more/pallas_call | solution.py:43
  65.2 2.3 %collective-permute-done.19.rest_1_ = bf16[64,768]{1,0:T(8,128)(2,1)S(1)} collective-permute-done((bf16[64,768]{1,0:T(8,128)(2,1)S(1)}, bf16[64,768]{1,0:T(8,128)(2,1)S(1)}, u32[]{:S(2)}, u32[]{:S(2)}) %collective-permute-start.19) | collective-permute-done | bytes 98336 | tf_op jit(solution)/shard_map/ppermute | solution.py:55
  67.5 3.1 %collective-permute-done.18.rest_0_ = bf16[64,768]{1,0:T(8,128)(2,1)S(1)} collective-permute-done((bf16[64,768]{1,0:T(8,128)(2,1)S(1)}, bf16[64,768]{1,0:T(8,128)(2,1)S(1)}, u32[]{:S(2)}, u32[]{:S(2)}) %collective-permute-start.18) | collective-permute-done | bytes 98336 | tf_op jit(solution)/shard_map/ppermute | solution.py:55
  70.6 1.4 %backward_3.1 = f32[3,64,768]{2,1,0:T(8,128)S(1)} custom-call(bf16[64,768]{1,0:T(8,128)(2,1)S(1)} %collective-permute-done.18.rest_0_, bf16[64,768]{1,0:T(8,128)(2,1)S(1)} %collective-permute-done.19.rest_1_, bf16[768,6144]{1,0:T(8,128)(2,1)S(1)} %get-tuple-element.52.rest_8_.rest_2_, bf16[768,6144]{1,0:T(8,128)(2,1)S(1)} %get-tuple-element.66.rest_3_, ...), custom_call_target="tpu_custom_call" | custom-call | tf_op jit(solution)/shard_map/backward_3/pallas_call | solution.py:43
  72.0 1.4 %backward_2.1.mine_ref = f32[3,64,768]{2,1,0:T(8,128)S(1)} custom-call(bf16[64,768]{1,0:T(8,128)(2,1)S(1)} %collective-permute-done.18.rest_0_, bf16[64,768]{1,0:T(8,128)(2,1)S(1)} %collective-permute-done.19.rest_1_, bf16[768,6144]{1,0:T(8,128)(2,1)S(1)} %get-tuple-element.52.rest_8_.rest_2_, bf16[768,6144]{1,0:T(8,128)(2,1)S(1)} %get-tuple-element.66.rest_3_, ...), custom_call_target="tpu_custom_call" | custom-call | tf_op jit(solution)/shard_map/backward_2/pallas_call | solution.py:43
  73.5 0.6 collective-permute-done.21.theirs_ref
  74.1 1.0 backward_1.1
  75.3 0.7 collective-permute-start.23
  75.9 1.4 %collective-permute-start.24 = (bf16[64,768]{1,0:T(8,128)(2,1)S(1)}, bf16[64,768]{1,0:T(8,128)(2,1)S(1)}, u32[]{:S(2)}, u32[]{:S(2)}) collective-permute-start(bf16[64,768]{1,0:T(8,128)(2,1)S(1)} %get-tuple-element.75), channel_id=1, source_target_pairs={{0,4},{1,5},{2,6},{3,7},{4,0},{5,1},{6,2},{7,3},{8,12},{9,13},{10,... | collective-permute-start | bytes 294920 | tf_op jit(solution)/shard_map/ppermute | solution.py:55
  77.4 1.4 %collective-permute-start.25 = (bf16[64,768]{1,0:T(8,128)(2,1)S(1)}, bf16[64,768]{1,0:T(8,128)(2,1)S(1)}, u32[]{:S(2)}, u32[]{:S(2)}) collective-permute-start(bf16[64,768]{1,0:T(8,128)(2,1)S(1)} %get-tuple-element.76), channel_id=1, source_target_pairs={{0,6},{1,7},{2,4},{3,5},{4,2},{5,3},{6,0},{7,1},{8,14},{9,15},{10,... | collective-permute-start | bytes 294920 | tf_op jit(solution)/shard_map/ppermute | solution.py:55
  78.8 2.1 %collective-permute-done.23.rest_2_ = bf16[64,768]{1,0:T(8,128)(2,1)S(1)} collective-permute-done((bf16[64,768]{1,0:T(8,128)(2,1)S(1)}, bf16[64,768]{1,0:T(8,128)(2,1)S(1)}, u32[]{:S(2)}, u32[]{:S(2)}) %collective-permute-start.23) | collective-permute-done | bytes 98336 | tf_op jit(solution)/shard_map/ppermute | solution.py:55
  80.9 0.9 collective-permute-done.24.rest_3_
  81.8 1.6 %collective-permute-done.25.rest_4_ = bf16[64,768]{1,0:T(8,128)(2,1)S(1)} collective-permute-done((bf16[64,768]{1,0:T(8,128)(2,1)S(1)}, bf16[64,768]{1,0:T(8,128)(2,1)S(1)}, u32[]{:S(2)}, u32[]{:S(2)}) %collective-permute-start.25) | collective-permute-done | bytes 98336 | tf_op jit(solution)/shard_map/ppermute | solution.py:55
  84.0 1.2 %collective-permute-done.26 = f32[32,448]{1,0:T(8,128)S(1)} collective-permute-done((f32[32,448]{1,0:T(8,128)S(1)}, f32[32,448]{1,0:T(8,128)S(1)}, u32[]{:S(2)}, u32[]{:S(2)}) %collective-permute-start.26) | collective-permute-done | bytes 57376 | tf_op jit(solution)/shard_map/ppermute | solution.py:55
  85.2 1.8 %collective-permute-start.29 = (f32[32,448]{1,0:T(8,128)S(1)}, f32[32,448]{1,0:T(8,128)S(1)}, u32[]{:S(2)}, u32[]{:S(2)}) collective-permute-start(f32[32,448]{1,0:T(8,128)S(1)} %add.70), channel_id=1, source_target_pairs={{0,6},{1,7},{2,4},{3,5},{4,2},{5,3},{6,0},{7,1},{8,14},{9,15},{10,... | collective-permute-start | bytes 172040 | tf_op jit(solution)/shard_map/ppermute | solution.py:55
  87.0 0.6 collective-permute-start.28
  87.6 1.1 collective-permute-start.27
  88.8 1.7 %collective-permute-done.29 = f32[32,448]{1,0:T(8,128)S(1)} collective-permute-done((f32[32,448]{1,0:T(8,128)S(1)}, f32[32,448]{1,0:T(8,128)S(1)}, u32[]{:S(2)}, u32[]{:S(2)}) %collective-permute-start.29) | collective-permute-done | bytes 57376 | tf_op jit(solution)/shard_map/ppermute | solution.py:55
  90.4 1.3 %collective-permute-done.28 = f32[32,448]{1,0:T(8,128)S(1)} collective-permute-done((f32[32,448]{1,0:T(8,128)S(1)}, f32[32,448]{1,0:T(8,128)S(1)}, u32[]{:S(2)}, u32[]{:S(2)}) %collective-permute-start.28) | collective-permute-done | bytes 57376 | tf_op jit(solution)/shard_map/ppermute | solution.py:55
  91.9 2.0 %collective-permute-start.32 = (f32[32,448]{1,0:T(8,128)S(1)}, f32[32,448]{1,0:T(8,128)S(1)}, u32[]{:S(2)}, u32[]{:S(2)}) collective-permute-start(f32[32,448]{1,0:T(8,128)S(1)} %add_add_fusion.1), channel_id=1, source_target_pairs={{0,24},{8,16},{16,8},{24,0},{1,25},{9,17},{17,9},{25,1},{2,26},{10... | collective-permute-start | bytes 172040 | tf_op jit(solution)/shard_map/ppermute | solution.py:55
  94.0 2.4 %collective-permute-start.30 = (f32[32,448]{1,0:T(8,128)S(1)}, f32[32,448]{1,0:T(8,128)S(1)}, u32[]{:S(2)}, u32[]{:S(2)}) collective-permute-start(f32[32,448]{1,0:T(8,128)S(1)} %add_add_fusion.1), channel_id=1, source_target_pairs={{0,8},{8,0},{16,24},{24,16},{1,9},{9,1},{17,25},{25,17},{2,10},{10... | collective-permute-start | bytes 172040 | tf_op jit(solution)/shard_map/ppermute | solution.py:55
  96.4 1.9 %collective-permute-done.32 = f32[32,448]{1,0:T(8,128)S(1)} collective-permute-done((f32[32,448]{1,0:T(8,128)S(1)}, f32[32,448]{1,0:T(8,128)S(1)}, u32[]{:S(2)}, u32[]{:S(2)}) %collective-permute-start.32) | collective-permute-done | bytes 57376 | tf_op jit(solution)/shard_map/ppermute | solution.py:55
  98.3 2.0 %collective-permute-done.31 = f32[32,448]{1,0:T(8,128)S(1)} collective-permute-done((f32[32,448]{1,0:T(8,128)S(1)}, f32[32,448]{1,0:T(8,128)S(1)}, u32[]{:S(2)}, u32[]{:S(2)}) %collective-permute-start.31) | collective-permute-done | bytes 57376 | tf_op jit(solution)/shard_map/ppermute | solution.py:55
  100.4 1.2 %collective-permute-done.33.other_ref = f32[32,448]{1,0:T(8,128)S(1)} collective-permute-done((f32[32,448]{1,0:T(8,128)S(1)}, f32[32,448]{1,0:T(8,128)S(1)}, u32[]{:S(2)}, u32[]{:S(2)}) %collective-permute-start.33) | collective-permute-done | bytes 57376 | tf_op jit(solution)/shard_map/ppermute | solution.py:55
  101.6 1.1 project.3
  102.9 1.0 collective-permute-done.34
  104.0 1.9 %collective-permute-start.37 = (f32[64,64]{1,0:T(8,128)S(1)}, f32[64,64]{1,0:T(8,128)S(1)}, u32[]{:S(2)}, u32[]{:S(2)}) collective-permute-start(f32[64,64]{1,0:T(8,128)S(1)} %add.77), channel_id=1, source_target_pairs={{0,6},{1,7},{2,4},{3,5},{4,2},{5,3},{6,0},{7,1},{8,14},{9,15},{10,... | collective-permute-start | bytes 49160 | tf_op jit(solution)/shard_map/ppermute | solution.py:55
  105.9 0.6 collective-permute-start.36
  106.5 1.0 collective-permute-start.35
  107.5 1.4 %collective-permute-done.37 = f32[64,64]{1,0:T(8,128)S(1)} collective-permute-done((f32[64,64]{1,0:T(8,128)S(1)}, f32[64,64]{1,0:T(8,128)S(1)}, u32[]{:S(2)}, u32[]{:S(2)}) %collective-permute-start.37) | collective-permute-done | bytes 16416 | tf_op jit(solution)/shard_map/ppermute | solution.py:55
  108.9 0.9 collective-permute-done.36
  109.8 0.6 collective-permute-done.35
  110.4 2.0 %collective-permute-start.40 = (f32[64,64]{1,0:T(8,128)S(1)}, f32[64,64]{1,0:T(8,128)S(1)}, u32[]{:S(2)}, u32[]{:S(2)}) collective-permute-start(f32[64,64]{1,0:T(8,128)S(1)} %add_add_fusion.5), channel_id=1, source_target_pairs={{0,24},{8,16},{16,8},{24,0},{1,25},{9,17},{17,9},{25,1},{2,26},{10... | collective-permute-start | bytes 49160 | tf_op jit(solution)/shard_map/ppermute | solution.py:55
  112.5 2.4 %collective-permute-start.38 = (f32[64,64]{1,0:T(8,128)S(1)}, f32[64,64]{1,0:T(8,128)S(1)}, u32[]{:S(2)}, u32[]{:S(2)}) collective-permute-start(f32[64,64]{1,0:T(8,128)S(1)} %add_add_fusion.5), channel_id=1, source_target_pairs={{0,8},{8,0},{16,24},{24,16},{1,9},{9,1},{17,25},{25,17},{2,10},{10... | collective-permute-start | bytes 49160 | tf_op jit(solution)/shard_map/ppermute | solution.py:55
  114.9 2.9 %factor_left.1 = (f32[64,64]{1,0:T(8,128)S(1)}, f32[64,64]{1,0:T(8,128)S(1)}, f32[64,768]{1,0:T(8,128)}) custom-call(f32[64,64]{1,0:T(8,128)S(1)} %get-tuple-element.84.gram_ref, f32[64,768]{1,0:T(8,128)S(1)} %get-tuple-element.85.rows_ref), custom_call_target="tpu_custom_call" | custom-call | tf_op jit(solution)/shard_map/factor_left/pallas_call | solution.py:43
  117.8 3.4 %factor_right.1 = (f32[2,64,64]{2,1,0:T(8,128)}, f32[64,768]{1,0:T(8,128)}) custom-call(f32[64,64]{1,0:T(8,128)S(1)} %add_add_fusion.4.gram_ref, f32[64,768]{1,0:T(8,128)S(1)} %get-tuple-element.88.rows_ref, f32[64,64]{1,0:T(8,128)S(1)} %get-tuple-element.89.left_low_ref, f32[64,64]{1,0:T(8,128)S(1)} %get-tuple-element.90.left_inverse_ref), custom_call_target="tpu_custom_call" | custom-call | tf_op jit(solution)/shard_map/factor_right/pallas_call | solution.py:43
  (49 shorter events, 4.3 us)
Async XLA Ops:
  1.6 12.7 %collective-permute-start.3 = (bf16[64,768]{1,0:T(8,128)(2,1)S(1)}, bf16[64,768]{1,0:T(8,128)(2,1)S(1)}, u32[]{:S(2)}, u32[]{:S(2)}) collective-permute-start(bf16[64,768]{1,0:T(8,128)(2,1)S(1)} %convert_element_type.3.rest_0_), channel_id=1, source_target_pairs={{0,6},{1,7},{2,4},{3,5},{4,2},{5,3},{6,0},{7,1},{8,14},{9,15},{10,... | collective-permute-start | bytes 294920 | tf_op jit(solution)/shard_map/ppermute | solution.py:55
  5.6 8.7 %collective-permute-start.2 = (bf16[64,768]{1,0:T(8,128)(2,1)S(1)}, bf16[64,768]{1,0:T(8,128)(2,1)S(1)}, u32[]{:S(2)}, u32[]{:S(2)}) collective-permute-start(bf16[64,768]{1,0:T(8,128)(2,1)S(1)} %convert_element_type.3.rest_0_), channel_id=1, source_target_pairs={{0,4},{1,5},{2,6},{3,7},{4,0},{5,1},{6,2},{7,3},{8,12},{9,13},{10,... | collective-permute-start | bytes 294920 | tf_op jit(solution)/shard_map/ppermute | solution.py:55
  6.1 8.2 %collective-permute-start.1 = (bf16[64,768]{1,0:T(8,128)(2,1)S(1)}, bf16[64,768]{1,0:T(8,128)(2,1)S(1)}, u32[]{:S(2)}, u32[]{:S(2)}) collective-permute-start(bf16[64,768]{1,0:T(8,128)(2,1)S(1)} %convert_element_type.3.rest_0_), channel_id=1, source_target_pairs={{0,2},{1,3},{2,0},{3,1},{4,6},{5,7},{6,4},{7,5},{8,10},{9,11},{10,... | collective-permute-start | bytes 294920 | tf_op jit(solution)/shard_map/ppermute | solution.py:55
  6.2 9.1 %collective-permute-start = (bf16[64,768]{1,0:T(8,128)(2,1)S(1)}, bf16[64,768]{1,0:T(8,128)(2,1)S(1)}, u32[]{:S(2)}, u32[]{:S(2)}) collective-permute-start(bf16[64,768]{1,0:T(8,128)(2,1)S(1)} %convert_element_type.3.rest_0_), channel_id=1, source_target_pairs={{0,1},{1,0},{2,3},{3,2},{4,5},{5,4},{6,7},{7,6},{8,9},{9,8},{10,11... | collective-permute-start | bytes 294920 | tf_op jit(solution)/shard_map/ppermute | solution.py:55
  6.2 1.2 copy-start
  7.4 1.2 copy-start.1
  8.6 0.9 copy-start.2
  14.3 1.5 %collective-permute-start.4 = (bf16[64,768]{1,0:T(8,128)(2,1)S(1)}, bf16[64,768]{1,0:T(8,128)(2,1)S(1)}, u32[]{:S(2)}, u32[]{:S(2)}) collective-permute-start(bf16[64,768]{1,0:T(8,128)(2,1)S(1)} %collective-permute-done.1.rest_2_), channel_id=1, source_target_pairs={{0,1},{1,0},{2,3},{3,2},{4,5},{5,4},{6,7},{7,6},{8,9},{9,8},{10,11... | collective-permute-start | bytes 294920 | tf_op jit(solution)/shard_map/ppermute | solution.py:55
  14.8 1.3 %collective-permute-start.5 = (bf16[64,768]{1,0:T(8,128)(2,1)S(1)}, bf16[64,768]{1,0:T(8,128)(2,1)S(1)}, u32[]{:S(2)}, u32[]{:S(2)}) collective-permute-start(bf16[64,768]{1,0:T(8,128)(2,1)S(1)} %collective-permute-done.2.rest_4_), channel_id=1, source_target_pairs={{0,1},{1,0},{2,3},{3,2},{4,5},{5,4},{6,7},{7,6},{8,9},{9,8},{10,11... | collective-permute-start | bytes 294920 | tf_op jit(solution)/shard_map/ppermute | solution.py:55
  14.9 1.4 %collective-permute-start.6 = (bf16[64,768]{1,0:T(8,128)(2,1)S(1)}, bf16[64,768]{1,0:T(8,128)(2,1)S(1)}, u32[]{:S(2)}, u32[]{:S(2)}) collective-permute-start(bf16[64,768]{1,0:T(8,128)(2,1)S(1)} %collective-permute-done.3.rest_6_), channel_id=1, source_target_pairs={{0,1},{1,0},{2,3},{3,2},{4,5},{5,4},{6,7},{7,6},{8,9},{9,8},{10,11... | collective-permute-start | bytes 294920 | tf_op jit(solution)/shard_map/ppermute | solution.py:55
  23.4 11.9 %collective-permute-start.8 = (bf16[64,768]{1,0:T(8,128)(2,1)S(1)}, bf16[64,768]{1,0:T(8,128)(2,1)S(1)}, u32[]{:S(2)}, u32[]{:S(2)}) collective-permute-start(bf16[64,768]{1,0:T(8,128)(2,1)S(1)} %get-tuple-element.57), channel_id=1, source_target_pairs={{0,16},{8,24},{16,0},{24,8},{1,17},{9,25},{17,1},{25,9},{2,18},{10... | collective-permute-start | bytes 294920 | tf_op jit(solution)/shard_map/ppermute | solution.py:55
  26.4 8.9 %collective-permute-start.9 = (bf16[64,768]{1,0:T(8,128)(2,1)S(1)}, bf16[64,768]{1,0:T(8,128)(2,1)S(1)}, u32[]{:S(2)}, u32[]{:S(2)}) collective-permute-start(bf16[64,768]{1,0:T(8,128)(2,1)S(1)} %get-tuple-element.58), channel_id=1, source_target_pairs={{0,24},{8,16},{16,8},{24,0},{1,25},{9,17},{17,9},{25,1},{2,26},{10... | collective-permute-start | bytes 294920 | tf_op jit(solution)/shard_map/ppermute | solution.py:55
  35.0 4.7 %collective-permute-start.7 = (bf16[64,768]{1,0:T(8,128)(2,1)S(1)}, bf16[64,768]{1,0:T(8,128)(2,1)S(1)}, u32[]{:S(2)}, u32[]{:S(2)}) collective-permute-start(bf16[64,768]{1,0:T(8,128)(2,1)S(1)} %get-tuple-element.56), channel_id=1, source_target_pairs={{0,8},{8,0},{16,24},{24,16},{1,9},{9,1},{17,25},{25,17},{2,10},{10... | collective-permute-start | bytes 294920 | tf_op jit(solution)/shard_map/ppermute | solution.py:55
  40.1 1.3 %collective-permute-start.10 = (f32[32,384]{1,0:T(8,128)S(1)}, f32[32,384]{1,0:T(8,128)S(1)}, u32[]{:S(2)}, u32[]{:S(2)}) collective-permute-start(f32[32,384]{1,0:T(8,128)S(1)} %get-tuple-element.64), channel_id=1, source_target_pairs={{0,1},{1,0},{2,3},{3,2},{4,5},{5,4},{6,7},{7,6},{8,9},{9,8},{10,11... | collective-permute-start | bytes 147464 | tf_op jit(solution)/shard_map/ppermute | solution.py:55
  41.4 5.1 %collective-permute-start.13 = (f32[32,384]{1,0:T(8,128)S(1)}, f32[32,384]{1,0:T(8,128)S(1)}, u32[]{:S(2)}, u32[]{:S(2)}) collective-permute-start(f32[32,384]{1,0:T(8,128)S(1)} %add.63), channel_id=1, source_target_pairs={{0,6},{1,7},{2,4},{3,5},{4,2},{5,3},{6,0},{7,1},{8,14},{9,15},{10,... | collective-permute-start | bytes 147464 | tf_op jit(solution)/shard_map/ppermute | solution.py:55
  43.9 4.1 %collective-permute-start.12 = (f32[32,384]{1,0:T(8,128)S(1)}, f32[32,384]{1,0:T(8,128)S(1)}, u32[]{:S(2)}, u32[]{:S(2)}) collective-permute-start(f32[32,384]{1,0:T(8,128)S(1)} %add.63), channel_id=1, source_target_pairs={{0,4},{1,5},{2,6},{3,7},{4,0},{5,1},{6,2},{7,3},{8,12},{9,13},{10,... | collective-permute-start | bytes 147464 | tf_op jit(solution)/shard_map/ppermute | solution.py:55
  44.4 4.1 %collective-permute-start.11 = (f32[32,384]{1,0:T(8,128)S(1)}, f32[32,384]{1,0:T(8,128)S(1)}, u32[]{:S(2)}, u32[]{:S(2)}) collective-permute-start(f32[32,384]{1,0:T(8,128)S(1)} %add.63), channel_id=1, source_target_pairs={{0,2},{1,3},{2,0},{3,1},{4,6},{5,7},{6,4},{7,5},{8,10},{9,11},{10,... | collective-permute-start | bytes 147464 | tf_op jit(solution)/shard_map/ppermute | solution.py:55
  48.5 6.5 %collective-permute-start.16 = (f32[32,384]{1,0:T(8,128)S(1)}, f32[32,384]{1,0:T(8,128)S(1)}, u32[]{:S(2)}, u32[]{:S(2)}) collective-permute-start(f32[32,384]{1,0:T(8,128)S(1)} %add_add_fusion.3), channel_id=1, source_target_pairs={{0,24},{8,16},{16,8},{24,0},{1,25},{9,17},{17,9},{25,1},{2,26},{10... | collective-permute-start | bytes 147464 | tf_op jit(solution)/shard_map/ppermute | solution.py:55
  51.1 5.0 %collective-permute-start.15 = (f32[32,384]{1,0:T(8,128)S(1)}, f32[32,384]{1,0:T(8,128)S(1)}, u32[]{:S(2)}, u32[]{:S(2)}) collective-permute-start(f32[32,384]{1,0:T(8,128)S(1)} %add_add_fusion.3), channel_id=1, source_target_pairs={{0,16},{8,24},{16,0},{24,8},{1,17},{9,25},{17,1},{25,9},{2,18},{10... | collective-permute-start | bytes 147464 | tf_op jit(solution)/shard_map/ppermute | solution.py:55
  51.1 5.0 %collective-permute-start.14 = (f32[32,384]{1,0:T(8,128)S(1)}, f32[32,384]{1,0:T(8,128)S(1)}, u32[]{:S(2)}, u32[]{:S(2)}) collective-permute-start(f32[32,384]{1,0:T(8,128)S(1)} %add_add_fusion.3), channel_id=1, source_target_pairs={{0,8},{8,0},{16,24},{24,16},{1,9},{9,1},{17,25},{25,17},{2,10},{10... | collective-permute-start | bytes 147464 | tf_op jit(solution)/shard_map/ppermute | solution.py:55
  56.1 1.3 %collective-permute-start.17 = (f32[32,384]{1,0:T(8,128)S(1)}, f32[32,384]{1,0:T(8,128)S(1)}, u32[]{:S(2)}, u32[]{:S(2)}) collective-permute-start(f32[32,384]{1,0:T(8,128)S(1)} %add_add_fusion.2.mine_ref), channel_id=1, source_target_pairs={{0,1},{1,0},{2,3},{3,2},{4,5},{5,4},{6,7},{7,6},{8,9},{9,8},{10,11... | collective-permute-start | bytes 147464 | tf_op jit(solution)/shard_map/ppermute | solution.py:55
  58.1 5.3 %collective-permute-start.20 = (bf16[64,768]{1,0:T(8,128)(2,1)S(1)}, bf16[64,768]{1,0:T(8,128)(2,1)S(1)}, u32[]{:S(2)}, u32[]{:S(2)}) collective-permute-start(bf16[64,768]{1,0:T(8,128)(2,1)S(1)} %get-tuple-element.65.p_ref), channel_id=1, source_target_pairs={{0,8},{8,0},{16,24},{24,16},{1,9},{9,1},{17,25},{25,17},{2,10},{10... | collective-permute-start | bytes 294920 | tf_op jit(solution)/shard_map/ppermute | solution.py:55
  59.2 8.3 %collective-permute-start.19 = (bf16[64,768]{1,0:T(8,128)(2,1)S(1)}, bf16[64,768]{1,0:T(8,128)(2,1)S(1)}, u32[]{:S(2)}, u32[]{:S(2)}) collective-permute-start(bf16[64,768]{1,0:T(8,128)(2,1)S(1)} %get-tuple-element.65.p_ref), channel_id=1, source_target_pairs={{0,24},{8,16},{16,8},{24,0},{1,25},{9,17},{17,9},{25,1},{2,26},{10... | collective-permute-start | bytes 294920 | tf_op jit(solution)/shard_map/ppermute | solution.py:55
  61.7 8.9 %collective-permute-start.18 = (bf16[64,768]{1,0:T(8,128)(2,1)S(1)}, bf16[64,768]{1,0:T(8,128)(2,1)S(1)}, u32[]{:S(2)}, u32[]{:S(2)}) collective-permute-start(bf16[64,768]{1,0:T(8,128)(2,1)S(1)} %get-tuple-element.65.p_ref), channel_id=1, source_target_pairs={{0,16},{8,24},{16,0},{24,8},{1,17},{9,25},{17,1},{25,9},{2,18},{10... | collective-permute-start | bytes 294920 | tf_op jit(solution)/shard_map/ppermute | solution.py:55
  72.0 2.1 %collective-permute-start.21 = (f32[3,64,768]{2,1,0:T(8,128)S(1)}, f32[3,64,768]{2,1,0:T(8,128)S(1)}, u32[]{:S(2)}, u32[]{:S(2)}) collective-permute-start(f32[3,64,768]{2,1,0:T(8,128)S(1)} %backward_3.1), channel_id=1, source_target_pairs={{0,1},{1,0},{2,3},{3,2},{4,5},{5,4},{6,7},{7,6},{8,9},{9,8},{10,11... | collective-permute-start | bytes 1769480 | tf_op jit(solution)/shard_map/ppermute | solution.py:55
  75.1 8.4 %collective-permute-start.22 = (f32[1,64,768]{2,1,0:T(8,128)S(1)}, f32[1,64,768]{2,1,0:T(8,128)S(1)}, u32[]{:S(2)}, u32[]{:S(2)}) collective-permute-start(f32[1,64,768]{2,1,0:T(8,128)S(1)} %get-tuple-element.73), channel_id=1, source_target_pairs={{0,1},{1,0},{2,3},{3,2},{4,5},{5,4},{6,7},{7,6},{8,9},{9,8},{10,11... | collective-permute-start | bytes 589832 | tf_op jit(solution)/shard_map/ppermute | solution.py:55
  75.3 5.6 %collective-permute-start.23 = (bf16[64,768]{1,0:T(8,128)(2,1)S(1)}, bf16[64,768]{1,0:T(8,128)(2,1)S(1)}, u32[]{:S(2)}, u32[]{:S(2)}) collective-permute-start(bf16[64,768]{1,0:T(8,128)(2,1)S(1)} %get-tuple-element.74), channel_id=1, source_target_pairs={{0,2},{1,3},{2,0},{3,1},{4,6},{5,7},{6,4},{7,5},{8,10},{9,11},{10,... | collective-permute-start | bytes 294920 | tf_op jit(solution)/shard_map/ppermute | solution.py:55
  75.9 5.9 %collective-permute-start.24 = (bf16[64,768]{1,0:T(8,128)(2,1)S(1)}, bf16[64,768]{1,0:T(8,128)(2,1)S(1)}, u32[]{:S(2)}, u32[]{:S(2)}) collective-permute-start(bf16[64,768]{1,0:T(8,128)(2,1)S(1)} %get-tuple-element.75), channel_id=1, source_target_pairs={{0,4},{1,5},{2,6},{3,7},{4,0},{5,1},{6,2},{7,3},{8,12},{9,13},{10,... | collective-permute-start | bytes 294920 | tf_op jit(solution)/shard_map/ppermute | solution.py:55
  77.4 6.1 %collective-permute-start.25 = (bf16[64,768]{1,0:T(8,128)(2,1)S(1)}, bf16[64,768]{1,0:T(8,128)(2,1)S(1)}, u32[]{:S(2)}, u32[]{:S(2)}) collective-permute-start(bf16[64,768]{1,0:T(8,128)(2,1)S(1)} %get-tuple-element.76), channel_id=1, source_target_pairs={{0,6},{1,7},{2,4},{3,5},{4,2},{5,3},{6,0},{7,1},{8,14},{9,15},{10,... | collective-permute-start | bytes 294920 | tf_op jit(solution)/shard_map/ppermute | solution.py:55
  83.9 1.3 %collective-permute-start.26 = (f32[32,448]{1,0:T(8,128)S(1)}, f32[32,448]{1,0:T(8,128)S(1)}, u32[]{:S(2)}, u32[]{:S(2)}) collective-permute-start(f32[32,448]{1,0:T(8,128)S(1)} %get-tuple-element.83), channel_id=1, source_target_pairs={{0,1},{1,0},{2,3},{3,2},{4,5},{5,4},{6,7},{7,6},{8,9},{9,8},{10,11... | collective-permute-start | bytes 172040 | tf_op jit(solution)/shard_map/ppermute | solution.py:55
  85.2 5.2 %collective-permute-start.29 = (f32[32,448]{1,0:T(8,128)S(1)}, f32[32,448]{1,0:T(8,128)S(1)}, u32[]{:S(2)}, u32[]{:S(2)}) collective-permute-start(f32[32,448]{1,0:T(8,128)S(1)} %add.70), channel_id=1, source_target_pairs={{0,6},{1,7},{2,4},{3,5},{4,2},{5,3},{6,0},{7,1},{8,14},{9,15},{10,... | collective-permute-start | bytes 172040 | tf_op jit(solution)/shard_map/ppermute | solution.py:55
  87.0 4.7 %collective-permute-start.28 = (f32[32,448]{1,0:T(8,128)S(1)}, f32[32,448]{1,0:T(8,128)S(1)}, u32[]{:S(2)}, u32[]{:S(2)}) collective-permute-start(f32[32,448]{1,0:T(8,128)S(1)} %add.70), channel_id=1, source_target_pairs={{0,4},{1,5},{2,6},{3,7},{4,0},{5,1},{6,2},{7,3},{8,12},{9,13},{10,... | collective-permute-start | bytes 172040 | tf_op jit(solution)/shard_map/ppermute | solution.py:55
  87.6 4.3 %collective-permute-start.27 = (f32[32,448]{1,0:T(8,128)S(1)}, f32[32,448]{1,0:T(8,128)S(1)}, u32[]{:S(2)}, u32[]{:S(2)}) collective-permute-start(f32[32,448]{1,0:T(8,128)S(1)} %add.70), channel_id=1, source_target_pairs={{0,2},{1,3},{2,0},{3,1},{4,6},{5,7},{6,4},{7,5},{8,10},{9,11},{10,... | collective-permute-start | bytes 172040 | tf_op jit(solution)/shard_map/ppermute | solution.py:55
  91.9 6.4 %collective-permute-start.32 = (f32[32,448]{1,0:T(8,128)S(1)}, f32[32,448]{1,0:T(8,128)S(1)}, u32[]{:S(2)}, u32[]{:S(2)}) collective-permute-start(f32[32,448]{1,0:T(8,128)S(1)} %add_add_fusion.1), channel_id=1, source_target_pairs={{0,24},{8,16},{16,8},{24,0},{1,25},{9,17},{17,9},{25,1},{2,26},{10... | collective-permute-start | bytes 172040 | tf_op jit(solution)/shard_map/ppermute | solution.py:55
  94.0 6.3 %collective-permute-start.31 = (f32[32,448]{1,0:T(8,128)S(1)}, f32[32,448]{1,0:T(8,128)S(1)}, u32[]{:S(2)}, u32[]{:S(2)}) collective-permute-start(f32[32,448]{1,0:T(8,128)S(1)} %add_add_fusion.1), channel_id=1, source_target_pairs={{0,16},{8,24},{16,0},{24,8},{1,17},{9,25},{17,1},{25,9},{2,18},{10... | collective-permute-start | bytes 172040 | tf_op jit(solution)/shard_map/ppermute | solution.py:55
  94.0 6.3 %collective-permute-start.30 = (f32[32,448]{1,0:T(8,128)S(1)}, f32[32,448]{1,0:T(8,128)S(1)}, u32[]{:S(2)}, u32[]{:S(2)}) collective-permute-start(f32[32,448]{1,0:T(8,128)S(1)} %add_add_fusion.1), channel_id=1, source_target_pairs={{0,8},{8,0},{16,24},{24,16},{1,9},{9,1},{17,25},{25,17},{2,10},{10... | collective-permute-start | bytes 172040 | tf_op jit(solution)/shard_map/ppermute | solution.py:55
  100.3 1.3 %collective-permute-start.33 = (f32[32,448]{1,0:T(8,128)S(1)}, f32[32,448]{1,0:T(8,128)S(1)}, u32[]{:S(2)}, u32[]{:S(2)}) collective-permute-start(f32[32,448]{1,0:T(8,128)S(1)} %add_add_fusion.mine_ref), channel_id=1, source_target_pairs={{0,1},{1,0},{2,3},{3,2},{4,5},{5,4},{6,7},{7,6},{8,9},{9,8},{10,11... | collective-permute-start | bytes 172040 | tf_op jit(solution)/shard_map/ppermute | solution.py:55
  102.8 1.2 collective-permute-start.34
  104.0 4.9 %collective-permute-start.37 = (f32[64,64]{1,0:T(8,128)S(1)}, f32[64,64]{1,0:T(8,128)S(1)}, u32[]{:S(2)}, u32[]{:S(2)}) collective-permute-start(f32[64,64]{1,0:T(8,128)S(1)} %add.77), channel_id=1, source_target_pairs={{0,6},{1,7},{2,4},{3,5},{4,2},{5,3},{6,0},{7,1},{8,14},{9,15},{10,... | collective-permute-start | bytes 49160 | tf_op jit(solution)/shard_map/ppermute | solution.py:55
  105.9 3.9 %collective-permute-start.36 = (f32[64,64]{1,0:T(8,128)S(1)}, f32[64,64]{1,0:T(8,128)S(1)}, u32[]{:S(2)}, u32[]{:S(2)}) collective-permute-start(f32[64,64]{1,0:T(8,128)S(1)} %add.77), channel_id=1, source_target_pairs={{0,4},{1,5},{2,6},{3,7},{4,0},{5,1},{6,2},{7,3},{8,12},{9,13},{10,... | collective-permute-start | bytes 49160 | tf_op jit(solution)/shard_map/ppermute | solution.py:55
  106.5 3.9 %collective-permute-start.35 = (f32[64,64]{1,0:T(8,128)S(1)}, f32[64,64]{1,0:T(8,128)S(1)}, u32[]{:S(2)}, u32[]{:S(2)}) collective-permute-start(f32[64,64]{1,0:T(8,128)S(1)} %add.77), channel_id=1, source_target_pairs={{0,2},{1,3},{2,0},{3,1},{4,6},{5,7},{6,4},{7,5},{8,10},{9,11},{10,... | collective-permute-start | bytes 49160 | tf_op jit(solution)/shard_map/ppermute | solution.py:55
  110.4 7.3 %collective-permute-start.40 = (f32[64,64]{1,0:T(8,128)S(1)}, f32[64,64]{1,0:T(8,128)S(1)}, u32[]{:S(2)}, u32[]{:S(2)}) collective-permute-start(f32[64,64]{1,0:T(8,128)S(1)} %add_add_fusion.5), channel_id=1, source_target_pairs={{0,24},{8,16},{16,8},{24,0},{1,25},{9,17},{17,9},{25,1},{2,26},{10... | collective-permute-start | bytes 49160 | tf_op jit(solution)/shard_map/ppermute | solution.py:55
  112.5 5.3 %collective-permute-start.39 = (f32[64,64]{1,0:T(8,128)S(1)}, f32[64,64]{1,0:T(8,128)S(1)}, u32[]{:S(2)}, u32[]{:S(2)}) collective-permute-start(f32[64,64]{1,0:T(8,128)S(1)} %add_add_fusion.5), channel_id=1, source_target_pairs={{0,16},{8,24},{16,0},{24,8},{1,17},{9,25},{17,1},{25,9},{2,18},{10... | collective-permute-start | bytes 49160 | tf_op jit(solution)/shard_map/ppermute | solution.py:55
  112.5 5.3 %collective-permute-start.38 = (f32[64,64]{1,0:T(8,128)S(1)}, f32[64,64]{1,0:T(8,128)S(1)}, u32[]{:S(2)}, u32[]{:S(2)}) collective-permute-start(f32[64,64]{1,0:T(8,128)S(1)} %add_add_fusion.5), channel_id=1, source_target_pairs={{0,8},{8,0},{16,24},{24,16},{1,9},{9,1},{17,25},{25,17},{2,10},{10... | collective-permute-start | bytes 49160 | tf_op jit(solution)/shard_map/ppermute | solution.py:55

commit v2 on v1

--- a/solution.py
+++ b/solution.py
@@ -7,6 +7,7 @@
 from jax.experimental.pallas import tpu as pltpu
 from jax.sharding import PartitionSpec as P
 
+
 f32 = jnp.float32
 bf16 = jnp.bfloat16
 CROSS = bf16
@@ -39,7 +40,7 @@
     return -(-count // 128) * 128
 
 
-def call(kernel, inputs, outputs, name, specs=None, scratch=(), mebibytes=8):
+def call(kernel, inputs, outputs, specs=None, scratch=(), mebibytes=8):
     return pl.pallas_call(
         kernel,
         in_specs=specs or [VMEM] * len(inputs),
@@ -47,7 +48,6 @@
         out_shape=outputs,
         scratch_shapes=list(scratch),
         compiler_params=limit(mebibytes),
-        name=name,
     )(*inputs)
 
 
@@ -85,72 +85,59 @@
     return copies
 
 
-def fetch(matrix, chunk, j, bases):
-    cols = matrix.shape[1]
-    flat = [b for group in bases for b in group]
-    width = flat[0].shape[1]
-    counts = [sum(b.shape[0] for b in group) for group in bases]
-    n_flat = len(flat)
-
-    def kernel(a_hbm, *rest):
-        sources, target, outs = rest[:n_flat], rest[n_flat], rest[n_flat + 1 : -n_flat - 2]
-        held, sems, base_sems = rest[-n_flat - 2 : -2], rest[-2], rest[-1]
-        brought = [pltpu.make_async_copy(src, dst, base_sems.at[n]) for n, (src, dst) in enumerate(zip(sources, held))]
+def fetch(matrix, chunk, j):
+    def kernel(a_hbm, target, sems):
         copies = fetch_copies(a_hbm, [target], sems, [j], chunk)
-        for copy in brought + copies:
+        for copy in copies:
             copy.start()
-        n_base = 0
-        for n, group in enumerate(bases):
-            rows_high, rows_low, turned = outs[3 * n : 3 * n + 3]
-            size = padded(counts[n])
-            if counts[n] != size:
-                rows_high[...] = jnp.zeros_like(rows_high)
-                rows_low[...] = jnp.zeros_like(rows_low)
-                turned[...] = jnp.zeros_like(turned)
-            at = 0
-            for _ in group:
-                brought[n_base].wait()
-                values = held[n_base][...]
-                n_base += 1
-                count = values.shape[0]
-                high, low = split(values)
-                rows_high[at : at + count, :] = high
-                rows_low[at : at + count, :] = low
-                high, low = split(values.T)
-                turned[:, at : at + count] = high
-                turned[:, size + at : size + at + count] = low
-                at += count
         for copy in copies:
             copy.wait()
 
-    outputs = [shape((chunk, cols), bf16)]
-    for count in counts:
-        size = padded(count)
-        outputs += [shape((size, width), bf16), shape((size, width), bf16), shape((width, 2 * size), bf16)]
-    return call(
-        kernel,
-        [matrix] + flat,
-        outputs,
-        "fetch",
-        specs=[ANY] * (1 + n_flat),
-        scratch=[pltpu.VMEM(b.shape, f32) for b in flat]
-        + [pltpu.SemaphoreType.DMA((1, HALVES)), pltpu.SemaphoreType.DMA((n_flat,))],
-    )
+    outputs = [shape((chunk, matrix.shape[1]), bf16)]
+    return call(kernel, [matrix], outputs, specs=[ANY], scratch=[pltpu.SemaphoreType.DMA((1, HALVES))], mebibytes=24)[0]
+
+
+def prepare(bases):
+    width = bases[0].shape[1]
+    total = sum(b.shape[0] for b in bases)
+    size = padded(total)
+
+    def kernel(*rest):
+        sources, (rows_high, rows_low, turned) = rest[: len(bases)], rest[len(bases) :]
+        if total != size:
+            rows_high[...] = jnp.zeros_like(rows_high)
+            rows_low[...] = jnp.zeros_like(rows_low)
+            turned[...] = jnp.zeros_like(turned)
+        at = 0
+        for source in sources:
+            values = source[...]
+            count = values.shape[0]
+            high, low = split(values)
+            rows_high[at : at + count, :] = high
+            rows_low[at : at + count, :] = low
+            high, low = split(values.T)
+            turned[:, at : at + count] = high
+            turned[:, size + at : size + at + count] = low
+            at += count
+
+    outputs = [shape((size, width), bf16), shape((size, width), bf16), shape((width, 2 * size), bf16)]
+    return call(kernel, list(bases), outputs)
 
 
 def forward(lefts, order, held, matrix, chunk, products, brought):
     cols = matrix.shape[1]
     block = lefts[0].shape[0]
     step = chunk // 3 if chunk % 384 == 0 else chunk
+    source = [matrix] if brought else []
 
     def kernel(*rest):
         rest = list(rest)
         parts = [rest.pop(0) for _ in lefts]
         chunks = {j: rest.pop(0) for j in held}
-        a_hbm = rest.pop(0)
+        a_hbm = [rest.pop(0) for _ in source]
         outs = [rest.pop(0) for _ in products]
         targets = [rest.pop(0) for _ in brought]
-        copies = fetch_copies(a_hbm, targets, rest[-1], brought, chunk)
+        copies = fetch_copies(a_hbm[0], targets, rest[-1], brought, chunk) if brought else []
         for copy in copies:
             copy.start()
         if order is None:
@@ -186,11 +173,11 @@
         outputs.append(shape((block, cols), bf16))
     return call(
         kernel,
-        list(lefts) + list(held.values()) + [matrix],
+        list(lefts) + list(held.values()) + source,
         outputs,
-        "forward_%d" % products[0],
-        specs=[VMEM] * (len(lefts) + len(held)) + [ANY],
-        scratch=[pltpu.SemaphoreType.DMA((len(brought), HALVES))],
+        specs=[VMEM] * (len(lefts) + len(held)) + [ANY] * len(source),
+        scratch=[pltpu.SemaphoreType.DMA((len(brought), HALVES))] if brought else [],
+        mebibytes=8,
     )
 
 
@@ -201,8 +188,7 @@
         got = dot16(p_ref[...], a_ref[...], ((1,), (0,)))
         rest[-1][...] = rest[0][...] + got if given else got
 
-    name = "backward_more" if given else "backward_own"
-    return call(kernel, [piece, chunk_j, *given], [shape((piece.shape[0], chunk_j.shape[1]))], name)[0]
+    return call(kernel, [piece, chunk_j, *given], [shape((piece.shape[0], chunk_j.shape[1]))])[0]
 
 
 def backward(pieces, chunks, begun, targets, parts):
@@ -222,7 +208,7 @@
                 out[n] = total
 
     outputs = [shape((len(wanted), block, width)) for wanted in targets]
-    return call(kernel, [*pieces, *chunks, begun], outputs, "backward_%d" % targets[0][0])
+    return call(kernel, [*pieces, *chunks, begun], outputs)
 
 
 def combine(mine, theirs):
@@ -232,7 +218,7 @@
         for n, out in enumerate(outs):
             out[...] = (mine_ref[n] + theirs_ref[n]).astype(CROSS)
 
-    return call(kernel, [mine, theirs], [shape((block, width), CROSS)] * count, "combine")
+    return call(kernel, [mine, theirs], [shape((block, width), CROSS)] * count)
 
 
 def coefficients(pieces, turned, total, further=None):
@@ -266,7 +252,6 @@
         kernel,
         [*pieces, turned, *given],
         [shape((block, width)), shape((half, count)), shape((half, count))],
-        "coefficients",
         scratch=[pltpu.VMEM((block, count), f32)],
     )
 
@@ -300,13 +285,7 @@
     outputs = [shape((block, width)), shape((block, width), bf16), shape((block, block))]
     if count > size:
         outputs.append(shape((block, count - size)))
-    return call(
-        kernel,
-        [image, rows_high, rows_low, mine, other],
-        outputs,
-        "project",
-        scratch=[pltpu.VMEM((block, count), f32)],
-    )
+    return call(kernel, [image, rows_high, rows_low, mine, other], outputs, scratch=[pltpu.VMEM((block, count), f32)])
 
 
 GROUP = 8
@@ -343,7 +322,7 @@
         new_ref[...] = dot32(inverse, rows_ref[...], ((1,), (0,)))
 
     small = shape(gram.shape)
-    return call(kernel, [gram, rows], [small, small, shape(rows.shape)], "factor_left")
+    return call(kernel, [gram, rows], [small, small, shape(rows.shape)])
 
 
 def factor_right(gram, rows, left_low, left_inverse):
@@ -355,25 +334,17 @@
         factors_ref[1] = low
         new_ref[...] = dot32(dot32(inverse, turn, ((1,), (0,))), rows_ref[...], ((1,), (0,)))
 
-    return call(
-        kernel,
-        [gram, rows, left_low, left_inverse],
-        [shape((2, *gram.shape)), shape(rows.shape)],
-        "factor_right",
-    )
+    return call(kernel, [gram, rows, left_low, left_inverse], [shape((2, *gram.shape)), shape(rows.shape)])
 
 
 def bases_split(bases):
-    out = []
-    for group in bases:
-        rows = jnp.concatenate(group, 0)
-        rows = jnp.pad(rows, ((0, padded(rows.shape[0]) - rows.shape[0]), (0, 0)))
-        high, low = split(rows)
-        out += [high, low, jnp.concatenate([high.T, low.T], 1)]
-    return out
-
-
-def shards(matrix, left_basis, right_basis, right_block, *, n_col, n_row):
+    rows = jnp.concatenate(bases, 0)
+    rows = jnp.pad(rows, ((0, padded(rows.shape[0]) - rows.shape[0]), (0, 0)))
+    high, low = split(rows)
+    return high, low, jnp.concatenate([high.T, low.T], 1)
+
+
+def step(matrix, left_basis, right_basis, right_block, *, n_col, n_row):
     total = left_basis.shape[1] * n_col * n_row
     chunk, width = matrix.shape[0] // n_col, matrix.shape[1] // n_row
     tiled = n_col == 4 and n_row == 8 and width % 128 == 0 and chunk % 32 == 0
@@ -392,11 +363,11 @@
         return mine, row_swap(mine, 1)
 
     rounded = right_block.astype(bf16)
-    bases = ([left_basis], [right_basis, right_block])
+    prepared_rows = prepare if tiled else bases_split
     if tiled:
         lefts = {m: row_swap(rounded, m) for m in range(2, n_row, 2)}
         lefts[0], lefts[1] = rounded, row_swap(rounded, 1)
-        chunk_2, *prepared = fetch(matrix, chunk, 2, bases)
+        chunk_2 = fetch(matrix, chunk, 2)
         chunk_2, *after = lax.optimization_barrier((chunk_2, *(lefts[m] for m in range(2, n_row, 2))))
         for m, values in zip(range(2, n_row, 2), after):
             lefts[m] = values
@@ -405,18 +376,22 @@
         piece_2, piece_3, chunk_3, chunk_1, whole = forward(
             [lefts[m] for m in order], order, {2: chunk_2}, matrix, chunk, [2, 3], [3, 1]
         )
-        piece_1, piece_0, chunk_0 = forward([whole], None, {1: chunk_1}, matrix, chunk, [1, 0], [0])
+        piece_1, chunk_0 = forward([whole], None, {1: chunk_1}, matrix, chunk, [1], [0])
+        (piece_0,) = forward([whole], None, {0: chunk_0}, matrix, chunk, [0], [])
         pieces = [piece_0, col_swap(piece_1, 1), col_swap(piece_2, 2), col_swap(piece_3, 3)]
     else:
-        prepared = bases_split(bases)
         whole = lax.all_gather(rounded, "row", axis=1, tiled=True)
         partial = dot16(whole, matrix, ((1,), (1,)))
         me = lax.axis_index("col")
         pieces = [lax.dynamic_slice_in_dim(partial, (me ^ j) * chunk, chunk, 1) for j in range(n_col)]
         pieces = [pieces[0]] + [col_swap(pieces[j].astype(CROSS), j) for j in range(1, n_col)]
-    left_high, left_low, left_turned, right_high, right_low, right_turned = prepared
-
+    if tiled:
+        pieces[0], left_basis = lax.optimization_barrier((pieces[0], left_basis))
+    left_high, left_low, left_turned = prepared_rows([left_basis])
     image, mine, theirs = coefficients(pieces, left_turned, total)
+    if tiled:
+        image, right_basis, right_block = lax.optimization_barrier((image, right_basis, right_block))
+    right_high, right_low, right_turned = prepared_rows([right_basis, right_block])
     mine, other = split_sum(mine, theirs)
     projected, low, gram = project(image, left_high, left_low, mine, other, total)
     lows = [col_swap(low, j) for j in range(1, n_col)]
@@ -457,5 +432,5 @@
         P(None, ("col", "row")),
     )
     out_specs = (P(None, ("row", "col")), P(None, ("col", "row")), P())
-    body = functools.partial(shards, n_col=mesh.shape["col"], n_row=mesh.shape["row"])
+    body = functools.partial(step, n_col=mesh.shape["col"], n_row=mesh.shape["row"])
     return jax.shard_map(body, mesh=mesh, in_specs=in_specs, out_specs=out_specs, check_vma=False)

time: 121 us -> 115 us (0.950)
  local copies, waits for them, and re-layouts: 3.33 us -> 0.02 us
  waiting for transfers between devices: 38.6 us -> 35.9 us
    unnamed x6, local copies, waits for them, and re-layouts: 3.33 us -> 0.02 us
    ppermute x41, waiting for transfers between devices: 38.6 us -> 35.9 us  [swap(): return lax.ppermute(values, axis, [(i, i ^ bit) for i in range(size)])]
    pallas_call x15 -> x18, Pallas kernels: 35.3 us -> 35.5 us  [call(): pl.pallas_call(kernel, in_specs=specs or [VMEM] * len(inputs), out_specs=...]
  transfers between devices with their start and end apart: 41 -> 41, of which waited for: 28 -> 30; matrix products, arithmetic and copies ran while one was open for 0% -> 0% of each run, Pallas kernels for 16% -> 17%
where the time goes in v2:
time: 115 us; the launch traced here: 114 us
  starting transfers between devices  41.1 us (36%)
  waiting for transfers between devices  35.9 us (31%)
  Pallas kernels  35.5 us (31%)
    ppermute x41, starting transfers between devices, swap(): return lax.ppermute(values, axis, [(i, i ^ bit) for i in range(size)])  41.1 us
    ppermute x41, waiting for transfers between devices, swap(): return lax.ppermute(values, axis, [(i, i ^ bit) for i in range(size)])  35.9 us
    pallas_call x18, Pallas kernels, call(): pl.pallas_call(kernel, in_specs=specs or [VMEM] * len(inputs), out_specs=...  35.5 us
  transfers between devices with their start and end apart: 41, of which 30 were waited for; matrix products, arithmetic and copies ran while one was open for 0% of the time, Pallas kernels for 17%

profile of v2, /device:TPU:0, one launch (start us, length us, event | category | flops | bytes accessed | tf_op | source)
XLA Modules:
  0.0 114.4 jit_solution(15453757816753692237)
XLA Ops:
  0.6 0.9 convert_element_type.3.rest_0_
  1.6 4.0 %collective-permute-start.3 = (bf16[64,768]{1,0:T(8,128)(2,1)S(1)}, bf16[64,768]{1,0:T(8,128)(2,1)S(1)}, u32[]{:S(2)}, u32[]{:S(2)}) collective-permute-start(bf16[64,768]{1,0:T(8,128)(2,1)S(1)} %convert_element_type.3.rest_0_), channel_id=1, source_target_pairs={{0,6},{1,7},{2,4},{3,5},{4,2},{5,3},{6,0},{7,1},{8,14},{9,15},{10,... | collective-permute-start | bytes 294920 | tf_op jit(solution)/shard_map/ppermute | solution.py:55
  5.6 0.5 collective-permute-start.2
  6.2 3.8 %shard_map.67.rest_8_.rest_2_ = bf16[768,6144]{1,0:T(8,128)(2,1)S(1)} custom-call(bf16[3072,6144]{1,0:T(8,128)(2,1)} %rest_2_.1), custom_call_target="tpu_custom_call" | custom-call | tf_op jit(solution)/shard_map/pallas_call | solution.py:44
  10.8 0.5 collective-permute-start.5
  11.3 0.8 collective-permute-done.4.rest_3_
  12.6 7.1 %shard_map.68 = (bf16[64,768]{1,0:T(8,128)(2,1)S(1)}, bf16[64,768]{1,0:T(8,128)(2,1)S(1)}, bf16[768,6144]{1,0:T(8,128)(2,1)S(1)}, bf16[768,6144]{1,0:T(8,128)(2,1)S(1)}, bf16[64,6144]{1,0:T(8,128)(2,1)S(1)}) custom-call(bf16[64,768]{1,0:T(8,128)(2,1)S(1)} %convert_element_type.3.rest_0_, bf16[64,768]{1,0:T(8,128)(2,1)S(1)} %collective-permute-done.rest_1_, ...), custom_call_target="tpu_custom_call" | custom-call | tf_op jit(solution)/shard_map/pallas_call | solution.py:44
  19.7 2.7 %collective-permute-start.8 = (bf16[64,768]{1,0:T(8,128)(2,1)S(1)}, bf16[64,768]{1,0:T(8,128)(2,1)S(1)}, u32[]{:S(2)}, u32[]{:S(2)}) collective-permute-start(bf16[64,768]{1,0:T(8,128)(2,1)S(1)} %get-tuple-element.60), channel_id=1, source_target_pairs={{0,16},{8,24},{16,0},{24,8},{1,17},{9,25},{17,1},{25,9},{2,18},{10... | collective-permute-start | bytes 294920 | tf_op jit(solution)/shard_map/ppermute | solution.py:55
  22.4 1.3 %collective-permute-start.9 = (bf16[64,768]{1,0:T(8,128)(2,1)S(1)}, bf16[64,768]{1,0:T(8,128)(2,1)S(1)}, u32[]{:S(2)}, u32[]{:S(2)}) collective-permute-start(bf16[64,768]{1,0:T(8,128)(2,1)S(1)} %get-tuple-element.61), channel_id=1, source_target_pairs={{0,24},{8,16},{16,8},{24,0},{1,25},{9,17},{17,9},{25,1},{2,26},{10... | collective-permute-start | bytes 294920 | tf_op jit(solution)/shard_map/ppermute | solution.py:55
  23.7 3.8 %shard_map.69 = (bf16[64,768]{1,0:T(8,128)(2,1)S(1)}, bf16[768,6144]{1,0:T(8,128)(2,1)S(1)}) custom-call(bf16[64,6144]{1,0:T(8,128)(2,1)S(1)} %get-tuple-element.55.rest_0_, bf16[768,6144]{1,0:T(8,128)(2,1)S(1)} %get-tuple-element.56.rest_1_.a_ref, bf16[3072,6144]{1,0:T(8,128)(2,1)} %rest_2_.1), custom_call_target="tpu_custom_call" | custom-call | tf_op jit(solution)/shard_map/pallas_call | solution.py:44
  27.8 3.4 %shard_map.70.rest_0_ = f32[64,768]{1,0:T(8,128)S(1)} custom-call(bf16[64,6144]{1,0:T(8,128)(2,1)S(1)} %get-tuple-element.55.rest_0_, bf16[768,6144]{1,0:T(8,128)(2,1)S(1)} %get-tuple-element.57.rest_1_.a_ref), custom_call_target="tpu_custom_call" | custom-call | tf_op jit(solution)/shard_map/pallas_call | solution.py:44
  31.7 0.6 collective-permute-done.7.rest_1_
  32.8 1.2 %collective-permute-done.10 = f32[32,384]{1,0:T(8,128)S(1)} collective-permute-done((f32[32,384]{1,0:T(8,128)S(1)}, f32[32,384]{1,0:T(8,128)S(1)}, u32[]{:S(2)}, u32[]{:S(2)}) %collective-permute-start.10) | collective-permute-done | bytes 49184 | tf_op jit(solution)/shard_map/ppermute | solution.py:55
  34.1 2.4 %collective-permute-start.13 = (f32[32,384]{1,0:T(8,128)S(1)}, f32[32,384]{1,0:T(8,128)S(1)}, u32[]{:S(2)}, u32[]{:S(2)}) collective-permute-start(f32[32,384]{1,0:T(8,128)S(1)} %add.63), channel_id=1, source_target_pairs={{0,6},{1,7},{2,4},{3,5},{4,2},{5,3},{6,0},{7,1},{8,14},{9,15},{10,... | collective-permute-start | bytes 147464 | tf_op jit(solution)/shard_map/ppermute | solution.py:55
  36.5 0.6 collective-permute-start.12
  37.1 0.6 collective-permute-start.11
  37.6 1.5 %collective-permute-done.13 = f32[32,384]{1,0:T(8,128)S(1)} collective-permute-done((f32[32,384]{1,0:T(8,128)S(1)}, f32[32,384]{1,0:T(8,128)S(1)}, u32[]{:S(2)}, u32[]{:S(2)}) %collective-permute-start.13) | collective-permute-done | bytes 49184 | tf_op jit(solution)/shard_map/ppermute | solution.py:55
  39.1 1.5 %collective-permute-done.12 = f32[32,384]{1,0:T(8,128)S(1)} collective-permute-done((f32[32,384]{1,0:T(8,128)S(1)}, f32[32,384]{1,0:T(8,128)S(1)}, u32[]{:S(2)}, u32[]{:S(2)}) %collective-permute-start.12) | collective-permute-done | bytes 49184 | tf_op jit(solution)/shard_map/ppermute | solution.py:55
  40.6 0.6 collective-permute-done.11
  41.2 3.2 %collective-permute-start.16 = (f32[32,384]{1,0:T(8,128)S(1)}, f32[32,384]{1,0:T(8,128)S(1)}, u32[]{:S(2)}, u32[]{:S(2)}) collective-permute-start(f32[32,384]{1,0:T(8,128)S(1)} %add_add_fusion.3), channel_id=1, source_target_pairs={{0,24},{8,16},{16,8},{24,0},{1,25},{9,17},{17,9},{25,1},{2,26},{10... | collective-permute-start | bytes 147464 | tf_op jit(solution)/shard_map/ppermute | solution.py:55
  44.3 1.3 %collective-permute-start.14 = (f32[32,384]{1,0:T(8,128)S(1)}, f32[32,384]{1,0:T(8,128)S(1)}, u32[]{:S(2)}, u32[]{:S(2)}) collective-permute-start(f32[32,384]{1,0:T(8,128)S(1)} %add_add_fusion.3), channel_id=1, source_target_pairs={{0,8},{8,0},{16,24},{24,16},{1,9},{9,1},{17,25},{25,17},{2,10},{10... | collective-permute-start | bytes 147464 | tf_op jit(solution)/shard_map/ppermute | solution.py:55
  45.6 1.5 %collective-permute-done.16 = f32[32,384]{1,0:T(8,128)S(1)} collective-permute-done((f32[32,384]{1,0:T(8,128)S(1)}, f32[32,384]{1,0:T(8,128)S(1)}, u32[]{:S(2)}, u32[]{:S(2)}) %collective-permute-start.16) | collective-permute-done | bytes 49184 | tf_op jit(solution)/shard_map/ppermute | solution.py:55
  47.2 2.2 %collective-permute-done.15 = f32[32,384]{1,0:T(8,128)S(1)} collective-permute-done((f32[32,384]{1,0:T(8,128)S(1)}, f32[32,384]{1,0:T(8,128)S(1)}, u32[]{:S(2)}, u32[]{:S(2)}) %collective-permute-start.15) | collective-permute-done | bytes 49184 | tf_op jit(solution)/shard_map/ppermute | solution.py:55
  49.4 1.2 %collective-permute-done.17.other_ref = f32[32,384]{1,0:T(8,128)S(1)} collective-permute-done((f32[32,384]{1,0:T(8,128)S(1)}, f32[32,384]{1,0:T(8,128)S(1)}, u32[]{:S(2)}, u32[]{:S(2)}) %collective-permute-start.17) | collective-permute-done | bytes 49184 | tf_op jit(solution)/shard_map/ppermute | solution.py:55
  50.6 0.7 shard_map.73
  51.8 3.1 %collective-permute-start.19 = (bf16[64,768]{1,0:T(8,128)(2,1)S(1)}, bf16[64,768]{1,0:T(8,128)(2,1)S(1)}, u32[]{:S(2)}, u32[]{:S(2)}) collective-permute-start(bf16[64,768]{1,0:T(8,128)(2,1)S(1)} %get-tuple-element.70.p_ref), channel_id=1, source_target_pairs={{0,24},{8,16},{16,8},{24,0},{1,25},{9,17},{17,9},{25,1},{2,26},{10... | collective-permute-start | bytes 294920 | tf_op jit(solution)/shard_map/ppermute | solution.py:55
  54.9 1.7 %shard_map.74.rest_0_ = f32[64,6144]{1,0:T(8,128)S(1)} custom-call(bf16[64,768]{1,0:T(8,128)(2,1)S(1)} %get-tuple-element.70.p_ref, bf16[768,6144]{1,0:T(8,128)(2,1)S(1)} %get-tuple-element.57.rest_1_.a_ref), custom_call_target="tpu_custom_call" | custom-call | tf_op jit(solution)/shard_map/pallas_call | solution.py:44
  56.7 1.7 %shard_map.75.rest_4_ = f32[64,6144]{1,0:T(8,128)S(1)} custom-call(bf16[64,768]{1,0:T(8,128)(2,1)S(1)} %collective-permute-done.20.p_ref, bf16[768,6144]{1,0:T(8,128)(2,1)S(1)} %get-tuple-element.56.rest_1_.a_ref, f32[64,6144]{1,0:T(8,128)S(1)} %shard_map.74.rest_0_), custom_call_target="tpu_custom_call" | custom-call | tf_op jit(solution)/shard_map/pallas_call | solution.py:44
  58.4 2.3 %collective-permute-done.19.rest_1_ = bf16[64,768]{1,0:T(8,128)(2,1)S(1)} collective-permute-done((bf16[64,768]{1,0:T(8,128)(2,1)S(1)}, bf16[64,768]{1,0:T(8,128)(2,1)S(1)}, u32[]{:S(2)}, u32[]{:S(2)}) %collective-permute-start.19) | collective-permute-done | bytes 98336 | tf_op jit(solution)/shard_map/ppermute | solution.py:55
  60.8 3.1 %collective-permute-done.18.rest_0_ = bf16[64,768]{1,0:T(8,128)(2,1)S(1)} collective-permute-done((bf16[64,768]{1,0:T(8,128)(2,1)S(1)}, bf16[64,768]{1,0:T(8,128)(2,1)S(1)}, u32[]{:S(2)}, u32[]{:S(2)}) %collective-permute-start.18) | collective-permute-done | bytes 98336 | tf_op jit(solution)/shard_map/ppermute | solution.py:55
  63.8 1.4 %shard_map.77 = f32[3,64,768]{2,1,0:T(8,128)S(1)} custom-call(bf16[64,768]{1,0:T(8,128)(2,1)S(1)} %collective-permute-done.18.rest_0_, bf16[64,768]{1,0:T(8,128)(2,1)S(1)} %collective-permute-done.19.rest_1_, bf16[768,6144]{1,0:T(8,128)(2,1)S(1)} %shard_map.67.rest_8_.rest_2_, bf16[768,6144]{1,0:T(8,128)(2,1)S(1)} %get-tuple-element.71.rest_3_, ...), custom_call_target="tpu_custom_call" | custom-call | tf_op jit(solution)/shard_map/pallas_call | solution.py:44
  65.3 1.4 %shard_map.76.mine_ref = f32[3,64,768]{2,1,0:T(8,128)S(1)} custom-call(bf16[64,768]{1,0:T(8,128)(2,1)S(1)} %collective-permute-done.18.rest_0_, bf16[64,768]{1,0:T(8,128)(2,1)S(1)} %collective-permute-done.19.rest_1_, bf16[768,6144]{1,0:T(8,128)(2,1)S(1)} %shard_map.67.rest_8_.rest_2_, bf16[768,6144]{1,0:T(8,128)(2,1)S(1)} %get-tuple-element.71.rest_3_, ...), custom_call_target="tpu_custom_call" | custom-call | tf_op jit(solution)/shard_map/pallas_call | solution.py:44
  66.7 0.6 collective-permute-done.21.theirs_ref
  67.4 1.0 shard_map.79
  68.5 0.6 collective-permute-start.23
  69.1 1.5 %collective-permute-start.24 = (bf16[64,768]{1,0:T(8,128)(2,1)S(1)}, bf16[64,768]{1,0:T(8,128)(2,1)S(1)}, u32[]{:S(2)}, u32[]{:S(2)}) collective-permute-start(bf16[64,768]{1,0:T(8,128)(2,1)S(1)} %get-tuple-element.79), channel_id=1, source_target_pairs={{0,4},{1,5},{2,6},{3,7},{4,0},{5,1},{6,2},{7,3},{8,12},{9,13},{10,... | collective-permute-start | bytes 294920 | tf_op jit(solution)/shard_map/ppermute | solution.py:55
  70.6 1.4 %collective-permute-start.25 = (bf16[64,768]{1,0:T(8,128)(2,1)S(1)}, bf16[64,768]{1,0:T(8,128)(2,1)S(1)}, u32[]{:S(2)}, u32[]{:S(2)}) collective-permute-start(bf16[64,768]{1,0:T(8,128)(2,1)S(1)} %get-tuple-element.80), channel_id=1, source_target_pairs={{0,6},{1,7},{2,4},{3,5},{4,2},{5,3},{6,0},{7,1},{8,14},{9,15},{10,... | collective-permute-start | bytes 294920 | tf_op jit(solution)/shard_map/ppermute | solution.py:55
  72.0 0.7 shard_map.80
  72.7 1.5 %collective-permute-done.23.rest_2_ = bf16[64,768]{1,0:T(8,128)(2,1)S(1)} collective-permute-done((bf16[64,768]{1,0:T(8,128)(2,1)S(1)}, bf16[64,768]{1,0:T(8,128)(2,1)S(1)}, u32[]{:S(2)}, u32[]{:S(2)}) %collective-permute-start.23) | collective-permute-done | bytes 98336 | tf_op jit(solution)/shard_map/ppermute | solution.py:55
  74.2 0.9 collective-permute-done.24.rest_3_
  75.1 1.6 %collective-permute-done.25.rest_4_ = bf16[64,768]{1,0:T(8,128)(2,1)S(1)} collective-permute-done((bf16[64,768]{1,0:T(8,128)(2,1)S(1)}, bf16[64,768]{1,0:T(8,128)(2,1)S(1)}, u32[]{:S(2)}, u32[]{:S(2)}) %collective-permute-start.25) | collective-permute-done | bytes 98336 | tf_op jit(solution)/shard_map/ppermute | solution.py:55
  77.2 1.2 %collective-permute-done.26 = f32[32,448]{1,0:T(8,128)S(1)} collective-permute-done((f32[32,448]{1,0:T(8,128)S(1)}, f32[32,448]{1,0:T(8,128)S(1)}, u32[]{:S(2)}, u32[]{:S(2)}) %collective-permute-start.26) | collective-permute-done | bytes 57376 | tf_op jit(solution)/shard_map/ppermute | solution.py:55
  78.5 1.8 %collective-permute-start.29 = (f32[32,448]{1,0:T(8,128)S(1)}, f32[32,448]{1,0:T(8,128)S(1)}, u32[]{:S(2)}, u32[]{:S(2)}) collective-permute-start(f32[32,448]{1,0:T(8,128)S(1)} %add.70), channel_id=1, source_target_pairs={{0,6},{1,7},{2,4},{3,5},{4,2},{5,3},{6,0},{7,1},{8,14},{9,15},{10,... | collective-permute-start | bytes 172040 | tf_op jit(solution)/shard_map/ppermute | solution.py:55
  80.3 0.6 collective-permute-start.28
  80.9 1.1 collective-permute-start.27
  82.0 1.7 %collective-permute-done.29 = f32[32,448]{1,0:T(8,128)S(1)} collective-permute-done((f32[32,448]{1,0:T(8,128)S(1)}, f32[32,448]{1,0:T(8,128)S(1)}, u32[]{:S(2)}, u32[]{:S(2)}) %collective-permute-start.29) | collective-permute-done | bytes 57376 | tf_op jit(solution)/shard_map/ppermute | solution.py:55
  83.7 1.3 %collective-permute-done.28 = f32[32,448]{1,0:T(8,128)S(1)} collective-permute-done((f32[32,448]{1,0:T(8,128)S(1)}, f32[32,448]{1,0:T(8,128)S(1)}, u32[]{:S(2)}, u32[]{:S(2)}) %collective-permute-start.28) | collective-permute-done | bytes 57376 | tf_op jit(solution)/shard_map/ppermute | solution.py:55
  85.2 1.9 %collective-permute-start.32 = (f32[32,448]{1,0:T(8,128)S(1)}, f32[32,448]{1,0:T(8,128)S(1)}, u32[]{:S(2)}, u32[]{:S(2)}) collective-permute-start(f32[32,448]{1,0:T(8,128)S(1)} %add_add_fusion.1), channel_id=1, source_target_pairs={{0,24},{8,16},{16,8},{24,0},{1,25},{9,17},{17,9},{25,1},{2,26},{10... | collective-permute-start | bytes 172040 | tf_op jit(solution)/shard_map/ppermute | solution.py:55
  87.1 2.6 %collective-permute-start.30 = (f32[32,448]{1,0:T(8,128)S(1)}, f32[32,448]{1,0:T(8,128)S(1)}, u32[]{:S(2)}, u32[]{:S(2)}) collective-permute-start(f32[32,448]{1,0:T(8,128)S(1)} %add_add_fusion.1), channel_id=1, source_target_pairs={{0,8},{8,0},{16,24},{24,16},{1,9},{9,1},{17,25},{25,17},{2,10},{10... | collective-permute-start | bytes 172040 | tf_op jit(solution)/shard_map/ppermute | solution.py:55
  89.7 2.1 %collective-permute-done.32 = f32[32,448]{1,0:T(8,128)S(1)} collective-permute-done((f32[32,448]{1,0:T(8,128)S(1)}, f32[32,448]{1,0:T(8,128)S(1)}, u32[]{:S(2)}, u32[]{:S(2)}) %collective-permute-start.32) | collective-permute-done | bytes 57376 | tf_op jit(solution)/shard_map/ppermute | solution.py:55
  91.8 1.8 %collective-permute-done.31 = f32[32,448]{1,0:T(8,128)S(1)} collective-permute-done((f32[32,448]{1,0:T(8,128)S(1)}, f32[32,448]{1,0:T(8,128)S(1)}, u32[]{:S(2)}, u32[]{:S(2)}) %collective-permute-start.31) | collective-permute-done | bytes 57376 | tf_op jit(solution)/shard_map/ppermute | solution.py:55
  93.7 1.2 %collective-permute-done.33.other_ref = f32[32,448]{1,0:T(8,128)S(1)} collective-permute-done((f32[32,448]{1,0:T(8,128)S(1)}, f32[32,448]{1,0:T(8,128)S(1)}, u32[]{:S(2)}, u32[]{:S(2)}) %collective-permute-start.33) | collective-permute-done | bytes 57376 | tf_op jit(solution)/shard_map/ppermute | solution.py:55
  94.9 1.1 shard_map.82
  96.2 1.1 collective-permute-done.34
  97.3 1.9 %collective-permute-start.37 = (f32[64,64]{1,0:T(8,128)S(1)}, f32[64,64]{1,0:T(8,128)S(1)}, u32[]{:S(2)}, u32[]{:S(2)}) collective-permute-start(f32[64,64]{1,0:T(8,128)S(1)} %add.77), channel_id=1, source_target_pairs={{0,6},{1,7},{2,4},{3,5},{4,2},{5,3},{6,0},{7,1},{8,14},{9,15},{10,... | collective-permute-start | bytes 49160 | tf_op jit(solution)/shard_map/ppermute | solution.py:55
  99.2 0.6 collective-permute-start.36
  99.8 1.0 collective-permute-start.35
  100.7 1.4 %collective-permute-done.37 = f32[64,64]{1,0:T(8,128)S(1)} collective-permute-done((f32[64,64]{1,0:T(8,128)S(1)}, f32[64,64]{1,0:T(8,128)S(1)}, u32[]{:S(2)}, u32[]{:S(2)}) %collective-permute-start.37) | collective-permute-done | bytes 16416 | tf_op jit(solution)/shard_map/ppermute | solution.py:55
  102.2 0.9 collective-permute-done.36
  103.1 0.6 collective-permute-done.35
  103.7 1.9 %collective-permute-start.40 = (f32[64,64]{1,0:T(8,128)S(1)}, f32[64,64]{1,0:T(8,128)S(1)}, u32[]{:S(2)}, u32[]{:S(2)}) collective-permute-start(f32[64,64]{1,0:T(8,128)S(1)} %add_add_fusion.5), channel_id=1, source_target_pairs={{0,24},{8,16},{16,8},{24,0},{1,25},{9,17},{17,9},{25,1},{2,26},{10... | collective-permute-start | bytes 49160 | tf_op jit(solution)/shard_map/ppermute | solution.py:55
  105.7 2.5 %collective-permute-start.38 = (f32[64,64]{1,0:T(8,128)S(1)}, f32[64,64]{1,0:T(8,128)S(1)}, u32[]{:S(2)}, u32[]{:S(2)}) collective-permute-start(f32[64,64]{1,0:T(8,128)S(1)} %add_add_fusion.5), channel_id=1, source_target_pairs={{0,8},{8,0},{16,24},{24,16},{1,9},{9,1},{17,25},{25,17},{2,10},{10... | collective-permute-start | bytes 49160 | tf_op jit(solution)/shard_map/ppermute | solution.py:55
  108.1 2.9 %shard_map.83 = (f32[64,64]{1,0:T(8,128)S(1)}, f32[64,64]{1,0:T(8,128)S(1)}, f32[64,768]{1,0:T(8,128)}) custom-call(f32[64,64]{1,0:T(8,128)S(1)} %get-tuple-element.90.gram_ref, f32[64,768]{1,0:T(8,128)S(1)} %get-tuple-element.91.rows_ref), custom_call_target="tpu_custom_call" | custom-call | tf_op jit(solution)/shard_map/pallas_call | solution.py:44
  111.1 3.4 %shard_map.84 = (f32[2,64,64]{2,1,0:T(8,128)}, f32[64,768]{1,0:T(8,128)}) custom-call(f32[64,64]{1,0:T(8,128)S(1)} %add_add_fusion.4.gram_ref, f32[64,768]{1,0:T(8,128)S(1)} %get-tuple-element.94.rows_ref, f32[64,64]{1,0:T(8,128)S(1)} %get-tuple-element.95.left_low_ref, f32[64,64]{1,0:T(8,128)S(1)} %get-tuple-element.96.left_inverse_ref), custom_call_target="tpu_custom_call" | custom-call | tf_op jit(solution)/shard_map/pallas_call | solution.py:44
  (52 shorter events, 4.7 us)
Async XLA Ops:
  1.6 8.4 %collective-permute-start.3 = (bf16[64,768]{1,0:T(8,128)(2,1)S(1)}, bf16[64,768]{1,0:T(8,128)(2,1)S(1)}, u32[]{:S(2)}, u32[]{:S(2)}) collective-permute-start(bf16[64,768]{1,0:T(8,128)(2,1)S(1)} %convert_element_type.3.rest_0_), channel_id=1, source_target_pairs={{0,6},{1,7},{2,4},{3,5},{4,2},{5,3},{6,0},{7,1},{8,14},{9,15},{10,... | collective-permute-start | bytes 294920 | tf_op jit(solution)/shard_map/ppermute | solution.py:55
  5.6 4.9 %collective-permute-start.2 = (bf16[64,768]{1,0:T(8,128)(2,1)S(1)}, bf16[64,768]{1,0:T(8,128)(2,1)S(1)}, u32[]{:S(2)}, u32[]{:S(2)}) collective-permute-start(bf16[64,768]{1,0:T(8,128)(2,1)S(1)} %convert_element_type.3.rest_0_), channel_id=1, source_target_pairs={{0,4},{1,5},{2,6},{3,7},{4,0},{5,1},{6,2},{7,3},{8,12},{9,13},{10,... | collective-permute-start | bytes 294920 | tf_op jit(solution)/shard_map/ppermute | solution.py:55
  6.1 4.7 %collective-permute-start.1 = (bf16[64,768]{1,0:T(8,128)(2,1)S(1)}, bf16[64,768]{1,0:T(8,128)(2,1)S(1)}, u32[]{:S(2)}, u32[]{:S(2)}) collective-permute-start(bf16[64,768]{1,0:T(8,128)(2,1)S(1)} %convert_element_type.3.rest_0_), channel_id=1, source_target_pairs={{0,2},{1,3},{2,0},{3,1},{4,6},{5,7},{6,4},{7,5},{8,10},{9,11},{10,... | collective-permute-start | bytes 294920 | tf_op jit(solution)/shard_map/ppermute | solution.py:55
  6.2 5.1 %collective-permute-start = (bf16[64,768]{1,0:T(8,128)(2,1)S(1)}, bf16[64,768]{1,0:T(8,128)(2,1)S(1)}, u32[]{:S(2)}, u32[]{:S(2)}) collective-permute-start(bf16[64,768]{1,0:T(8,128)(2,1)S(1)} %convert_element_type.3.rest_0_), channel_id=1, source_target_pairs={{0,1},{1,0},{2,3},{3,2},{4,5},{5,4},{6,7},{7,6},{8,9},{9,8},{10,11... | collective-permute-start | bytes 294920 | tf_op jit(solution)/shard_map/ppermute | solution.py:55
  10.8 1.3 %collective-permute-start.4 = (bf16[64,768]{1,0:T(8,128)(2,1)S(1)}, bf16[64,768]{1,0:T(8,128)(2,1)S(1)}, u32[]{:S(2)}, u32[]{:S(2)}) collective-permute-start(bf16[64,768]{1,0:T(8,128)(2,1)S(1)} %collective-permute-done.1.rest_2_), channel_id=1, source_target_pairs={{0,1},{1,0},{2,3},{3,2},{4,5},{5,4},{6,7},{7,6},{8,9},{9,8},{10,11... | collective-permute-start | bytes 294920 | tf_op jit(solution)/shard_map/ppermute | solution.py:55
  10.8 1.5 %collective-permute-start.5 = (bf16[64,768]{1,0:T(8,128)(2,1)S(1)}, bf16[64,768]{1,0:T(8,128)(2,1)S(1)}, u32[]{:S(2)}, u32[]{:S(2)}) collective-permute-start(bf16[64,768]{1,0:T(8,128)(2,1)S(1)} %collective-permute-done.2.rest_4_), channel_id=1, source_target_pairs={{0,1},{1,0},{2,3},{3,2},{4,5},{5,4},{6,7},{7,6},{8,9},{9,8},{10,11... | collective-permute-start | bytes 294920 | tf_op jit(solution)/shard_map/ppermute | solution.py:55
  11.3 1.3 %collective-permute-start.6 = (bf16[64,768]{1,0:T(8,128)(2,1)S(1)}, bf16[64,768]{1,0:T(8,128)(2,1)S(1)}, u32[]{:S(2)}, u32[]{:S(2)}) collective-permute-start(bf16[64,768]{1,0:T(8,128)(2,1)S(1)} %collective-permute-done.3.rest_6_), channel_id=1, source_target_pairs={{0,1},{1,0},{2,3},{3,2},{4,5},{5,4},{6,7},{7,6},{8,9},{9,8},{10,11... | collective-permute-start | bytes 294920 | tf_op jit(solution)/shard_map/ppermute | solution.py:55
  19.7 12.0 %collective-permute-start.8 = (bf16[64,768]{1,0:T(8,128)(2,1)S(1)}, bf16[64,768]{1,0:T(8,128)(2,1)S(1)}, u32[]{:S(2)}, u32[]{:S(2)}) collective-permute-start(bf16[64,768]{1,0:T(8,128)(2,1)S(1)} %get-tuple-element.60), channel_id=1, source_target_pairs={{0,16},{8,24},{16,0},{24,8},{1,17},{9,25},{17,1},{25,9},{2,18},{10... | collective-permute-start | bytes 294920 | tf_op jit(solution)/shard_map/ppermute | solution.py:55
  22.4 9.3 %collective-permute-start.9 = (bf16[64,768]{1,0:T(8,128)(2,1)S(1)}, bf16[64,768]{1,0:T(8,128)(2,1)S(1)}, u32[]{:S(2)}, u32[]{:S(2)}) collective-permute-start(bf16[64,768]{1,0:T(8,128)(2,1)S(1)} %get-tuple-element.61), channel_id=1, source_target_pairs={{0,24},{8,16},{16,8},{24,0},{1,25},{9,17},{17,9},{25,1},{2,26},{10... | collective-permute-start | bytes 294920 | tf_op jit(solution)/shard_map/ppermute | solution.py:55
  27.5 3.7 %copy-start = (f32[320,768]{1,0:T(8,128)S(1)}, f32[320,768]{1,0:T(8,128)}, u32[]{:S(2)}) copy-start(f32[320,768]{1,0:T(8,128)} %rest_0_) | copy-start | bytes 2949124
  27.5 4.8 %collective-permute-start.7 = (bf16[64,768]{1,0:T(8,128)(2,1)S(1)}, bf16[64,768]{1,0:T(8,128)(2,1)S(1)}, u32[]{:S(2)}, u32[]{:S(2)}) collective-permute-start(bf16[64,768]{1,0:T(8,128)(2,1)S(1)} %get-tuple-element.59), channel_id=1, source_target_pairs={{0,8},{8,0},{16,24},{24,16},{1,9},{9,1},{17,25},{25,17},{2,10},{10... | collective-permute-start | bytes 294920 | tf_op jit(solution)/shard_map/ppermute | solution.py:55
  32.7 1.3 %collective-permute-start.10 = (f32[32,384]{1,0:T(8,128)S(1)}, f32[32,384]{1,0:T(8,128)S(1)}, u32[]{:S(2)}, u32[]{:S(2)}) collective-permute-start(f32[32,384]{1,0:T(8,128)S(1)} %get-tuple-element.69), channel_id=1, source_target_pairs={{0,1},{1,0},{2,3},{3,2},{4,5},{5,4},{6,7},{7,6},{8,9},{9,8},{10,11... | collective-permute-start | bytes 147464 | tf_op jit(solution)/shard_map/ppermute | solution.py:55
  34.1 5.1 %collective-permute-start.13 = (f32[32,384]{1,0:T(8,128)S(1)}, f32[32,384]{1,0:T(8,128)S(1)}, u32[]{:S(2)}, u32[]{:S(2)}) collective-permute-start(f32[32,384]{1,0:T(8,128)S(1)} %add.63), channel_id=1, source_target_pairs={{0,6},{1,7},{2,4},{3,5},{4,2},{5,3},{6,0},{7,1},{8,14},{9,15},{10,... | collective-permute-start | bytes 147464 | tf_op jit(solution)/shard_map/ppermute | solution.py:55
  36.5 4.1 %collective-permute-start.12 = (f32[32,384]{1,0:T(8,128)S(1)}, f32[32,384]{1,0:T(8,128)S(1)}, u32[]{:S(2)}, u32[]{:S(2)}) collective-permute-start(f32[32,384]{1,0:T(8,128)S(1)} %add.63), channel_id=1, source_target_pairs={{0,4},{1,5},{2,6},{3,7},{4,0},{5,1},{6,2},{7,3},{8,12},{9,13},{10,... | collective-permute-start | bytes 147464 | tf_op jit(solution)/shard_map/ppermute | solution.py:55
  37.1 4.1 %collective-permute-start.11 = (f32[32,384]{1,0:T(8,128)S(1)}, f32[32,384]{1,0:T(8,128)S(1)}, u32[]{:S(2)}, u32[]{:S(2)}) collective-permute-start(f32[32,384]{1,0:T(8,128)S(1)} %add.63), channel_id=1, source_target_pairs={{0,2},{1,3},{2,0},{3,1},{4,6},{5,7},{6,4},{7,5},{8,10},{9,11},{10,... | collective-permute-start | bytes 147464 | tf_op jit(solution)/shard_map/ppermute | solution.py:55
  41.2 6.0 %collective-permute-start.16 = (f32[32,384]{1,0:T(8,128)S(1)}, f32[32,384]{1,0:T(8,128)S(1)}, u32[]{:S(2)}, u32[]{:S(2)}) collective-permute-start(f32[32,384]{1,0:T(8,128)S(1)} %add_add_fusion.3), channel_id=1, source_target_pairs={{0,24},{8,16},{16,8},{24,0},{1,25},{9,17},{17,9},{25,1},{2,26},{10... | collective-permute-start | bytes 147464 | tf_op jit(solution)/shard_map/ppermute | solution.py:55
  44.3 5.0 %collective-permute-start.15 = (f32[32,384]{1,0:T(8,128)S(1)}, f32[32,384]{1,0:T(8,128)S(1)}, u32[]{:S(2)}, u32[]{:S(2)}) collective-permute-start(f32[32,384]{1,0:T(8,128)S(1)} %add_add_fusion.3), channel_id=1, source_target_pairs={{0,16},{8,24},{16,0},{24,8},{1,17},{9,25},{17,1},{25,9},{2,18},{10... | collective-permute-start | bytes 147464 | tf_op jit(solution)/shard_map/ppermute | solution.py:55
  44.3 5.0 %collective-permute-start.14 = (f32[32,384]{1,0:T(8,128)S(1)}, f32[32,384]{1,0:T(8,128)S(1)}, u32[]{:S(2)}, u32[]{:S(2)}) collective-permute-start(f32[32,384]{1,0:T(8,128)S(1)} %add_add_fusion.3), channel_id=1, source_target_pairs={{0,8},{8,0},{16,24},{24,16},{1,9},{9,1},{17,25},{25,17},{2,10},{10... | collective-permute-start | bytes 147464 | tf_op jit(solution)/shard_map/ppermute | solution.py:55
  49.3 1.3 %collective-permute-start.17 = (f32[32,384]{1,0:T(8,128)S(1)}, f32[32,384]{1,0:T(8,128)S(1)}, u32[]{:S(2)}, u32[]{:S(2)}) collective-permute-start(f32[32,384]{1,0:T(8,128)S(1)} %add_add_fusion.2.mine_ref), channel_id=1, source_target_pairs={{0,1},{1,0},{2,3},{3,2},{4,5},{5,4},{6,7},{7,6},{8,9},{9,8},{10,11... | collective-permute-start | bytes 147464 | tf_op jit(solution)/shard_map/ppermute | solution.py:55
  51.4 5.3 %collective-permute-start.20 = (bf16[64,768]{1,0:T(8,128)(2,1)S(1)}, bf16[64,768]{1,0:T(8,128)(2,1)S(1)}, u32[]{:S(2)}, u32[]{:S(2)}) collective-permute-start(bf16[64,768]{1,0:T(8,128)(2,1)S(1)} %get-tuple-element.70.p_ref), channel_id=1, source_target_pairs={{0,8},{8,0},{16,24},{24,16},{1,9},{9,1},{17,25},{25,17},{2,10},{10... | collective-permute-start | bytes 294920 | tf_op jit(solution)/shard_map/ppermute | solution.py:55
  51.8 9.0 %collective-permute-start.19 = (bf16[64,768]{1,0:T(8,128)(2,1)S(1)}, bf16[64,768]{1,0:T(8,128)(2,1)S(1)}, u32[]{:S(2)}, u32[]{:S(2)}) collective-permute-start(bf16[64,768]{1,0:T(8,128)(2,1)S(1)} %get-tuple-element.70.p_ref), channel_id=1, source_target_pairs={{0,24},{8,16},{16,8},{24,0},{1,25},{9,17},{17,9},{25,1},{2,26},{10... | collective-permute-start | bytes 294920 | tf_op jit(solution)/shard_map/ppermute | solution.py:55
  54.9 8.9 %collective-permute-start.18 = (bf16[64,768]{1,0:T(8,128)(2,1)S(1)}, bf16[64,768]{1,0:T(8,128)(2,1)S(1)}, u32[]{:S(2)}, u32[]{:S(2)}) collective-permute-start(bf16[64,768]{1,0:T(8,128)(2,1)S(1)} %get-tuple-element.70.p_ref), channel_id=1, source_target_pairs={{0,16},{8,24},{16,0},{24,8},{1,17},{9,25},{17,1},{25,9},{2,18},{10... | collective-permute-start | bytes 294920 | tf_op jit(solution)/shard_map/ppermute | solution.py:55
  65.2 2.1 %collective-permute-start.21 = (f32[3,64,768]{2,1,0:T(8,128)S(1)}, f32[3,64,768]{2,1,0:T(8,128)S(1)}, u32[]{:S(2)}, u32[]{:S(2)}) collective-permute-start(f32[3,64,768]{2,1,0:T(8,128)S(1)} %shard_map.77), channel_id=1, source_target_pairs={{0,1},{1,0},{2,3},{3,2},{4,5},{5,4},{6,7},{7,6},{8,9},{9,8},{10,11... | collective-permute-start | bytes 1769480 | tf_op jit(solution)/shard_map/ppermute | solution.py:55
  67.4 4.7 %copy-start.1 = (f32[320,768]{1,0:T(8,128)S(1)}, f32[320,768]{1,0:T(8,128)}, u32[]{:S(2)}) copy-start(f32[320,768]{1,0:T(8,128)} %rest_0_.1) | copy-start | bytes 2949124
  67.4 4.7 %copy-start.2 = (f32[64,768]{1,0:T(8,128)S(1)}, f32[64,768]{1,0:T(8,128)}, u32[]{:S(2)}) copy-start(f32[64,768]{1,0:T(8,128)} %rest_1_) | copy-start | bytes 589828
  68.4 8.3 %collective-permute-start.22 = (f32[1,64,768]{2,1,0:T(8,128)S(1)}, f32[1,64,768]{2,1,0:T(8,128)S(1)}, u32[]{:S(2)}, u32[]{:S(2)}) collective-permute-start(f32[1,64,768]{2,1,0:T(8,128)S(1)} %get-tuple-element.77), channel_id=1, source_target_pairs={{0,1},{1,0},{2,3},{3,2},{4,5},{5,4},{6,7},{7,6},{8,9},{9,8},{10,11... | collective-permute-start | bytes 589832 | tf_op jit(solution)/shard_map/ppermute | solution.py:55
  68.5 5.7 %collective-permute-start.23 = (bf16[64,768]{1,0:T(8,128)(2,1)S(1)}, bf16[64,768]{1,0:T(8,128)(2,1)S(1)}, u32[]{:S(2)}, u32[]{:S(2)}) collective-permute-start(bf16[64,768]{1,0:T(8,128)(2,1)S(1)} %get-tuple-element.78), channel_id=1, source_target_pairs={{0,2},{1,3},{2,0},{3,1},{4,6},{5,7},{6,4},{7,5},{8,10},{9,11},{10,... | collective-permute-start | bytes 294920 | tf_op jit(solution)/shard_map/ppermute | solution.py:55
  69.1 6.0 %collective-permute-start.24 = (bf16[64,768]{1,0:T(8,128)(2,1)S(1)}, bf16[64,768]{1,0:T(8,128)(2,1)S(1)}, u32[]{:S(2)}, u32[]{:S(2)}) collective-permute-start(bf16[64,768]{1,0:T(8,128)(2,1)S(1)} %get-tuple-element.79), channel_id=1, source_target_pairs={{0,4},{1,5},{2,6},{3,7},{4,0},{5,1},{6,2},{7,3},{8,12},{9,13},{10,... | collective-permute-start | bytes 294920 | tf_op jit(solution)/shard_map/ppermute | solution.py:55
  70.6 6.1 %collective-permute-start.25 = (bf16[64,768]{1,0:T(8,128)(2,1)S(1)}, bf16[64,768]{1,0:T(8,128)(2,1)S(1)}, u32[]{:S(2)}, u32[]{:S(2)}) collective-permute-start(bf16[64,768]{1,0:T(8,128)(2,1)S(1)} %get-tuple-element.80), channel_id=1, source_target_pairs={{0,6},{1,7},{2,4},{3,5},{4,2},{5,3},{6,0},{7,1},{8,14},{9,15},{10,... | collective-permute-start | bytes 294920 | tf_op jit(solution)/shard_map/ppermute | solution.py:55
  77.1 1.3 %collective-permute-start.26 = (f32[32,448]{1,0:T(8,128)S(1)}, f32[32,448]{1,0:T(8,128)S(1)}, u32[]{:S(2)}, u32[]{:S(2)}) collective-permute-start(f32[32,448]{1,0:T(8,128)S(1)} %get-tuple-element.89), channel_id=1, source_target_pairs={{0,1},{1,0},{2,3},{3,2},{4,5},{5,4},{6,7},{7,6},{8,9},{9,8},{10,11... | collective-permute-start | bytes 172040 | tf_op jit(solution)/shard_map/ppermute | solution.py:55
  78.5 5.2 %collective-permute-start.29 = (f32[32,448]{1,0:T(8,128)S(1)}, f32[32,448]{1,0:T(8,128)S(1)}, u32[]{:S(2)}, u32[]{:S(2)}) collective-permute-start(f32[32,448]{1,0:T(8,128)S(1)} %add.70), channel_id=1, source_target_pairs={{0,6},{1,7},{2,4},{3,5},{4,2},{5,3},{6,0},{7,1},{8,14},{9,15},{10,... | collective-permute-start | bytes 172040 | tf_op jit(solution)/shard_map/ppermute | solution.py:55
  80.3 4.7 %collective-permute-start.28 = (f32[32,448]{1,0:T(8,128)S(1)}, f32[32,448]{1,0:T(8,128)S(1)}, u32[]{:S(2)}, u32[]{:S(2)}) collective-permute-start(f32[32,448]{1,0:T(8,128)S(1)} %add.70), channel_id=1, source_target_pairs={{0,4},{1,5},{2,6},{3,7},{4,0},{5,1},{6,2},{7,3},{8,12},{9,13},{10,... | collective-permute-start | bytes 172040 | tf_op jit(solution)/shard_map/ppermute | solution.py:55
  80.9 4.3 %collective-permute-start.27 = (f32[32,448]{1,0:T(8,128)S(1)}, f32[32,448]{1,0:T(8,128)S(1)}, u32[]{:S(2)}, u32[]{:S(2)}) collective-permute-start(f32[32,448]{1,0:T(8,128)S(1)} %add.70), channel_id=1, source_target_pairs={{0,2},{1,3},{2,0},{3,1},{4,6},{5,7},{6,4},{7,5},{8,10},{9,11},{10,... | collective-permute-start | bytes 172040 | tf_op jit(solution)/shard_map/ppermute | solution.py:55
  85.2 6.6 %collective-permute-start.32 = (f32[32,448]{1,0:T(8,128)S(1)}, f32[32,448]{1,0:T(8,128)S(1)}, u32[]{:S(2)}, u32[]{:S(2)}) collective-permute-start(f32[32,448]{1,0:T(8,128)S(1)} %add_add_fusion.1), channel_id=1, source_target_pairs={{0,24},{8,16},{16,8},{24,0},{1,25},{9,17},{17,9},{25,1},{2,26},{10... | collective-permute-start | bytes 172040 | tf_op jit(solution)/shard_map/ppermute | solution.py:55
  87.0 6.5 %collective-permute-start.31 = (f32[32,448]{1,0:T(8,128)S(1)}, f32[32,448]{1,0:T(8,128)S(1)}, u32[]{:S(2)}, u32[]{:S(2)}) collective-permute-start(f32[32,448]{1,0:T(8,128)S(1)} %add_add_fusion.1), channel_id=1, source_target_pairs={{0,16},{8,24},{16,0},{24,8},{1,17},{9,25},{17,1},{25,9},{2,18},{10... | collective-permute-start | bytes 172040 | tf_op jit(solution)/shard_map/ppermute | solution.py:55
  87.1 6.5 %collective-permute-start.30 = (f32[32,448]{1,0:T(8,128)S(1)}, f32[32,448]{1,0:T(8,128)S(1)}, u32[]{:S(2)}, u32[]{:S(2)}) collective-permute-start(f32[32,448]{1,0:T(8,128)S(1)} %add_add_fusion.1), channel_id=1, source_target_pairs={{0,8},{8,0},{16,24},{24,16},{1,9},{9,1},{17,25},{25,17},{2,10},{10... | collective-permute-start | bytes 172040 | tf_op jit(solution)/shard_map/ppermute | solution.py:55
  93.6 1.3 %collective-permute-start.33 = (f32[32,448]{1,0:T(8,128)S(1)}, f32[32,448]{1,0:T(8,128)S(1)}, u32[]{:S(2)}, u32[]{:S(2)}) collective-permute-start(f32[32,448]{1,0:T(8,128)S(1)} %add_add_fusion.mine_ref), channel_id=1, source_target_pairs={{0,1},{1,0},{2,3},{3,2},{4,5},{5,4},{6,7},{7,6},{8,9},{9,8},{10,11... | collective-permute-start | bytes 172040 | tf_op jit(solution)/shard_map/ppermute | solution.py:55
  96.0 1.2 %collective-permute-start.34 = (f32[64,64]{1,0:T(8,128)S(1)}, f32[64,64]{1,0:T(8,128)S(1)}, u32[]{:S(2)}, u32[]{:S(2)}) collective-permute-start(f32[64,64]{1,0:T(8,128)S(1)} %get-tuple-element.93), channel_id=1, source_target_pairs={{0,1},{1,0},{2,3},{3,2},{4,5},{5,4},{6,7},{7,6},{8,9},{9,8},{10,11... | collective-permute-start | bytes 49160 | tf_op jit(solution)/shard_map/ppermute | solution.py:55
  97.3 4.9 %collective-permute-start.37 = (f32[64,64]{1,0:T(8,128)S(1)}, f32[64,64]{1,0:T(8,128)S(1)}, u32[]{:S(2)}, u32[]{:S(2)}) collective-permute-start(f32[64,64]{1,0:T(8,128)S(1)} %add.77), channel_id=1, source_target_pairs={{0,6},{1,7},{2,4},{3,5},{4,2},{5,3},{6,0},{7,1},{8,14},{9,15},{10,... | collective-permute-start | bytes 49160 | tf_op jit(solution)/shard_map/ppermute | solution.py:55
  99.2 3.9 %collective-permute-start.36 = (f32[64,64]{1,0:T(8,128)S(1)}, f32[64,64]{1,0:T(8,128)S(1)}, u32[]{:S(2)}, u32[]{:S(2)}) collective-permute-start(f32[64,64]{1,0:T(8,128)S(1)} %add.77), channel_id=1, source_target_pairs={{0,4},{1,5},{2,6},{3,7},{4,0},{5,1},{6,2},{7,3},{8,12},{9,13},{10,... | collective-permute-start | bytes 49160 | tf_op jit(solution)/shard_map/ppermute | solution.py:55
  99.8 3.9 %collective-permute-start.35 = (f32[64,64]{1,0:T(8,128)S(1)}, f32[64,64]{1,0:T(8,128)S(1)}, u32[]{:S(2)}, u32[]{:S(2)}) collective-permute-start(f32[64,64]{1,0:T(8,128)S(1)} %add.77), channel_id=1, source_target_pairs={{0,2},{1,3},{2,0},{3,1},{4,6},{5,7},{6,4},{7,5},{8,10},{9,11},{10,... | collective-permute-start | bytes 49160 | tf_op jit(solution)/shard_map/ppermute | solution.py:55
  103.7 7.3 %collective-permute-start.40 = (f32[64,64]{1,0:T(8,128)S(1)}, f32[64,64]{1,0:T(8,128)S(1)}, u32[]{:S(2)}, u32[]{:S(2)}) collective-permute-start(f32[64,64]{1,0:T(8,128)S(1)} %add_add_fusion.5), channel_id=1, source_target_pairs={{0,24},{8,16},{16,8},{24,0},{1,25},{9,17},{17,9},{25,1},{2,26},{10... | collective-permute-start | bytes 49160 | tf_op jit(solution)/shard_map/ppermute | solution.py:55
  105.5 5.5 %collective-permute-start.39 = (f32[64,64]{1,0:T(8,128)S(1)}, f32[64,64]{1,0:T(8,128)S(1)}, u32[]{:S(2)}, u32[]{:S(2)}) collective-permute-start(f32[64,64]{1,0:T(8,128)S(1)} %add_add_fusion.5), channel_id=1, source_target_pairs={{0,16},{8,24},{16,0},{24,8},{1,17},{9,25},{17,1},{25,9},{2,18},{10... | collective-permute-start | bytes 49160 | tf_op jit(solution)/shard_map/ppermute | solution.py:55
  105.7 5.4 %collective-permute-start.38 = (f32[64,64]{1,0:T(8,128)S(1)}, f32[64,64]{1,0:T(8,128)S(1)}, u32[]{:S(2)}, u32[]{:S(2)}) collective-permute-start(f32[64,64]{1,0:T(8,128)S(1)} %add_add_fusion.5), channel_id=1, source_target_pairs={{0,8},{8,0},{16,24},{24,16},{1,9},{9,1},{17,25},{25,17},{2,10},{10... | collective-permute-start | bytes 49160 | tf_op jit(solution)/shard_map/ppermute | solution.py:55

commit v3 on v2

--- a/solution.py
+++ b/solution.py
@@ -327,12 +327,12 @@
 
 def factor_right(gram, rows, left_low, left_inverse):
     def kernel(gram_ref, rows_ref, left_low_ref, left_inverse_ref, factors_ref, new_ref):
-        turn = left_inverse_ref[...]
-        gram_here = dot32(dot32(turn, gram_ref[...], ((1,), (0,))), turn, ((1,), (1,)))
-        low, inverse = eliminate(gram_here)
+        low, inverse = eliminate(gram_ref[...])
+        new_ref[...] = dot32(inverse, rows_ref[...], ((1,), (0,)))
         factors_ref[0] = left_low_ref[...]
-        factors_ref[1] = low
-        new_ref[...] = dot32(dot32(inverse, turn, ((1,), (0,))), rows_ref[...], ((1,), (0,)))
+        line = lax.broadcasted_iota(jnp.int32, low.shape, 0)
+        lane = lax.broadcasted_iota(jnp.int32, low.shape, 1)
+        factors_ref[1] = jnp.where(line >= lane, dot32(left_inverse_ref[...], low, ((1,), (0,))), 0.0)
 
     return call(kernel, [gram, rows, left_low, left_inverse], [shape((2, *gram.shape)), shape(rows.shape)])
 
@@ -389,15 +389,14 @@
         pieces[0], left_basis = lax.optimization_barrier((pieces[0], left_basis))
     left_high, left_low, left_turned = prepared_rows([left_basis])
     image, mine, theirs = coefficients(pieces, left_turned, total)
-    if tiled:
-        image, right_basis, right_block = lax.optimization_barrier((image, right_basis, right_block))
-    right_high, right_low, right_turned = prepared_rows([right_basis, right_block])
     mine, other = split_sum(mine, theirs)
     projected, low, gram = project(image, left_high, left_low, mine, other, total)
-    lows = [col_swap(low, j) for j in range(1, n_col)]
     if tiled:
+        lows = [col_swap(low, j) for j in range(1, n_col)]
         begun = backward_begin(lows[0], chunk_1, backward_begin(low, chunk_0))
-        ready = (lows[1:], [chunk_2, chunk_3], begun)
+        begun = backward_begin(lows[1], chunk_2, begun)
+        begun, right_basis, right_block = lax.optimization_barrier((begun, right_basis, right_block))
+        ready = (lows[2:], [chunk_3], begun)
         far = list(range(2, n_row, 2))
         (theirs,) = backward(*ready, [[m + 1 for m in far]], n_row)
         theirs = row_swap(theirs, 1)
@@ -407,6 +406,7 @@
         theirs, mine = backward(*ready[:2], begun, [[1], [0]], n_row)
         pieces = [mine, row_swap(theirs, 1)] + pieces
     else:
+        lows = [col_swap(low, j) for j in range(1, n_col)]
         me_col, me = lax.axis_index("col"), lax.axis_index("row")
         partial = sum(
             dot16(piece, lax.dynamic_slice_in_dim(matrix, (me_col ^ g) * chunk, chunk, 0), ((1,), (0,)))
@@ -415,6 +415,7 @@
         cut = [lax.dynamic_slice_in_dim(partial, (me ^ j) * width, width, 1) for j in range(n_row)]
         mine = jnp.stack(cut[0::2]) + row_swap(jnp.stack(cut[1::2]), 1)
         pieces = [mine[0]] + [row_swap(mine[m].astype(CROSS), 2 * m) for m in range(1, n_row // 2)]
+    right_high, right_low, right_turned = prepared_rows([right_basis, right_block])
     coimage, mine, theirs = coefficients(pieces, right_turned, total, gram)
     mine, other = split_sum(mine, theirs)
     coprojected, _, cogram, gram = project(coimage, right_high, right_low, mine, other, total)

time: 115 us -> 113 us (0.983)
  waiting for transfers between devices: 35.9 us -> 33.2 us
  starting transfers between devices: 41.1 us -> 42.8 us
    ppermute x41, waiting for transfers between devices: 35.9 us -> 33.2 us  [swap(): return lax.ppermute(values, axis, [(i, i ^ bit) for i in range(size)])]
    ppermute x41, starting transfers between devices: 41.1 us -> 42.8 us  [swap(): return lax.ppermute(values, axis, [(i, i ^ bit) for i in range(size)])]
    pallas_call x18 -> x19, Pallas kernels: 35.5 us -> 35.2 us  [call(): pl.pallas_call(kernel, in_specs=specs or [VMEM] * len(inputs), out_specs=...]
  transfers between devices with their start and end apart: 41 -> 41, of which waited for: 30 -> 31; matrix products, arithmetic and copies ran while one was open for 0% -> 0% of each run, Pallas kernels for 17% -> 19%
where the time goes in v3:
time: 113 us
  starting transfers between devices  42.8 us (38%)
  Pallas kernels  35.2 us (31%)
  waiting for transfers between devices  33.2 us (29%)
    ppermute x41, starting transfers between devices, swap(): return lax.ppermute(values, axis, [(i, i ^ bit) for i in range(size)])  42.8 us
    pallas_call x19, Pallas kernels, call(): pl.pallas_call(kernel, in_specs=specs or [VMEM] * len(inputs), out_specs=...  35.2 us
    ppermute x41, waiting for transfers between devices, swap(): return lax.ppermute(values, axis, [(i, i ^ bit) for i in range(size)])  33.2 us
  transfers between devices with their start and end apart: 41, of which 31 were waited for; matrix products, arithmetic and copies ran while one was open for 0% of the time, Pallas kernels for 19%

profile of v3, /device:TPU:0, one launch (start us, length us, event | category | flops | bytes accessed | tf_op | source)
XLA Modules:
  0.0 113.2 jit_solution(10217027632210555367)
XLA Ops:
  0.6 0.9 convert_element_type.3.rest_0_
  1.6 4.0 %collective-permute-start.3 = (bf16[64,768]{1,0:T(8,128)(2,1)S(1)}, bf16[64,768]{1,0:T(8,128)(2,1)S(1)}, u32[]{:S(2)}, u32[]{:S(2)}) collective-permute-start(bf16[64,768]{1,0:T(8,128)(2,1)S(1)} %convert_element_type.3.rest_0_), channel_id=1, source_target_pairs={{0,6},{1,7},{2,4},{3,5},{4,2},{5,3},{6,0},{7,1},{8,14},{9,15},{10,... | collective-permute-start | bytes 294920 | tf_op jit(solution)/shard_map/ppermute | solution.py:55
  6.2 3.8 %shard_map.67.rest_8_.a_ref = bf16[768,6144]{1,0:T(8,128)(2,1)S(1)} custom-call(bf16[3072,6144]{1,0:T(8,128)(2,1)} %rest_2_.1), custom_call_target="tpu_custom_call" | custom-call | tf_op jit(solution)/shard_map/pallas_call | solution.py:44
  10.8 0.5 collective-permute-start.5
  11.3 0.8 collective-permute-done.4.rest_3_
  12.6 7.1 %shard_map.68 = (bf16[64,768]{1,0:T(8,128)(2,1)S(1)}, bf16[64,768]{1,0:T(8,128)(2,1)S(1)}, bf16[768,6144]{1,0:T(8,128)(2,1)S(1)}, bf16[768,6144]{1,0:T(8,128)(2,1)S(1)}, bf16[64,6144]{1,0:T(8,128)(2,1)S(1)}) custom-call(bf16[64,768]{1,0:T(8,128)(2,1)S(1)} %convert_element_type.3.rest_0_, bf16[64,768]{1,0:T(8,128)(2,1)S(1)} %collective-permute-done.rest_1_, ...), custom_call_target="tpu_custom_call" | custom-call | tf_op jit(solution)/shard_map/pallas_call | solution.py:44
  19.7 2.7 %collective-permute-start.8 = (bf16[64,768]{1,0:T(8,128)(2,1)S(1)}, bf16[64,768]{1,0:T(8,128)(2,1)S(1)}, u32[]{:S(2)}, u32[]{:S(2)}) collective-permute-start(bf16[64,768]{1,0:T(8,128)(2,1)S(1)} %get-tuple-element.60), channel_id=1, source_target_pairs={{0,16},{8,24},{16,0},{24,8},{1,17},{9,25},{17,1},{25,9},{2,18},{10... | collective-permute-start | bytes 294920 | tf_op jit(solution)/shard_map/ppermute | solution.py:55
  22.4 1.3 %collective-permute-start.9 = (bf16[64,768]{1,0:T(8,128)(2,1)S(1)}, bf16[64,768]{1,0:T(8,128)(2,1)S(1)}, u32[]{:S(2)}, u32[]{:S(2)}) collective-permute-start(bf16[64,768]{1,0:T(8,128)(2,1)S(1)} %get-tuple-element.61), channel_id=1, source_target_pairs={{0,24},{8,16},{16,8},{24,0},{1,25},{9,17},{17,9},{25,1},{2,26},{10... | collective-permute-start | bytes 294920 | tf_op jit(solution)/shard_map/ppermute | solution.py:55
  23.7 3.8 %shard_map.69 = (bf16[64,768]{1,0:T(8,128)(2,1)S(1)}, bf16[768,6144]{1,0:T(8,128)(2,1)S(1)}) custom-call(bf16[64,6144]{1,0:T(8,128)(2,1)S(1)} %get-tuple-element.55.rest_0_, bf16[768,6144]{1,0:T(8,128)(2,1)S(1)} %get-tuple-element.56.rest_1_.a_ref, bf16[3072,6144]{1,0:T(8,128)(2,1)} %rest_2_.1), custom_call_target="tpu_custom_call" | custom-call | tf_op jit(solution)/shard_map/pallas_call | solution.py:44
  27.8 3.4 %shard_map.70.rest_0_ = f32[64,768]{1,0:T(8,128)S(1)} custom-call(bf16[64,6144]{1,0:T(8,128)(2,1)S(1)} %get-tuple-element.55.rest_0_, bf16[768,6144]{1,0:T(8,128)(2,1)S(1)} %get-tuple-element.57.rest_1_.a_ref), custom_call_target="tpu_custom_call" | custom-call | tf_op jit(solution)/shard_map/pallas_call | solution.py:44
  31.7 0.6 collective-permute-done.7.rest_1_
  32.8 1.2 %collective-permute-done.10 = f32[32,384]{1,0:T(8,128)S(1)} collective-permute-done((f32[32,384]{1,0:T(8,128)S(1)}, f32[32,384]{1,0:T(8,128)S(1)}, u32[]{:S(2)}, u32[]{:S(2)}) %collective-permute-start.10) | collective-permute-done | bytes 49184 | tf_op jit(solution)/shard_map/ppermute | solution.py:55
  34.1 2.4 %collective-permute-start.13 = (f32[32,384]{1,0:T(8,128)S(1)}, f32[32,384]{1,0:T(8,128)S(1)}, u32[]{:S(2)}, u32[]{:S(2)}) collective-permute-start(f32[32,384]{1,0:T(8,128)S(1)} %add.63), channel_id=1, source_target_pairs={{0,6},{1,7},{2,4},{3,5},{4,2},{5,3},{6,0},{7,1},{8,14},{9,15},{10,... | collective-permute-start | bytes 147464 | tf_op jit(solution)/shard_map/ppermute | solution.py:55
  36.5 0.6 collective-permute-start.12
  37.1 0.6 collective-permute-start.11
  37.6 1.5 %collective-permute-done.13 = f32[32,384]{1,0:T(8,128)S(1)} collective-permute-done((f32[32,384]{1,0:T(8,128)S(1)}, f32[32,384]{1,0:T(8,128)S(1)}, u32[]{:S(2)}, u32[]{:S(2)}) %collective-permute-start.13) | collective-permute-done | bytes 49184 | tf_op jit(solution)/shard_map/ppermute | solution.py:55
  39.1 1.5 %collective-permute-done.12 = f32[32,384]{1,0:T(8,128)S(1)} collective-permute-done((f32[32,384]{1,0:T(8,128)S(1)}, f32[32,384]{1,0:T(8,128)S(1)}, u32[]{:S(2)}, u32[]{:S(2)}) %collective-permute-start.12) | collective-permute-done | bytes 49184 | tf_op jit(solution)/shard_map/ppermute | solution.py:55
  40.6 0.6 collective-permute-done.11
  41.2 3.2 %collective-permute-start.16 = (f32[32,384]{1,0:T(8,128)S(1)}, f32[32,384]{1,0:T(8,128)S(1)}, u32[]{:S(2)}, u32[]{:S(2)}) collective-permute-start(f32[32,384]{1,0:T(8,128)S(1)} %add_add_fusion.3), channel_id=1, source_target_pairs={{0,24},{8,16},{16,8},{24,0},{1,25},{9,17},{17,9},{25,1},{2,26},{10... | collective-permute-start | bytes 147464 | tf_op jit(solution)/shard_map/ppermute | solution.py:55
  44.3 1.3 %collective-permute-start.14 = (f32[32,384]{1,0:T(8,128)S(1)}, f32[32,384]{1,0:T(8,128)S(1)}, u32[]{:S(2)}, u32[]{:S(2)}) collective-permute-start(f32[32,384]{1,0:T(8,128)S(1)} %add_add_fusion.3), channel_id=1, source_target_pairs={{0,8},{8,0},{16,24},{24,16},{1,9},{9,1},{17,25},{25,17},{2,10},{10... | collective-permute-start | bytes 147464 | tf_op jit(solution)/shard_map/ppermute | solution.py:55
  45.6 1.5 %collective-permute-done.16 = f32[32,384]{1,0:T(8,128)S(1)} collective-permute-done((f32[32,384]{1,0:T(8,128)S(1)}, f32[32,384]{1,0:T(8,128)S(1)}, u32[]{:S(2)}, u32[]{:S(2)}) %collective-permute-start.16) | collective-permute-done | bytes 49184 | tf_op jit(solution)/shard_map/ppermute | solution.py:55
  47.2 2.2 %collective-permute-done.15 = f32[32,384]{1,0:T(8,128)S(1)} collective-permute-done((f32[32,384]{1,0:T(8,128)S(1)}, f32[32,384]{1,0:T(8,128)S(1)}, u32[]{:S(2)}, u32[]{:S(2)}) %collective-permute-start.15) | collective-permute-done | bytes 49184 | tf_op jit(solution)/shard_map/ppermute | solution.py:55
  49.4 1.2 %collective-permute-done.17.other_ref = f32[32,384]{1,0:T(8,128)S(1)} collective-permute-done((f32[32,384]{1,0:T(8,128)S(1)}, f32[32,384]{1,0:T(8,128)S(1)}, u32[]{:S(2)}, u32[]{:S(2)}) %collective-permute-start.17) | collective-permute-done | bytes 49184 | tf_op jit(solution)/shard_map/ppermute | solution.py:55
  50.6 0.7 shard_map.73
  51.8 2.0 %collective-permute-start.19 = (bf16[64,768]{1,0:T(8,128)(2,1)S(1)}, bf16[64,768]{1,0:T(8,128)(2,1)S(1)}, u32[]{:S(2)}, u32[]{:S(2)}) collective-permute-start(bf16[64,768]{1,0:T(8,128)(2,1)S(1)} %get-tuple-element.69.p_ref), channel_id=1, source_target_pairs={{0,16},{8,24},{16,0},{24,8},{1,17},{9,25},{17,1},{25,9},{2,18},{10... | collective-permute-start | bytes 294920 | tf_op jit(solution)/shard_map/ppermute | solution.py:55
  53.8 2.0 %collective-permute-start.18 = (bf16[64,768]{1,0:T(8,128)(2,1)S(1)}, bf16[64,768]{1,0:T(8,128)(2,1)S(1)}, u32[]{:S(2)}, u32[]{:S(2)}) collective-permute-start(bf16[64,768]{1,0:T(8,128)(2,1)S(1)} %get-tuple-element.69.p_ref), channel_id=1, source_target_pairs={{0,24},{8,16},{16,8},{24,0},{1,25},{9,17},{17,9},{25,1},{2,26},{10... | collective-permute-start | bytes 294920 | tf_op jit(solution)/shard_map/ppermute | solution.py:55
  55.8 1.7 %shard_map.74.rest_0_ = f32[64,6144]{1,0:T(8,128)S(1)} custom-call(bf16[64,768]{1,0:T(8,128)(2,1)S(1)} %get-tuple-element.69.p_ref, bf16[768,6144]{1,0:T(8,128)(2,1)S(1)} %get-tuple-element.57.rest_1_.a_ref), custom_call_target="tpu_custom_call" | custom-call | tf_op jit(solution)/shard_map/pallas_call | solution.py:44
  57.6 0.8 collective-permute-done.20.p_ref
  58.4 1.7 %shard_map.75.rest_0_ = f32[64,6144]{1,0:T(8,128)S(1)} custom-call(bf16[64,768]{1,0:T(8,128)(2,1)S(1)} %collective-permute-done.20.p_ref, bf16[768,6144]{1,0:T(8,128)(2,1)S(1)} %get-tuple-element.56.rest_1_.a_ref, f32[64,6144]{1,0:T(8,128)S(1)} %shard_map.74.rest_0_), custom_call_target="tpu_custom_call" | custom-call | tf_op jit(solution)/shard_map/pallas_call | solution.py:44
  60.2 1.7 %shard_map.76.rest_2_ = f32[64,6144]{1,0:T(8,128)S(1)} custom-call(bf16[64,768]{1,0:T(8,128)(2,1)S(1)} %collective-permute-done.19.p_ref, bf16[768,6144]{1,0:T(8,128)(2,1)S(1)} %shard_map.67.rest_8_.a_ref, f32[64,6144]{1,0:T(8,128)S(1)} %shard_map.75.rest_0_), custom_call_target="tpu_custom_call" | custom-call | tf_op jit(solution)/shard_map/pallas_call | solution.py:44
  62.1 0.8 shard_map.78
  63.0 0.8 shard_map.77.mine_ref
  63.8 1.2 %collective-permute-done.21.theirs_ref = f32[3,64,768]{2,1,0:T(8,128)S(1)} collective-permute-done((f32[3,64,768]{2,1,0:T(8,128)S(1)}, f32[3,64,768]{2,1,0:T(8,128)S(1)}, u32[]{:S(2)}, u32[]{:S(2)}) %collective-permute-start.21) | collective-permute-done | bytes 589856 | tf_op jit(solution)/shard_map/ppermute | solution.py:55
  65.0 0.6 shard_map.80
  65.8 0.5 collective-permute-start.23
  66.3 1.5 %collective-permute-start.24 = (bf16[64,768]{1,0:T(8,128)(2,1)S(1)}, bf16[64,768]{1,0:T(8,128)(2,1)S(1)}, u32[]{:S(2)}, u32[]{:S(2)}) collective-permute-start(bf16[64,768]{1,0:T(8,128)(2,1)S(1)} %get-tuple-element.79), channel_id=1, source_target_pairs={{0,4},{1,5},{2,6},{3,7},{4,0},{5,1},{6,2},{7,3},{8,12},{9,13},{10,... | collective-permute-start | bytes 294920 | tf_op jit(solution)/shard_map/ppermute | solution.py:55
  67.8 1.4 %collective-permute-start.25 = (bf16[64,768]{1,0:T(8,128)(2,1)S(1)}, bf16[64,768]{1,0:T(8,128)(2,1)S(1)}, u32[]{:S(2)}, u32[]{:S(2)}) collective-permute-start(bf16[64,768]{1,0:T(8,128)(2,1)S(1)} %get-tuple-element.80), channel_id=1, source_target_pairs={{0,6},{1,7},{2,4},{3,5},{4,2},{5,3},{6,0},{7,1},{8,14},{9,15},{10,... | collective-permute-start | bytes 294920 | tf_op jit(solution)/shard_map/ppermute | solution.py:55
  69.3 0.7 shard_map.81
  69.9 1.5 %collective-permute-done.23.rest_2_ = bf16[64,768]{1,0:T(8,128)(2,1)S(1)} collective-permute-done((bf16[64,768]{1,0:T(8,128)(2,1)S(1)}, bf16[64,768]{1,0:T(8,128)(2,1)S(1)}, u32[]{:S(2)}, u32[]{:S(2)}) %collective-permute-start.23) | collective-permute-done | bytes 98336 | tf_op jit(solution)/shard_map/ppermute | solution.py:55
  71.4 0.8 collective-permute-done.24.rest_3_
  72.3 1.6 %collective-permute-done.25.rest_4_ = bf16[64,768]{1,0:T(8,128)(2,1)S(1)} collective-permute-done((bf16[64,768]{1,0:T(8,128)(2,1)S(1)}, bf16[64,768]{1,0:T(8,128)(2,1)S(1)}, u32[]{:S(2)}, u32[]{:S(2)}) %collective-permute-start.25) | collective-permute-done | bytes 98336 | tf_op jit(solution)/shard_map/ppermute | solution.py:55
  74.4 1.2 %collective-permute-done.26 = f32[32,448]{1,0:T(8,128)S(1)} collective-permute-done((f32[32,448]{1,0:T(8,128)S(1)}, f32[32,448]{1,0:T(8,128)S(1)}, u32[]{:S(2)}, u32[]{:S(2)}) %collective-permute-start.26) | collective-permute-done | bytes 57376 | tf_op jit(solution)/shard_map/ppermute | solution.py:55
  75.7 1.8 %collective-permute-start.29 = (f32[32,448]{1,0:T(8,128)S(1)}, f32[32,448]{1,0:T(8,128)S(1)}, u32[]{:S(2)}, u32[]{:S(2)}) collective-permute-start(f32[32,448]{1,0:T(8,128)S(1)} %add.70), channel_id=1, source_target_pairs={{0,6},{1,7},{2,4},{3,5},{4,2},{5,3},{6,0},{7,1},{8,14},{9,15},{10,... | collective-permute-start | bytes 172040 | tf_op jit(solution)/shard_map/ppermute | solution.py:55
  77.5 0.6 collective-permute-start.28
  78.1 1.1 collective-permute-start.27
  79.2 1.7 %collective-permute-done.29 = f32[32,448]{1,0:T(8,128)S(1)} collective-permute-done((f32[32,448]{1,0:T(8,128)S(1)}, f32[32,448]{1,0:T(8,128)S(1)}, u32[]{:S(2)}, u32[]{:S(2)}) %collective-permute-start.29) | collective-permute-done | bytes 57376 | tf_op jit(solution)/shard_map/ppermute | solution.py:55
  80.9 1.3 %collective-permute-done.28 = f32[32,448]{1,0:T(8,128)S(1)} collective-permute-done((f32[32,448]{1,0:T(8,128)S(1)}, f32[32,448]{1,0:T(8,128)S(1)}, u32[]{:S(2)}, u32[]{:S(2)}) %collective-permute-start.28) | collective-permute-done | bytes 57376 | tf_op jit(solution)/shard_map/ppermute | solution.py:55
  82.4 4.6 %collective-permute-start.32 = (f32[32,448]{1,0:T(8,128)S(1)}, f32[32,448]{1,0:T(8,128)S(1)}, u32[]{:S(2)}, u32[]{:S(2)}) collective-permute-start(f32[32,448]{1,0:T(8,128)S(1)} %add_add_fusion.1), channel_id=1, source_target_pairs={{0,24},{8,16},{16,8},{24,0},{1,25},{9,17},{17,9},{25,1},{2,26},{10... | collective-permute-start | bytes 172040 | tf_op jit(solution)/shard_map/ppermute | solution.py:55
  87.0 0.6 collective-permute-start.30
  87.7 1.9 %collective-permute-done.32 = f32[32,448]{1,0:T(8,128)S(1)} collective-permute-done((f32[32,448]{1,0:T(8,128)S(1)}, f32[32,448]{1,0:T(8,128)S(1)}, u32[]{:S(2)}, u32[]{:S(2)}) %collective-permute-start.32) | collective-permute-done | bytes 57376 | tf_op jit(solution)/shard_map/ppermute | solution.py:55
  89.5 2.9 %collective-permute-done.31 = f32[32,448]{1,0:T(8,128)S(1)} collective-permute-done((f32[32,448]{1,0:T(8,128)S(1)}, f32[32,448]{1,0:T(8,128)S(1)}, u32[]{:S(2)}, u32[]{:S(2)}) %collective-permute-start.31) | collective-permute-done | bytes 57376 | tf_op jit(solution)/shard_map/ppermute | solution.py:55
  92.6 1.2 %collective-permute-done.33.other_ref = f32[32,448]{1,0:T(8,128)S(1)} collective-permute-done((f32[32,448]{1,0:T(8,128)S(1)}, f32[32,448]{1,0:T(8,128)S(1)}, u32[]{:S(2)}, u32[]{:S(2)}) %collective-permute-start.33) | collective-permute-done | bytes 57376 | tf_op jit(solution)/shard_map/ppermute | solution.py:55
  93.8 1.1 %shard_map.83 = (f32[64,768]{1,0:T(8,128)S(1)}, bf16[64,768]{1,0:T(8,128)(2,1)}, f32[64,64]{1,0:T(8,128)S(1)}, f32[64,64]{1,0:T(8,128)S(1)}) custom-call(f32[64,768]{1,0:T(8,128)S(1)} %get-tuple-element.85.image_ref, bf16[384,768]{1,0:T(8,128)(2,1)S(1)} %get-tuple-element.86.high_ref, bf16[384,768]{1,0:T(8,128)(2,1)S(1)} %get-tuple-element.87.low_ref, ...), custom_call_target="tpu_custom_call" | custom-call | tf_op jit(solution)/shard_map/pallas_call | solution.py:44
  95.1 1.1 collective-permute-done.34
  96.2 1.7 %collective-permute-start.37 = (f32[64,64]{1,0:T(8,128)S(1)}, f32[64,64]{1,0:T(8,128)S(1)}, u32[]{:S(2)}, u32[]{:S(2)}) collective-permute-start(f32[64,64]{1,0:T(8,128)S(1)} %add.77), channel_id=1, source_target_pairs={{0,6},{1,7},{2,4},{3,5},{4,2},{5,3},{6,0},{7,1},{8,14},{9,15},{10,... | collective-permute-start | bytes 49160 | tf_op jit(solution)/shard_map/ppermute | solution.py:55
  97.8 0.8 collective-permute-start.36
  98.7 0.9 collective-permute-start.35
  99.6 1.4 %collective-permute-done.37 = f32[64,64]{1,0:T(8,128)S(1)} collective-permute-done((f32[64,64]{1,0:T(8,128)S(1)}, f32[64,64]{1,0:T(8,128)S(1)}, u32[]{:S(2)}, u32[]{:S(2)}) %collective-permute-start.37) | collective-permute-done | bytes 16416 | tf_op jit(solution)/shard_map/ppermute | solution.py:55
  101.0 0.7 collective-permute-done.36
  101.8 0.8 collective-permute-done.35
  102.6 2.8 %collective-permute-start.40 = (f32[64,64]{1,0:T(8,128)S(1)}, f32[64,64]{1,0:T(8,128)S(1)}, u32[]{:S(2)}, u32[]{:S(2)}) collective-permute-start(f32[64,64]{1,0:T(8,128)S(1)} %add_add_fusion.5), channel_id=1, source_target_pairs={{0,24},{8,16},{16,8},{24,0},{1,25},{9,17},{17,9},{25,1},{2,26},{10... | collective-permute-start | bytes 49160 | tf_op jit(solution)/shard_map/ppermute | solution.py:55
  105.4 1.7 %collective-permute-start.38 = (f32[64,64]{1,0:T(8,128)S(1)}, f32[64,64]{1,0:T(8,128)S(1)}, u32[]{:S(2)}, u32[]{:S(2)}) collective-permute-start(f32[64,64]{1,0:T(8,128)S(1)} %add_add_fusion.5), channel_id=1, source_target_pairs={{0,8},{8,0},{16,24},{24,16},{1,9},{9,1},{17,25},{25,17},{2,10},{10... | collective-permute-start | bytes 49160 | tf_op jit(solution)/shard_map/ppermute | solution.py:55
  107.1 2.9 %shard_map.84 = (f32[64,64]{1,0:T(8,128)S(1)}, f32[64,64]{1,0:T(8,128)S(1)}, f32[64,768]{1,0:T(8,128)}) custom-call(f32[64,64]{1,0:T(8,128)S(1)} %get-tuple-element.90.gram_ref, f32[64,768]{1,0:T(8,128)S(1)} %get-tuple-element.91.rows_ref), custom_call_target="tpu_custom_call" | custom-call | tf_op jit(solution)/shard_map/pallas_call | solution.py:44
  110.2 3.0 %shard_map.85 = (f32[2,64,64]{2,1,0:T(8,128)}, f32[64,768]{1,0:T(8,128)}) custom-call(f32[64,64]{1,0:T(8,128)S(1)} %add_add_fusion.4.gram_ref, f32[64,768]{1,0:T(8,128)S(1)} %get-tuple-element.94.rows_ref, f32[64,64]{1,0:T(8,128)S(1)} %get-tuple-element.95.left_low_ref, f32[64,64]{1,0:T(8,128)S(1)} %get-tuple-element.96.left_inverse_ref), custom_call_target="tpu_custom_call" | custom-call | tf_op jit(solution)/shard_map/pallas_call | solution.py:44
  (53 shorter events, 5.5 us)
Async XLA Ops:
  1.6 8.4 %collective-permute-start.3 = (bf16[64,768]{1,0:T(8,128)(2,1)S(1)}, bf16[64,768]{1,0:T(8,128)(2,1)S(1)}, u32[]{:S(2)}, u32[]{:S(2)}) collective-permute-start(bf16[64,768]{1,0:T(8,128)(2,1)S(1)} %convert_element_type.3.rest_0_), channel_id=1, source_target_pairs={{0,6},{1,7},{2,4},{3,5},{4,2},{5,3},{6,0},{7,1},{8,14},{9,15},{10,... | collective-permute-start | bytes 294920 | tf_op jit(solution)/shard_map/ppermute | solution.py:55
  5.6 4.9 %collective-permute-start.2 = (bf16[64,768]{1,0:T(8,128)(2,1)S(1)}, bf16[64,768]{1,0:T(8,128)(2,1)S(1)}, u32[]{:S(2)}, u32[]{:S(2)}) collective-permute-start(bf16[64,768]{1,0:T(8,128)(2,1)S(1)} %convert_element_type.3.rest_0_), channel_id=1, source_target_pairs={{0,4},{1,5},{2,6},{3,7},{4,0},{5,1},{6,2},{7,3},{8,12},{9,13},{10,... | collective-permute-start | bytes 294920 | tf_op jit(solution)/shard_map/ppermute | solution.py:55
  6.1 4.7 %collective-permute-start.1 = (bf16[64,768]{1,0:T(8,128)(2,1)S(1)}, bf16[64,768]{1,0:T(8,128)(2,1)S(1)}, u32[]{:S(2)}, u32[]{:S(2)}) collective-permute-start(bf16[64,768]{1,0:T(8,128)(2,1)S(1)} %convert_element_type.3.rest_0_), channel_id=1, source_target_pairs={{0,2},{1,3},{2,0},{3,1},{4,6},{5,7},{6,4},{7,5},{8,10},{9,11},{10,... | collective-permute-start | bytes 294920 | tf_op jit(solution)/shard_map/ppermute | solution.py:55
  6.2 5.1 %collective-permute-start = (bf16[64,768]{1,0:T(8,128)(2,1)S(1)}, bf16[64,768]{1,0:T(8,128)(2,1)S(1)}, u32[]{:S(2)}, u32[]{:S(2)}) collective-permute-start(bf16[64,768]{1,0:T(8,128)(2,1)S(1)} %convert_element_type.3.rest_0_), channel_id=1, source_target_pairs={{0,1},{1,0},{2,3},{3,2},{4,5},{5,4},{6,7},{7,6},{8,9},{9,8},{10,11... | collective-permute-start | bytes 294920 | tf_op jit(solution)/shard_map/ppermute | solution.py:55
  10.8 1.3 %collective-permute-start.4 = (bf16[64,768]{1,0:T(8,128)(2,1)S(1)}, bf16[64,768]{1,0:T(8,128)(2,1)S(1)}, u32[]{:S(2)}, u32[]{:S(2)}) collective-permute-start(bf16[64,768]{1,0:T(8,128)(2,1)S(1)} %collective-permute-done.1.rest_2_), channel_id=1, source_target_pairs={{0,1},{1,0},{2,3},{3,2},{4,5},{5,4},{6,7},{7,6},{8,9},{9,8},{10,11... | collective-permute-start | bytes 294920 | tf_op jit(solution)/shard_map/ppermute | solution.py:55
  10.8 1.5 %collective-permute-start.5 = (bf16[64,768]{1,0:T(8,128)(2,1)S(1)}, bf16[64,768]{1,0:T(8,128)(2,1)S(1)}, u32[]{:S(2)}, u32[]{:S(2)}) collective-permute-start(bf16[64,768]{1,0:T(8,128)(2,1)S(1)} %collective-permute-done.2.rest_4_), channel_id=1, source_target_pairs={{0,1},{1,0},{2,3},{3,2},{4,5},{5,4},{6,7},{7,6},{8,9},{9,8},{10,11... | collective-permute-start | bytes 294920 | tf_op jit(solution)/shard_map/ppermute | solution.py:55
  11.3 1.3 %collective-permute-start.6 = (bf16[64,768]{1,0:T(8,128)(2,1)S(1)}, bf16[64,768]{1,0:T(8,128)(2,1)S(1)}, u32[]{:S(2)}, u32[]{:S(2)}) collective-permute-start(bf16[64,768]{1,0:T(8,128)(2,1)S(1)} %collective-permute-done.3.rest_6_), channel_id=1, source_target_pairs={{0,1},{1,0},{2,3},{3,2},{4,5},{5,4},{6,7},{7,6},{8,9},{9,8},{10,11... | collective-permute-start | bytes 294920 | tf_op jit(solution)/shard_map/ppermute | solution.py:55
  19.7 12.0 %collective-permute-start.8 = (bf16[64,768]{1,0:T(8,128)(2,1)S(1)}, bf16[64,768]{1,0:T(8,128)(2,1)S(1)}, u32[]{:S(2)}, u32[]{:S(2)}) collective-permute-start(bf16[64,768]{1,0:T(8,128)(2,1)S(1)} %get-tuple-element.60), channel_id=1, source_target_pairs={{0,16},{8,24},{16,0},{24,8},{1,17},{9,25},{17,1},{25,9},{2,18},{10... | collective-permute-start | bytes 294920 | tf_op jit(solution)/shard_map/ppermute | solution.py:55
  22.4 9.3 %collective-permute-start.9 = (bf16[64,768]{1,0:T(8,128)(2,1)S(1)}, bf16[64,768]{1,0:T(8,128)(2,1)S(1)}, u32[]{:S(2)}, u32[]{:S(2)}) collective-permute-start(bf16[64,768]{1,0:T(8,128)(2,1)S(1)} %get-tuple-element.61), channel_id=1, source_target_pairs={{0,24},{8,16},{16,8},{24,0},{1,25},{9,17},{17,9},{25,1},{2,26},{10... | collective-permute-start | bytes 294920 | tf_op jit(solution)/shard_map/ppermute | solution.py:55
  27.5 3.7 %copy-start = (f32[320,768]{1,0:T(8,128)S(1)}, f32[320,768]{1,0:T(8,128)}, u32[]{:S(2)}) copy-start(f32[320,768]{1,0:T(8,128)} %rest_0_) | copy-start | bytes 2949124
  27.5 4.8 %collective-permute-start.7 = (bf16[64,768]{1,0:T(8,128)(2,1)S(1)}, bf16[64,768]{1,0:T(8,128)(2,1)S(1)}, u32[]{:S(2)}, u32[]{:S(2)}) collective-permute-start(bf16[64,768]{1,0:T(8,128)(2,1)S(1)} %get-tuple-element.59), channel_id=1, source_target_pairs={{0,8},{8,0},{16,24},{24,16},{1,9},{9,1},{17,25},{25,17},{2,10},{10... | collective-permute-start | bytes 294920 | tf_op jit(solution)/shard_map/ppermute | solution.py:55
  32.7 1.3 %collective-permute-start.10 = (f32[32,384]{1,0:T(8,128)S(1)}, f32[32,384]{1,0:T(8,128)S(1)}, u32[]{:S(2)}, u32[]{:S(2)}) collective-permute-start(f32[32,384]{1,0:T(8,128)S(1)} %get-tuple-element.68), channel_id=1, source_target_pairs={{0,1},{1,0},{2,3},{3,2},{4,5},{5,4},{6,7},{7,6},{8,9},{9,8},{10,11... | collective-permute-start | bytes 147464 | tf_op jit(solution)/shard_map/ppermute | solution.py:55
  34.1 5.1 %collective-permute-start.13 = (f32[32,384]{1,0:T(8,128)S(1)}, f32[32,384]{1,0:T(8,128)S(1)}, u32[]{:S(2)}, u32[]{:S(2)}) collective-permute-start(f32[32,384]{1,0:T(8,128)S(1)} %add.63), channel_id=1, source_target_pairs={{0,6},{1,7},{2,4},{3,5},{4,2},{5,3},{6,0},{7,1},{8,14},{9,15},{10,... | collective-permute-start | bytes 147464 | tf_op jit(solution)/shard_map/ppermute | solution.py:55
  36.5 4.1 %collective-permute-start.12 = (f32[32,384]{1,0:T(8,128)S(1)}, f32[32,384]{1,0:T(8,128)S(1)}, u32[]{:S(2)}, u32[]{:S(2)}) collective-permute-start(f32[32,384]{1,0:T(8,128)S(1)} %add.63), channel_id=1, source_target_pairs={{0,4},{1,5},{2,6},{3,7},{4,0},{5,1},{6,2},{7,3},{8,12},{9,13},{10,... | collective-permute-start | bytes 147464 | tf_op jit(solution)/shard_map/ppermute | solution.py:55
  37.1 4.1 %collective-permute-start.11 = (f32[32,384]{1,0:T(8,128)S(1)}, f32[32,384]{1,0:T(8,128)S(1)}, u32[]{:S(2)}, u32[]{:S(2)}) collective-permute-start(f32[32,384]{1,0:T(8,128)S(1)} %add.63), channel_id=1, source_target_pairs={{0,2},{1,3},{2,0},{3,1},{4,6},{5,7},{6,4},{7,5},{8,10},{9,11},{10,... | collective-permute-start | bytes 147464 | tf_op jit(solution)/shard_map/ppermute | solution.py:55
  41.2 6.0 %collective-permute-start.16 = (f32[32,384]{1,0:T(8,128)S(1)}, f32[32,384]{1,0:T(8,128)S(1)}, u32[]{:S(2)}, u32[]{:S(2)}) collective-permute-start(f32[32,384]{1,0:T(8,128)S(1)} %add_add_fusion.3), channel_id=1, source_target_pairs={{0,24},{8,16},{16,8},{24,0},{1,25},{9,17},{17,9},{25,1},{2,26},{10... | collective-permute-start | bytes 147464 | tf_op jit(solution)/shard_map/ppermute | solution.py:55
  44.3 5.0 %collective-permute-start.15 = (f32[32,384]{1,0:T(8,128)S(1)}, f32[32,384]{1,0:T(8,128)S(1)}, u32[]{:S(2)}, u32[]{:S(2)}) collective-permute-start(f32[32,384]{1,0:T(8,128)S(1)} %add_add_fusion.3), channel_id=1, source_target_pairs={{0,16},{8,24},{16,0},{24,8},{1,17},{9,25},{17,1},{25,9},{2,18},{10... | collective-permute-start | bytes 147464 | tf_op jit(solution)/shard_map/ppermute | solution.py:55
  44.3 5.0 %collective-permute-start.14 = (f32[32,384]{1,0:T(8,128)S(1)}, f32[32,384]{1,0:T(8,128)S(1)}, u32[]{:S(2)}, u32[]{:S(2)}) collective-permute-start(f32[32,384]{1,0:T(8,128)S(1)} %add_add_fusion.3), channel_id=1, source_target_pairs={{0,8},{8,0},{16,24},{24,16},{1,9},{9,1},{17,25},{25,17},{2,10},{10... | collective-permute-start | bytes 147464 | tf_op jit(solution)/shard_map/ppermute | solution.py:55
  49.3 1.3 %collective-permute-start.17 = (f32[32,384]{1,0:T(8,128)S(1)}, f32[32,384]{1,0:T(8,128)S(1)}, u32[]{:S(2)}, u32[]{:S(2)}) collective-permute-start(f32[32,384]{1,0:T(8,128)S(1)} %add_add_fusion.2.mine_ref), channel_id=1, source_target_pairs={{0,1},{1,0},{2,3},{3,2},{4,5},{5,4},{6,7},{7,6},{8,9},{9,8},{10,11... | collective-permute-start | bytes 147464 | tf_op jit(solution)/shard_map/ppermute | solution.py:55
  51.4 7.0 %collective-permute-start.20 = (bf16[64,768]{1,0:T(8,128)(2,1)S(1)}, bf16[64,768]{1,0:T(8,128)(2,1)S(1)}, u32[]{:S(2)}, u32[]{:S(2)}) collective-permute-start(bf16[64,768]{1,0:T(8,128)(2,1)S(1)} %get-tuple-element.69.p_ref), channel_id=1, source_target_pairs={{0,8},{8,0},{16,24},{24,16},{1,9},{9,1},{17,25},{25,17},{2,10},{10... | collective-permute-start | bytes 294920 | tf_op jit(solution)/shard_map/ppermute | solution.py:55
  51.8 8.3 %collective-permute-start.19 = (bf16[64,768]{1,0:T(8,128)(2,1)S(1)}, bf16[64,768]{1,0:T(8,128)(2,1)S(1)}, u32[]{:S(2)}, u32[]{:S(2)}) collective-permute-start(bf16[64,768]{1,0:T(8,128)(2,1)S(1)} %get-tuple-element.69.p_ref), channel_id=1, source_target_pairs={{0,16},{8,24},{16,0},{24,8},{1,17},{9,25},{17,1},{25,9},{2,18},{10... | collective-permute-start | bytes 294920 | tf_op jit(solution)/shard_map/ppermute | solution.py:55
  53.8 8.3 %collective-permute-start.18 = (bf16[64,768]{1,0:T(8,128)(2,1)S(1)}, bf16[64,768]{1,0:T(8,128)(2,1)S(1)}, u32[]{:S(2)}, u32[]{:S(2)}) collective-permute-start(bf16[64,768]{1,0:T(8,128)(2,1)S(1)} %get-tuple-element.69.p_ref), channel_id=1, source_target_pairs={{0,24},{8,16},{16,8},{24,0},{1,25},{9,17},{17,9},{25,1},{2,26},{10... | collective-permute-start | bytes 294920 | tf_op jit(solution)/shard_map/ppermute | solution.py:55
  62.9 6.4 %copy-start.1 = (f32[320,768]{1,0:T(8,128)S(1)}, f32[320,768]{1,0:T(8,128)}, u32[]{:S(2)}) copy-start(f32[320,768]{1,0:T(8,128)} %rest_0_.1) | copy-start | bytes 2949124
  62.9 6.4 %copy-start.2 = (f32[64,768]{1,0:T(8,128)S(1)}, f32[64,768]{1,0:T(8,128)}, u32[]{:S(2)}) copy-start(f32[64,768]{1,0:T(8,128)} %rest_1_) | copy-start | bytes 589828
  62.9 2.1 %collective-permute-start.21 = (f32[3,64,768]{2,1,0:T(8,128)S(1)}, f32[3,64,768]{2,1,0:T(8,128)S(1)}, u32[]{:S(2)}, u32[]{:S(2)}) collective-permute-start(f32[3,64,768]{2,1,0:T(8,128)S(1)} %shard_map.78), channel_id=1, source_target_pairs={{0,1},{1,0},{2,3},{3,2},{4,5},{5,4},{6,7},{7,6},{8,9},{9,8},{10,11... | collective-permute-start | bytes 1769480 | tf_op jit(solution)/shard_map/ppermute | solution.py:55
  65.6 8.3 %collective-permute-start.22 = (f32[1,64,768]{2,1,0:T(8,128)S(1)}, f32[1,64,768]{2,1,0:T(8,128)S(1)}, u32[]{:S(2)}, u32[]{:S(2)}) collective-permute-start(f32[1,64,768]{2,1,0:T(8,128)S(1)} %get-tuple-element.77), channel_id=1, source_target_pairs={{0,1},{1,0},{2,3},{3,2},{4,5},{5,4},{6,7},{7,6},{8,9},{9,8},{10,11... | collective-permute-start | bytes 589832 | tf_op jit(solution)/shard_map/ppermute | solution.py:55
  65.8 5.7 %collective-permute-start.23 = (bf16[64,768]{1,0:T(8,128)(2,1)S(1)}, bf16[64,768]{1,0:T(8,128)(2,1)S(1)}, u32[]{:S(2)}, u32[]{:S(2)}) collective-permute-start(bf16[64,768]{1,0:T(8,128)(2,1)S(1)} %get-tuple-element.78), channel_id=1, source_target_pairs={{0,2},{1,3},{2,0},{3,1},{4,6},{5,7},{6,4},{7,5},{8,10},{9,11},{10,... | collective-permute-start | bytes 294920 | tf_op jit(solution)/shard_map/ppermute | solution.py:55
  66.3 6.0 %collective-permute-start.24 = (bf16[64,768]{1,0:T(8,128)(2,1)S(1)}, bf16[64,768]{1,0:T(8,128)(2,1)S(1)}, u32[]{:S(2)}, u32[]{:S(2)}) collective-permute-start(bf16[64,768]{1,0:T(8,128)(2,1)S(1)} %get-tuple-element.79), channel_id=1, source_target_pairs={{0,4},{1,5},{2,6},{3,7},{4,0},{5,1},{6,2},{7,3},{8,12},{9,13},{10,... | collective-permute-start | bytes 294920 | tf_op jit(solution)/shard_map/ppermute | solution.py:55
  67.8 6.1 %collective-permute-start.25 = (bf16[64,768]{1,0:T(8,128)(2,1)S(1)}, bf16[64,768]{1,0:T(8,128)(2,1)S(1)}, u32[]{:S(2)}, u32[]{:S(2)}) collective-permute-start(bf16[64,768]{1,0:T(8,128)(2,1)S(1)} %get-tuple-element.80), channel_id=1, source_target_pairs={{0,6},{1,7},{2,4},{3,5},{4,2},{5,3},{6,0},{7,1},{8,14},{9,15},{10,... | collective-permute-start | bytes 294920 | tf_op jit(solution)/shard_map/ppermute | solution.py:55
  74.3 1.3 %collective-permute-start.26 = (f32[32,448]{1,0:T(8,128)S(1)}, f32[32,448]{1,0:T(8,128)S(1)}, u32[]{:S(2)}, u32[]{:S(2)}) collective-permute-start(f32[32,448]{1,0:T(8,128)S(1)} %get-tuple-element.89), channel_id=1, source_target_pairs={{0,1},{1,0},{2,3},{3,2},{4,5},{5,4},{6,7},{7,6},{8,9},{9,8},{10,11... | collective-permute-start | bytes 172040 | tf_op jit(solution)/shard_map/ppermute | solution.py:55
  75.7 5.2 %collective-permute-start.29 = (f32[32,448]{1,0:T(8,128)S(1)}, f32[32,448]{1,0:T(8,128)S(1)}, u32[]{:S(2)}, u32[]{:S(2)}) collective-permute-start(f32[32,448]{1,0:T(8,128)S(1)} %add.70), channel_id=1, source_target_pairs={{0,6},{1,7},{2,4},{3,5},{4,2},{5,3},{6,0},{7,1},{8,14},{9,15},{10,... | collective-permute-start | bytes 172040 | tf_op jit(solution)/shard_map/ppermute | solution.py:55
  77.5 4.7 %collective-permute-start.28 = (f32[32,448]{1,0:T(8,128)S(1)}, f32[32,448]{1,0:T(8,128)S(1)}, u32[]{:S(2)}, u32[]{:S(2)}) collective-permute-start(f32[32,448]{1,0:T(8,128)S(1)} %add.70), channel_id=1, source_target_pairs={{0,4},{1,5},{2,6},{3,7},{4,0},{5,1},{6,2},{7,3},{8,12},{9,13},{10,... | collective-permute-start | bytes 172040 | tf_op jit(solution)/shard_map/ppermute | solution.py:55
  78.1 4.3 %collective-permute-start.27 = (f32[32,448]{1,0:T(8,128)S(1)}, f32[32,448]{1,0:T(8,128)S(1)}, u32[]{:S(2)}, u32[]{:S(2)}) collective-permute-start(f32[32,448]{1,0:T(8,128)S(1)} %add.70), channel_id=1, source_target_pairs={{0,2},{1,3},{2,0},{3,1},{4,6},{5,7},{6,4},{7,5},{8,10},{9,11},{10,... | collective-permute-start | bytes 172040 | tf_op jit(solution)/shard_map/ppermute | solution.py:55
  82.4 7.1 %collective-permute-start.32 = (f32[32,448]{1,0:T(8,128)S(1)}, f32[32,448]{1,0:T(8,128)S(1)}, u32[]{:S(2)}, u32[]{:S(2)}) collective-permute-start(f32[32,448]{1,0:T(8,128)S(1)} %add_add_fusion.1), channel_id=1, source_target_pairs={{0,24},{8,16},{16,8},{24,0},{1,25},{9,17},{17,9},{25,1},{2,26},{10... | collective-permute-start | bytes 172040 | tf_op jit(solution)/shard_map/ppermute | solution.py:55
  87.0 5.4 %collective-permute-start.31 = (f32[32,448]{1,0:T(8,128)S(1)}, f32[32,448]{1,0:T(8,128)S(1)}, u32[]{:S(2)}, u32[]{:S(2)}) collective-permute-start(f32[32,448]{1,0:T(8,128)S(1)} %add_add_fusion.1), channel_id=1, source_target_pairs={{0,16},{8,24},{16,0},{24,8},{1,17},{9,25},{17,1},{25,9},{2,18},{10... | collective-permute-start | bytes 172040 | tf_op jit(solution)/shard_map/ppermute | solution.py:55
  87.0 5.4 %collective-permute-start.30 = (f32[32,448]{1,0:T(8,128)S(1)}, f32[32,448]{1,0:T(8,128)S(1)}, u32[]{:S(2)}, u32[]{:S(2)}) collective-permute-start(f32[32,448]{1,0:T(8,128)S(1)} %add_add_fusion.1), channel_id=1, source_target_pairs={{0,8},{8,0},{16,24},{24,16},{1,9},{9,1},{17,25},{25,17},{2,10},{10... | collective-permute-start | bytes 172040 | tf_op jit(solution)/shard_map/ppermute | solution.py:55
  92.5 1.3 %collective-permute-start.33 = (f32[32,448]{1,0:T(8,128)S(1)}, f32[32,448]{1,0:T(8,128)S(1)}, u32[]{:S(2)}, u32[]{:S(2)}) collective-permute-start(f32[32,448]{1,0:T(8,128)S(1)} %add_add_fusion.mine_ref), channel_id=1, source_target_pairs={{0,1},{1,0},{2,3},{3,2},{4,5},{5,4},{6,7},{7,6},{8,9},{9,8},{10,11... | collective-permute-start | bytes 172040 | tf_op jit(solution)/shard_map/ppermute | solution.py:55
  94.9 1.2 %collective-permute-start.34 = (f32[64,64]{1,0:T(8,128)S(1)}, f32[64,64]{1,0:T(8,128)S(1)}, u32[]{:S(2)}, u32[]{:S(2)}) collective-permute-start(f32[64,64]{1,0:T(8,128)S(1)} %get-tuple-element.93), channel_id=1, source_target_pairs={{0,1},{1,0},{2,3},{3,2},{4,5},{5,4},{6,7},{7,6},{8,9},{9,8},{10,11... | collective-permute-start | bytes 49160 | tf_op jit(solution)/shard_map/ppermute | solution.py:55
  96.2 4.9 %collective-permute-start.37 = (f32[64,64]{1,0:T(8,128)S(1)}, f32[64,64]{1,0:T(8,128)S(1)}, u32[]{:S(2)}, u32[]{:S(2)}) collective-permute-start(f32[64,64]{1,0:T(8,128)S(1)} %add.77), channel_id=1, source_target_pairs={{0,6},{1,7},{2,4},{3,5},{4,2},{5,3},{6,0},{7,1},{8,14},{9,15},{10,... | collective-permute-start | bytes 49160 | tf_op jit(solution)/shard_map/ppermute | solution.py:55
  97.8 3.9 %collective-permute-start.36 = (f32[64,64]{1,0:T(8,128)S(1)}, f32[64,64]{1,0:T(8,128)S(1)}, u32[]{:S(2)}, u32[]{:S(2)}) collective-permute-start(f32[64,64]{1,0:T(8,128)S(1)} %add.77), channel_id=1, source_target_pairs={{0,4},{1,5},{2,6},{3,7},{4,0},{5,1},{6,2},{7,3},{8,12},{9,13},{10,... | collective-permute-start | bytes 49160 | tf_op jit(solution)/shard_map/ppermute | solution.py:55
  98.7 3.9 %collective-permute-start.35 = (f32[64,64]{1,0:T(8,128)S(1)}, f32[64,64]{1,0:T(8,128)S(1)}, u32[]{:S(2)}, u32[]{:S(2)}) collective-permute-start(f32[64,64]{1,0:T(8,128)S(1)} %add.77), channel_id=1, source_target_pairs={{0,2},{1,3},{2,0},{3,1},{4,6},{5,7},{6,4},{7,5},{8,10},{9,11},{10,... | collective-permute-start | bytes 49160 | tf_op jit(solution)/shard_map/ppermute | solution.py:55
  102.6 7.3 %collective-permute-start.40 = (f32[64,64]{1,0:T(8,128)S(1)}, f32[64,64]{1,0:T(8,128)S(1)}, u32[]{:S(2)}, u32[]{:S(2)}) collective-permute-start(f32[64,64]{1,0:T(8,128)S(1)} %add_add_fusion.5), channel_id=1, source_target_pairs={{0,24},{8,16},{16,8},{24,0},{1,25},{9,17},{17,9},{25,1},{2,26},{10... | collective-permute-start | bytes 49160 | tf_op jit(solution)/shard_map/ppermute | solution.py:55
  105.4 4.8 %collective-permute-start.39 = (f32[64,64]{1,0:T(8,128)S(1)}, f32[64,64]{1,0:T(8,128)S(1)}, u32[]{:S(2)}, u32[]{:S(2)}) collective-permute-start(f32[64,64]{1,0:T(8,128)S(1)} %add_add_fusion.5), channel_id=1, source_target_pairs={{0,16},{8,24},{16,0},{24,8},{1,17},{9,25},{17,1},{25,9},{2,18},{10... | collective-permute-start | bytes 49160 | tf_op jit(solution)/shard_map/ppermute | solution.py:55
  105.4 4.8 %collective-permute-start.38 = (f32[64,64]{1,0:T(8,128)S(1)}, f32[64,64]{1,0:T(8,128)S(1)}, u32[]{:S(2)}, u32[]{:S(2)}) collective-permute-start(f32[64,64]{1,0:T(8,128)S(1)} %add_add_fusion.5), channel_id=1, source_target_pairs={{0,8},{8,0},{16,24},{24,16},{1,9},{9,1},{17,25},{25,17},{2,10},{10... | collective-permute-start | bytes 49160 | tf_op jit(solution)/shard_map/ppermute | solution.py:55
